TPU v7x, 32 devices: a whole 2x2x4 slice. The times are simulated.
32 devices in a mesh: rep: 2 (over x), fsdp: 4 (over z), ctx: 4 (over y, core).
Axes of the slice: x: 2, y: 2, z: 4, core: 2. Of those that a mesh axis runs over, the one named last changes fastest.
Arguments:
- inputs: bfloat16 [8, 1024, 2048], P(('rep', 'fsdp'), 'ctx'), may hold values from -6 to 6
- prefix: int32 [8], P(('rep', 'fsdp')), may hold values from 102 to 512
- joined_weight: bfloat16 [2048, 6144], P(('fsdp', 'ctx')), may hold values from -0.125 to 0.125
- query_bias: bfloat16 [2048], P(('fsdp', 'ctx')), may hold values from -3 to 3
- value_bias: bfloat16 [2048], P(('fsdp', 'ctx')), may hold values from -3 to 3
- dense_weight: bfloat16 [2048, 2048], P(('fsdp', 'ctx')), may hold values from -0.5 to 0.5
- dense_bias: bfloat16 [2048], P(('fsdp', 'ctx')), may hold values from -2 to 2
- expand_weight: bfloat16 [2048, 8192], P(('fsdp', 'ctx')), may hold values from -0.125 to 0.125
- expand_bias: bfloat16 [8192], P(('fsdp', 'ctx')), may hold values from -3 to 3
- shrink_weight: bfloat16 [8192, 2048], P(('fsdp', 'ctx')), may hold values from -0.0625 to 0.0625
- shrink_bias: bfloat16 [2048], P(('fsdp', 'ctx')), may hold values from -2 to 2
- first_gain: bfloat16 [2048], P(('fsdp', 'ctx')), may hold values from 0.5 to 1.5
- first_shift: bfloat16 [2048], P(('fsdp', 'ctx')), may hold values from -2 to 2
- second_gain: bfloat16 [2048], P(('fsdp', 'ctx')), may hold values from 0.5 to 1.5
- second_shift: bfloat16 [2048], P(('fsdp', 'ctx')), may hold values from -2 to 2
- cotangent: bfloat16 [8, 1024, 2048], P(('rep', 'fsdp'), 'ctx'), may hold values from -6 to 6
Outputs:
- layer_output: float32 [8, 1024, 2048], P(('rep', 'fsdp'), 'ctx')
- input_gradient: float32 [8, 1024, 2048], P(('rep', 'fsdp'), 'ctx')
- joined_gradient: float32 [2048, 6144], P(('fsdp', 'ctx'))
- query_bias_gradient: float32 [2048], P(('fsdp', 'ctx'))
- value_bias_gradient: float32 [2048], P(('fsdp', 'ctx'))
- dense_gradient: float32 [2048, 2048], P(('fsdp', 'ctx'))
- dense_bias_gradient: float32 [2048], P(('fsdp', 'ctx'))
- expand_gradient: float32 [2048, 8192], P(('fsdp', 'ctx'))
- expand_bias_gradient: float32 [8192], P(('fsdp', 'ctx'))
- shrink_gradient: float32 [8192, 2048], P(('fsdp', 'ctx'))
- shrink_bias_gradient: float32 [2048], P(('fsdp', 'ctx'))
- first_gain_gradient: float32 [2048], P(('fsdp', 'ctx'))
- first_shift_gradient: float32 [2048], P(('fsdp', 'ctx'))
- second_gain_gradient: float32 [2048], P(('fsdp', 'ctx'))
- second_shift_gradient: float32 [2048], P(('fsdp', 'ctx'))
All inputs are finite; a program needn't handle non-finite values.
Results may differ from a plain program's by a relative error of at most 0.014.
Values may be sent and summed in bfloat16 or wider, within the bound.
No kernel may reach another device: no remote copies, remote signals or barrier semaphores. Data moves between devices by JAX's collectives and lax.ppermute only.
A program may use at most 576 MiB of HBM per device.

v0:
```python
import jax
import jax.numpy as jnp
from jax import lax
from jax.sharding import PartitionSpec as P

H = 32
HD = 64


def layer_norm(values, gain, shift):
    average = jnp.mean(values, axis=-1, keepdims=True)
    centred = values - average
    variance = jnp.mean(centred * centred, axis=-1, keepdims=True)
    return centred * lax.rsqrt(variance + 1e-05) * gain + shift


def exact_gelu(values):
    return jax.nn.gelu(values, approximate=False)


def score_logits(query_heads, key_heads, prefix, first_place):
    raw = jnp.einsum("sqhe,skhe->shqk", query_heads, key_heads, preferred_element_type=jnp.float32)
    queries_here = query_heads.shape[1]
    length = key_heads.shape[1]
    heads = query_heads.shape[2]
    query_place = first_place + jnp.arange(queries_here, dtype=jnp.int32)
    key_place = jnp.arange(length, dtype=jnp.int32)
    distance = jnp.abs(query_place[:, None] - key_place[None, :]).astype(jnp.float32)
    allowed = (key_place[None, None, :] <= query_place[None, :, None]) | (
        key_place[None, None, :] < prefix[:, None, None]
    )
    order = jnp.arange(heads, dtype=jnp.int32).astype(jnp.float32)
    slopes = jnp.exp2(-8.0 * (order + 1.0) / heads)
    logits = raw * 0.125 - slopes[None, :, None, None] * distance[None, None]
    return (logits, allowed[:, None])


def shards(
    inputs,
    prefix,
    joined_weight,
    query_bias,
    value_bias,
    dense_weight,
    dense_bias,
    expand_weight,
    expand_bias,
    shrink_weight,
    shrink_bias,
    first_gain,
    first_shift,
    second_gain,
    second_shift,
    cotangent,
):
    sequences, span_rows, features = inputs.shape
    tokens = sequences * span_rows
    attn_parts = (
        lax.all_gather(joined_weight, ("fsdp", "ctx"), axis=0, tiled=True),
        lax.all_gather(query_bias, ("fsdp", "ctx"), axis=0, tiled=True),
        lax.all_gather(value_bias, ("fsdp", "ctx"), axis=0, tiled=True),
        lax.all_gather(dense_weight, ("fsdp", "ctx"), axis=0, tiled=True),
        lax.all_gather(dense_bias, ("fsdp", "ctx"), axis=0, tiled=True),
        lax.all_gather(first_gain, ("fsdp", "ctx"), axis=0, tiled=True),
        lax.all_gather(first_shift, ("fsdp", "ctx"), axis=0, tiled=True),
    )
    joined_all, qbias_all, vbias_all, dense_all, dbias_all, gain_one, shift_one = attn_parts
    start = inputs.astype(jnp.float32).reshape(tokens, features)
    gain_first = gain_one.astype(jnp.float32)
    shift_first = shift_one.astype(jnp.float32)
    normed = layer_norm(start, gain_first, shift_first).astype(jnp.bfloat16)
    projected = jnp.dot(normed, joined_all, preferred_element_type=jnp.float32)
    queries = (projected[:, :features] + qbias_all.astype(jnp.float32)).astype(jnp.bfloat16)
    keys_own = projected[:, features : 2 * features].astype(jnp.bfloat16)
    values_own = (projected[:, 2 * features :] + vbias_all.astype(jnp.float32)).astype(jnp.bfloat16)
    keys_all, values_all = (
        lax.all_gather(keys_own.reshape(sequences, span_rows, features), "ctx", axis=1, tiled=True),
        lax.all_gather(
            values_own.reshape(sequences, span_rows, features), "ctx", axis=1, tiled=True
        ),
    )
    length = keys_all.shape[1]
    query_heads = queries.reshape(sequences, span_rows, H, HD)
    key_heads = keys_all.reshape(sequences, length, H, HD)
    value_heads = values_all.reshape(sequences, length, H, HD)
    first_place = lax.axis_index("ctx") * span_rows
    logits, allowed = score_logits(query_heads, key_heads, prefix, first_place)
    masked = jnp.where(allowed, logits, -1e30)
    largest = jnp.max(masked, axis=-1, keepdims=True)
    exponent = jnp.exp(masked - largest)
    totals = jnp.sum(exponent, axis=-1, keepdims=True)
    log_total = largest + jnp.log(totals)
    probs_low = (exponent / totals).astype(jnp.bfloat16)
    mixture = jnp.einsum(
        "shqk,skhe->sqhe", probs_low, value_heads, preferred_element_type=jnp.float32
    )
    attended = mixture.reshape(tokens, features).astype(jnp.bfloat16)
    midway = (
        start
        + jnp.dot(attended, dense_all, preferred_element_type=jnp.float32)
        + dbias_all.astype(jnp.float32)
    )
    mlp_parts = (
        lax.all_gather(expand_weight, ("fsdp", "ctx"), axis=0, tiled=True),
        lax.all_gather(expand_bias, ("fsdp", "ctx"), axis=0, tiled=True),
        lax.all_gather(shrink_weight, ("fsdp", "ctx"), axis=0, tiled=True),
        lax.all_gather(shrink_bias, ("fsdp", "ctx"), axis=0, tiled=True),
        lax.all_gather(second_gain, ("fsdp", "ctx"), axis=0, tiled=True),
        lax.all_gather(second_shift, ("fsdp", "ctx"), axis=0, tiled=True),
    )
    expand_all, ebias_all, shrink_all, sbias_all, gain_two, shift_two = mlp_parts
    gain_second = gain_two.astype(jnp.float32)
    shift_second = shift_two.astype(jnp.float32)
    normed_two = layer_norm(midway, gain_second, shift_second).astype(jnp.bfloat16)
    expanded = jnp.dot(
        normed_two, expand_all, preferred_element_type=jnp.float32
    ) + ebias_all.astype(jnp.float32)
    activated = exact_gelu(expanded).astype(jnp.bfloat16)
    result = (
        midway
        + jnp.dot(activated, shrink_all, preferred_element_type=jnp.float32)
        + sbias_all.astype(jnp.float32)
    )
    again_mlp = (
        lax.all_gather(expand_weight, ("fsdp", "ctx"), axis=0, tiled=True),
        lax.all_gather(shrink_weight, ("fsdp", "ctx"), axis=0, tiled=True),
        lax.all_gather(second_gain, ("fsdp", "ctx"), axis=0, tiled=True),
    )
    back_expand, back_shrink = (again_mlp[0], again_mlp[1])
    back_gain_two = again_mlp[2].astype(jnp.float32)
    grad_out = cotangent.reshape(tokens, features)
    grad_out_float = grad_out.astype(jnp.float32)
    shrink_term = jnp.einsum("rf,rd->fd", activated, grad_out, preferred_element_type=jnp.float32)
    sbias_term = jnp.sum(grad_out_float, axis=0)
    d_activated = jnp.einsum("rd,fd->rf", grad_out, back_shrink, preferred_element_type=jnp.float32)
    d_expanded = jax.vjp(exact_gelu, expanded)[1](d_activated)[0].astype(jnp.bfloat16)
    expand_term = jnp.einsum(
        "rd,rf->df", normed_two, d_expanded, preferred_element_type=jnp.float32
    )
    ebias_term = jnp.sum(d_expanded.astype(jnp.float32), axis=0)
    d_normed_two = jnp.einsum(
        "rf,df->rd", d_expanded, back_expand, preferred_element_type=jnp.float32
    )
    norm_back_two = jax.vjp(layer_norm, midway, back_gain_two, shift_second)[1]
    d_mid_norm, gain_two_term, shift_two_term = norm_back_two(d_normed_two)
    d_midway = grad_out_float + d_mid_norm
    mlp_grads = (
        lax.psum_scatter(expand_term, ("fsdp", "ctx"), scatter_dimension=0, tiled=True),
        lax.psum_scatter(ebias_term, ("fsdp", "ctx"), scatter_dimension=0, tiled=True),
        lax.psum_scatter(shrink_term, ("fsdp", "ctx"), scatter_dimension=0, tiled=True),
        lax.psum_scatter(sbias_term, ("fsdp", "ctx"), scatter_dimension=0, tiled=True),
        lax.psum_scatter(gain_two_term, ("fsdp", "ctx"), scatter_dimension=0, tiled=True),
        lax.psum_scatter(shift_two_term, ("fsdp", "ctx"), scatter_dimension=0, tiled=True),
    )
    again_attn = (
        lax.all_gather(joined_weight, ("fsdp", "ctx"), axis=0, tiled=True),
        lax.all_gather(dense_weight, ("fsdp", "ctx"), axis=0, tiled=True),
        lax.all_gather(first_gain, ("fsdp", "ctx"), axis=0, tiled=True),
    )
    back_joined, back_dense = (again_attn[0], again_attn[1])
    back_gain_one = again_attn[2].astype(jnp.float32)
    d_attended_out = d_midway.astype(jnp.bfloat16)
    dense_term = jnp.einsum(
        "rd,re->de", attended, d_attended_out, preferred_element_type=jnp.float32
    )
    dbias_term = jnp.sum(d_attended_out.astype(jnp.float32), axis=0)
    d_attended = jnp.einsum(
        "re,de->rd", d_attended_out, back_dense, preferred_element_type=jnp.float32
    ).astype(jnp.bfloat16)
    d_heads = d_attended.reshape(sequences, span_rows, H, HD)
    logits_again, allowed_again = score_logits(query_heads, key_heads, prefix, first_place)
    probs = jnp.where(allowed_again, jnp.exp(logits_again - log_total), 0.0)
    probs_again = probs.astype(jnp.bfloat16)
    d_probs = jnp.einsum(
        "sqhe,skhe->shqk", d_heads, value_heads, preferred_element_type=jnp.float32
    )
    weighted = jnp.sum(probs * d_probs, axis=-1, keepdims=True)
    d_raw = (probs * (d_probs - weighted) * 0.125).astype(jnp.bfloat16)
    d_queries = jnp.einsum("shqk,skhe->sqhe", d_raw, key_heads, preferred_element_type=jnp.float32)
    d_keys_full = jnp.einsum(
        "shqk,sqhe->skhe", d_raw, query_heads, preferred_element_type=jnp.float32
    )
    d_values_full = jnp.einsum(
        "shqk,sqhe->skhe", probs_again, d_heads, preferred_element_type=jnp.float32
    )
    d_keys, d_values = (
        lax.psum_scatter(
            d_keys_full.reshape(sequences, length, features).astype(jnp.bfloat16),
            "ctx",
            scatter_dimension=1,
            tiled=True,
        ).astype(jnp.float32),
        lax.psum_scatter(
            d_values_full.reshape(sequences, length, features).astype(jnp.bfloat16),
            "ctx",
            scatter_dimension=1,
            tiled=True,
        ).astype(jnp.float32),
    )
    d_queries_low = d_queries.reshape(tokens, features).astype(jnp.bfloat16)
    d_keys_low = d_keys.reshape(tokens, features).astype(jnp.bfloat16)
    d_values_low = d_values.reshape(tokens, features).astype(jnp.bfloat16)
    qbias_term = jnp.sum(d_queries_low.astype(jnp.float32), axis=0)
    vbias_term = jnp.sum(d_values_low.astype(jnp.float32), axis=0)
    d_projected = jnp.concatenate([d_queries_low, d_keys_low, d_values_low], axis=1)
    joined_term = jnp.einsum("rd,re->de", normed, d_projected, preferred_element_type=jnp.float32)
    d_normed = jnp.einsum("re,de->rd", d_projected, back_joined, preferred_element_type=jnp.float32)
    norm_back_one = jax.vjp(layer_norm, start, back_gain_one, shift_first)[1]
    d_start_norm, gain_one_term, shift_one_term = norm_back_one(d_normed)
    input_gradient = d_midway + d_start_norm
    attn_grads = (
        lax.psum_scatter(joined_term, ("fsdp", "ctx"), scatter_dimension=0, tiled=True),
        lax.psum_scatter(qbias_term, ("fsdp", "ctx"), scatter_dimension=0, tiled=True),
        lax.psum_scatter(vbias_term, ("fsdp", "ctx"), scatter_dimension=0, tiled=True),
        lax.psum_scatter(dense_term, ("fsdp", "ctx"), scatter_dimension=0, tiled=True),
        lax.psum_scatter(dbias_term, ("fsdp", "ctx"), scatter_dimension=0, tiled=True),
        lax.psum_scatter(gain_one_term, ("fsdp", "ctx"), scatter_dimension=0, tiled=True),
        lax.psum_scatter(shift_one_term, ("fsdp", "ctx"), scatter_dimension=0, tiled=True),
    )
    summed = (
        lax.psum(attn_grads[0].astype(jnp.bfloat16), "rep").astype(jnp.float32),
        lax.psum(attn_grads[1].astype(jnp.bfloat16), "rep").astype(jnp.float32),
        lax.psum(attn_grads[2].astype(jnp.bfloat16), "rep").astype(jnp.float32),
        lax.psum(attn_grads[3].astype(jnp.bfloat16), "rep").astype(jnp.float32),
        lax.psum(attn_grads[4].astype(jnp.bfloat16), "rep").astype(jnp.float32),
        lax.psum(attn_grads[5].astype(jnp.bfloat16), "rep").astype(jnp.float32),
        lax.psum(attn_grads[6].astype(jnp.bfloat16), "rep").astype(jnp.float32),
        lax.psum(mlp_grads[0].astype(jnp.bfloat16), "rep").astype(jnp.float32),
        lax.psum(mlp_grads[1].astype(jnp.bfloat16), "rep").astype(jnp.float32),
        lax.psum(mlp_grads[2].astype(jnp.bfloat16), "rep").astype(jnp.float32),
        lax.psum(mlp_grads[3].astype(jnp.bfloat16), "rep").astype(jnp.float32),
        lax.psum(mlp_grads[4].astype(jnp.bfloat16), "rep").astype(jnp.float32),
        lax.psum(mlp_grads[5].astype(jnp.bfloat16), "rep").astype(jnp.float32),
    )
    attn_grads = summed[:7]
    mlp_grads = summed[7:]
    return (
        result.reshape(sequences, span_rows, features),
        input_gradient.reshape(sequences, span_rows, features),
        attn_grads[0],
        attn_grads[1],
        attn_grads[2],
        attn_grads[3],
        attn_grads[4],
        mlp_grads[0],
        mlp_grads[1],
        mlp_grads[2],
        mlp_grads[3],
        attn_grads[5],
        attn_grads[6],
        mlp_grads[4],
        mlp_grads[5],
    )


def solution(mesh):
    in_specs = (
        P(("rep", "fsdp"), "ctx", None),
        P(("rep", "fsdp")),
        P(("fsdp", "ctx"), None),
        P(("fsdp", "ctx")),
        P(("fsdp", "ctx")),
        P(("fsdp", "ctx"), None),
        P(("fsdp", "ctx")),
        P(("fsdp", "ctx"), None),
        P(("fsdp", "ctx")),
        P(("fsdp", "ctx"), None),
        P(("fsdp", "ctx")),
        P(("fsdp", "ctx")),
        P(("fsdp", "ctx")),
        P(("fsdp", "ctx")),
        P(("fsdp", "ctx")),
        P(("rep", "fsdp"), "ctx", None),
    )
    out_specs = (
        P(("rep", "fsdp"), "ctx", None),
        P(("rep", "fsdp"), "ctx", None),
        P(("fsdp", "ctx"), None),
        P(("fsdp", "ctx")),
        P(("fsdp", "ctx")),
        P(("fsdp", "ctx"), None),
        P(("fsdp", "ctx")),
        P(("fsdp", "ctx"), None),
        P(("fsdp", "ctx")),
        P(("fsdp", "ctx"), None),
        P(("fsdp", "ctx")),
        P(("fsdp", "ctx")),
        P(("fsdp", "ctx")),
        P(("fsdp", "ctx")),
        P(("fsdp", "ctx")),
    )
    return jax.shard_map(shards, mesh=mesh, in_specs=in_specs, out_specs=out_specs, check_vma=False)
```

profile of v0, /device:TPU:0, one launch (start us, length us, event | category | flops | bytes accessed | tf_op | source)
XLA Modules:
  0.0 2958.3 jit_solution(15318190174671491095)
XLA Ops:
  8.0 23.2 all-gather.5
  48.7 18.9 all-gather.2
  88.3 52.7 %all-gather.18.cloned.1.call-done = bf16[2048,6144]{1,0:T(8,128)(2,1)} async-done(((bf16[128,6144]{1,0:T(8,128)(2,1)}), bf16[2048,6144]{1,0:T(8,128)(2,1)}) %all-gather.18.cloned.1.call-update) | async-done | bytes 25165840 | tf_op jit(solution)/shard_map/all_gather | solution.py:59
  162.6 20.3 all-gather.6
  200.3 18.7 all-gather.8
  251.6 18.6 select_reduce_fusion
  312.6 161.2 %all-gather.22.cloned.1.call-done = bf16[2048,8192]{1,0:T(8,128)(2,1)} async-done(((bf16[128,8192]{1,0:T(8,128)(2,1)}), bf16[2048,8192]{1,0:T(8,128)(2,1)}) %all-gather.22.cloned.1.call-update) | async-done | bytes 33554448 | tf_op jit(solution)/shard_map/all_gather | solution.py:104
  473.9 20.1 convolution_add_fusion
  493.9 149.5 %all-gather.24.cloned.1.call-done = bf16[8192,2048]{1,0:T(8,128)(2,1)} async-done(((bf16[512,2048]{1,0:T(8,128)(2,1)}), bf16[8192,2048]{1,0:T(8,128)(2,1)}) %all-gather.24.cloned.1.call-update) | async-done | bytes 33554448 | tf_op jit(solution)/shard_map/all_gather | solution.py:106
  643.4 33.6 %convert_reduce_fusion = (f32[8192]{0:T(1024)}, bf16[256,8192]{1,0:T(8,128)(2,1)}) fusion(f32[256,8192]{1,0:T(8,128)} %convolution_add_fusion, bf16[8192,2048]{1,0:T(8,128)(2,1)} %all-gather.24.cloned.1.call-done, bf16[1,256,2048]{2,1,0:T(8,128)(2,1)S(1)} %copy-done.10), kind=kOutput, calls=%fused_computation.24 | convolution fusion | flops 8745115648 | bytes 47218688 | tf_op jit(solution)/shard_map/rd,fd->rf/dot_general | solution.py:135
  677.0 18.6 multiply_reduce_fusion.1
  741.2 61.5 %fusion.27 = bf16[32,64,1024]{2,1,0:T(8,128)(2,1)} fusion(bf16[256,32,64]{0,2,1:T(8,128)(2,1)} %bitcast.141, f32[32,256,1024]{2,1,0:T(8,128)} %fusion.88, f32[32,256,1024]{2,1,0:T(8,128)} %get-tuple-element.53, f32[32,256]{1,0:T(8,128)S(1)} %log_add_fusion, pred[256,1024]{1,0:T(8,128)(4,1)S(1)} %fusion.64), kind=kOutput, calls=%fused_computation.43 | convolution fusion | flops 1151345664 | bytes 72646656 | tf_op jit(solution)/shard_map/shqk,sqhe->skhe/dot_general | solution.py:180
  812.6 61.4 %convert_reduce_fusion.5 = (f32[32,64]{1,0:T(8,128)}, bf16[32,64,256]{2,1,0:T(8,128)(2,1)S(1)}) fusion(bf16[1024,32,64]{0,2,1:T(8,128)(2,1)} %bitcast.134, f32[32,256,1024]{2,1,0:T(8,128)} %fusion.88, f32[32,256,1024]{2,1,0:T(8,128)} %get-tuple-element.53, f32[32,256]{1,0:T(8,128)S(1)} %log_add_fusion, pred[256,1024]{1,0:T(8,128)(4,1)S(1)} %fusion.64), kind=kOutput, calls=%fused_computation.75 | convolution fusion | flops 1150819328 | bytes 72654848 | tf_op jit(solution)/shard_map/shqk,skhe->sqhe/dot_general | solution.py:179
  874.1 20.8 fusion.56
  894.9 34.6 %fusion.58 = f32[8192,2048]{1,0:T(8,128)} fusion(bf16[1,256,2048]{2,1,0:T(8,128)(2,1)S(1)} %copy-done.10, f32[256,8192]{1,0:T(8,128)} %convolution_add_fusion), kind=kOutput, calls=%fused_computation.85 | convolution fusion | flops 8726249472 | bytes 76546048 | tf_op jit(solution)/shard_map/rf,rd->fd/dot_general | solution.py:133
  931.1 26.1 fusion.81
  959.8 20.3 all-gather.10
  980.1 50.4 %reduce-scatter.13.cloned.1.call-done = f32[128,2048]{1,0:T(8,128)} async-done(((f32[2048,2048]{1,0:T(8,128)}), f32[128,2048]{1,0:T(8,128)}) %reduce-scatter.13.cloned.1.call-update) | async-done | bytes 1048592 | tf_op jit(solution)/shard_map/reduce_scatter | solution.py:215
  1032.5 468.8 %reduce-scatter.11.cloned.1.call-done = f32[128,6144]{1,0:T(8,128)} async-done(((f32[2048,6144]{1,0:T(8,128)}), f32[128,6144]{1,0:T(8,128)}) %reduce-scatter.11.cloned.1.call-update) | async-done | bytes 3145744 | tf_op jit(solution)/shard_map/reduce_scatter | solution.py:212
  1504.6 637.3 %reduce-scatter.17.cloned.1.call-done = f32[512,2048]{1,0:T(8,128)} async-done(((f32[8192,2048]{1,0:T(8,128)}), f32[512,2048]{1,0:T(8,128)}) %reduce-scatter.17.cloned.1.call-update) | async-done | bytes 4194320 | tf_op jit(solution)/shard_map/reduce_scatter | solution.py:150
  2145.7 636.3 %reduce-scatter.15.cloned.1.call-done = f32[128,8192]{1,0:T(8,128)} async-done(((f32[2048,8192]{1,0:T(8,128)}), f32[128,8192]{1,0:T(8,128)}) %reduce-scatter.15.cloned.1.call-update) | async-done | bytes 4194320 | tf_op jit(solution)/shard_map/reduce_scatter | solution.py:148
  2785.8 31.7 %fusion.40 = f32[1,256,2048]{2,1,0:T(8,128)} fusion(f32[256,2048]{1,0:T(8,128)S(1)} %copy-done.4, bf16[8192,2048]{1,0:T(8,128)(2,1)} %all-gather.24.cloned.1.call-done, f32[2048]{0:T(1024)S(1)} %bitcast.159, f32[256,8192]{1,0:T(8,128)} %convolution_add_fusion), kind=kOutput, calls=%fused_computation.57 | convolution fusion | flops 8727298048 | bytes 46145536 | tf_op jit(solution)/shard_map/dot_general | solution.py:121
  2837.6 60.8 %all-reduce.9 = (bf16[2048]{0:T(1024)(128)(2,1)S(1)}, bf16[2048]{0:T(1024)(128)(2,1)S(1)}, bf16[2048]{0:T(1024)(128)(2,1)S(1)}, bf16[8192]{0:T(1024)(128)(2,1)S(...) all-reduce(f32[2048]{0:T(1024)S(1)} %reduce_sum.189, ...), channel_id=7, replica_groups=mesh['rep'=2,'fsdp'=4,'ctx'=4] {'fsdp','ctx'}, use_global_device_ids=true, to_apply=%region_16.17.clone | all-reduce | flops 24576 | bytes 147456
  2908.9 30.5 %all-reduce.14.cloned.1.call-done = (bf16[128,6144]{1,0:T(8,128)(2,1)}, bf16[128,2048]{1,0:T(8,128)(2,1)}, bf16[128,8192]{1,0:T(8,128)(2,1)}, bf16[512,2048]{1,0:T(8,128)(2,1)}) async-done(((bf16[128,6144]{1,0:T(8,128)(2,1)}, bf16[128,2048]{1,0:T(8,128)(2,1)}, bf16[128,8192]{1,0:T(8,128)(2,1)}, bf16[512,2048]{1,0:T(8,128)(2,1)}), (bf16[128,6144]{1,0:T(8,128)(2,1)}, bf16[128,2048]{1,0:T(8,128)(2,1)}, ...) | async-done | bytes 6291472 | tf_op jit(solution)/shard_map/psum | solution.py:221
  (209 shorter events, 265.9 us)
Async XLA Ops:
  7.2 133.9 %all-gather.18.cloned.1.call-start = ((), (), s32[]{:S(2)}) async-start(), calls=%async_computation.6 | async-start | bytes 26738688 | tf_op jit(solution)/shard_map/all_gather | solution.py:59
  7.9 230.5 %all-gather.26.cloned.1.call-start = ((), (), s32[]{:S(2)}) async-start(), calls=%async_computation.16 | async-start | bytes 5242880 | tf_op jit(solution)/shard_map/all_gather | solution.py:78
  67.6 85.6 %copy-start.15 = (f32[16,1,128]{2,1,0:T(1,128)}, f32[16,1,128]{2,1,0:T(1,128)S(1)}, u32[]{:S(2)}) copy-start(f32[16,1,128]{2,1,0:T(1,128)S(1)} %convert_element_type.330) | copy-start | bytes 24580
  85.1 68.1 %copy-start.18 = (f32[16,1,128]{2,1,0:T(1,128)}, f32[16,1,128]{2,1,0:T(1,128)S(1)}, u32[]{:S(2)}) copy-start(f32[16,1,128]{2,1,0:T(1,128)S(1)} %convert_element_type.331) | copy-start | bytes 24580
  86.6 66.5 %copy-start.24 = (f32[256]{0:T(256)}, f32[256]{0:T(256)S(1)}, u32[]{:S(2)}) copy-start(f32[256]{0:T(256)S(1)} %broadcast_multiply_fusion.1) | copy-start | bytes 3076
  88.3 64.9 %copy-start.39 = (f32[256]{0:T(256)}, f32[256]{0:T(256)S(1)}, u32[]{:S(2)}) copy-start(f32[256]{0:T(256)S(1)} %fusion.47) | copy-start | bytes 3076
  88.3 64.8 %copy-start.27 = (f32[256]{0:T(256)}, f32[256]{0:T(256)S(1)}, u32[]{:S(2)}) copy-start(f32[256]{0:T(256)S(1)} %fusion.65) | copy-start | bytes 3076
  157.3 87.9 %all-gather.28.cloned.1.call-start = ((), (), s32[]{:S(2)}) async-start(), calls=%async_computation.17 | async-start | bytes 5242880 | tf_op jit(solution)/shard_map/all_gather | solution.py:77
  160.1 145.9 %all-gather.20.cloned.1.call-start = ((), (), s32[]{:S(2)}) async-start(), calls=%async_computation.7 | async-start | bytes 8912896 | tf_op jit(solution)/shard_map/all_gather | solution.py:62
  160.7 313.2 %all-gather.22.cloned.1.call-start = ((), (), s32[]{:S(2)}) async-start(), calls=%async_computation.8 | async-start | bytes 35651584 | tf_op jit(solution)/shard_map/all_gather | solution.py:104
  161.3 482.1 %all-gather.24.cloned.1.call-start = ((), (), s32[]{:S(2)}) async-start(), calls=%async_computation.9 | async-start | bytes 35651584 | tf_op jit(solution)/shard_map/all_gather | solution.py:106
  161.9 712.2 %reduce-scatter.9.cloned.1.call-start = ((), (), s32[]{:S(2)}) async-start(), calls=%async_computation.11 | async-start | bytes 5242880 | tf_op jit(solution)/shard_map/reduce_scatter | solution.py:193
  200.3 495.3 %copy-start.20 = (f32[16,1,128]{2,1,0:T(1,128)}, f32[16,1,128]{2,1,0:T(1,128)S(1)}, u32[]{:S(2)}) copy-start(f32[16,1,128]{2,1,0:T(1,128)S(1)} %convert_element_type.335) | copy-start | bytes 24580
  219.0 254.9 %copy-start.22 = (f32[16,1,128]{2,1,0:T(1,128)}, f32[16,1,128]{2,1,0:T(1,128)S(1)}, u32[]{:S(2)}) copy-start(f32[16,1,128]{2,1,0:T(1,128)S(1)} %convert_element_type.336) | copy-start | bytes 24580
  312.2 383.4 %copy-start.3 = (f32[256,2048]{1,0:T(8,128)}, f32[256,2048]{1,0:T(8,128)S(1)}, u32[]{:S(2)}) copy-start(f32[256,2048]{1,0:T(8,128)S(1)} %get-tuple-element.55) | copy-start | bytes 6291460
  312.2 383.4 %copy-start.30 = (f32[256]{0:T(256)}, f32[256]{0:T(256)S(1)}, u32[]{:S(2)}) copy-start(f32[256]{0:T(256)S(1)} %broadcast_multiply_fusion) | copy-start | bytes 3076
  312.6 383.0 %copy-start.32 = (f32[256]{0:T(256)}, f32[256]{0:T(256)S(1)}, u32[]{:S(2)}) copy-start(f32[256]{0:T(256)S(1)} %fusion.66) | copy-start | bytes 3076
  473.9 169.6 %copy-start.10 = (bf16[1,256,2048]{2,1,0:T(8,128)(2,1)S(1)}, bf16[1,256,2048]{2,1,0:T(8,128)(2,1)}, u32[]{:S(2)}) copy-start(bf16[1,256,2048]{2,1,0:T(8,128)(2,1)} %param.31) | copy-start | bytes 3145732
  723.9 150.1 %reduce-scatter.7.cloned.1.call-start = ((), (), s32[]{:S(2)}) async-start(), calls=%async_computation.10 | async-start | bytes 5242880 | tf_op jit(solution)/shard_map/reduce_scatter | solution.py:187
  802.7 227.7 %reduce-scatter.13.cloned.1.call-start = ((), (), s32[]{:S(2)}) async-start(), calls=%async_computation.13 | async-start | bytes 17825792 | tf_op jit(solution)/shard_map/reduce_scatter | solution.py:215
  812.5 688.8 %reduce-scatter.11.cloned.1.call-start = ((), (), s32[]{:S(2)}) async-start(), calls=%async_computation.12 | async-start | bytes 53477376 | tf_op jit(solution)/shard_map/reduce_scatter | solution.py:212
  894.9 1247.0 %reduce-scatter.17.cloned.1.call-start = ((), (), s32[]{:S(2)}) async-start(), calls=%async_computation.15 | async-start | bytes 71303168 | tf_op jit(solution)/shard_map/reduce_scatter | solution.py:150
  929.5 1852.5 %reduce-scatter.15.cloned.1.call-start = ((), (), s32[]{:S(2)}) async-start(), calls=%async_computation.14 | async-start | bytes 71303168 | tf_op jit(solution)/shard_map/reduce_scatter | solution.py:148
  957.2 1982.1 %all-reduce.14.cloned.1.call-start = ((), (), s32[]{:S(2)}) async-start(), calls=%async_computation.18 | async-start | bytes 12582912 | tf_op jit(solution)/shard_map/psum | solution.py:221
  (38 other events, 792.2 us)
Sparse Core Ops, SparseCore 0:
  9.6 131.3 all-gather.17
  157.4 34.7 all-gather.25
  194.3 34.6 all-gather.27
  231.1 74.8 all-gather.19
  307.5 166.3 all-gather.21
  475.3 168.0 all-gather.23
  724.0 44.4 reduce-scatter.8
  802.8 44.7 reduce-scatter.6
  851.7 178.6 reduce-scatter.12
  1034.5 466.7 reduce-scatter.10
  1505.6 636.2 reduce-scatter.16
  2146.0 635.9 reduce-scatter.14
  2785.9 153.4 all-reduce.13
where the time goes:
time: 2960 us
  waiting for transfers between devices  2190 us (74%)
  matrix products  424 us (14%)
  blocking collectives  237 us (8%)
  other arithmetic  59.3 us (2%)
    reduce_scatter x1, waiting for transfers between devices, shards(): lax.psum_scatter(shrink_term, ('fsdp', 'ctx'), scatter_dimension=0, tiled...  637 us
    reduce_scatter x1, waiting for transfers between devices, shards(): lax.psum_scatter(expand_term, ('fsdp', 'ctx'), scatter_dimension=0, tiled...  636 us
    reduce_scatter x1, waiting for transfers between devices, shards(): lax.psum_scatter(joined_term, ('fsdp', 'ctx'), scatter_dimension=0, tiled...  469 us
    all_gather x1, waiting for transfers between devices, shards(): lax.all_gather(expand_weight, ('fsdp', 'ctx'), axis=0, tiled=True)  161 us
    all_gather x1, waiting for transfers between devices, shards(): lax.all_gather(shrink_weight, ('fsdp', 'ctx'), axis=0, tiled=True)  149 us
    dot_general x1, matrix products, shards(): jnp.einsum('shqk,sqhe->skhe', d_raw, query_heads, preferred_element_type=...  61.5 us
    dot_general x1, matrix products, shards(): jnp.einsum('shqk,skhe->sqhe', d_raw, key_heads, preferred_element_type=jn...  61.4 us
    unnamed x1, blocking collectives  60.8 us
  transfers between devices with their start and end apart: 13, of which 9 were waited for; matrix products, arithmetic and copies ran while one was open for 13% of the time, Pallas kernels for 0%

commit v1 on v0

v1 whole, which is shorter than its diff:
```python
import jax
import jax.numpy as jnp
from jax import lax
from jax.sharding import PartitionSpec as P

H = 32
HD = 64
TP = ("rep", "ctx")
BF = jnp.bfloat16
F32 = jnp.float32


def dot(a, b, ca, cb):
    return lax.dot_general(a, b, (((ca,), (cb,)), ((), ())), preferred_element_type=F32)


def norm_stats(values):
    average = jnp.mean(values, axis=-1, keepdims=True)
    centred = values - average
    variance = jnp.mean(centred * centred, axis=-1, keepdims=True)
    inverse = lax.rsqrt(variance + 1e-05)
    return centred * inverse, inverse


def norm_back(normed, inverse, gain, grad):
    u = grad * gain
    mean_u = jnp.mean(u, axis=-1, keepdims=True)
    mean_un = jnp.mean(u * normed, axis=-1, keepdims=True)
    return (u - mean_u - normed * mean_un) * inverse


def gelu(values):
    return 0.5 * values * (1.0 + lax.erf(values * 0.7071067811865476))


def gelu_slope(values):
    density = jnp.exp(values * values * -0.5) * 0.3989422804014327
    return 0.5 * (1.0 + lax.erf(values * 0.7071067811865476)) + values * density


def gather_tp(x):
    return lax.all_gather(x, TP, axis=0, tiled=True)


def scatter_tp(x):
    return lax.psum_scatter(x, TP, scatter_dimension=0, tiled=True)


def swap_tp(x):
    return lax.all_to_all(x, TP, 0, 0, tiled=True)


def attention_logits(q, k, heads, prefix):
    raw = jnp.einsum("sqhe,skhe->shqk", q, k, preferred_element_type=F32)
    length = k.shape[1]
    place = jnp.arange(length, dtype=jnp.int32)
    distance = jnp.abs(place[:, None] - place[None, :]).astype(F32)
    allowed = (place[None, None, :] <= place[None, :, None]) | (place[None, None, :] < prefix[:, None, None])
    slopes = jnp.exp2(-8.0 * (heads.astype(F32) + 1.0) / H)
    logits = raw * 0.125 - slopes[None, :, None, None] * distance[None, None]
    return logits, allowed[:, None]


def attention_forward(q, k, v, heads, prefix):
    logits, allowed = attention_logits(q, k, heads, prefix)
    masked = jnp.where(allowed, logits, -1e30)
    largest = jnp.max(masked, axis=-1, keepdims=True)
    exponent = jnp.exp(masked - largest)
    totals = jnp.sum(exponent, axis=-1, keepdims=True)
    probs = (exponent / totals).astype(BF)
    out = jnp.einsum("shqk,skhe->sqhe", probs, v, preferred_element_type=F32).astype(BF)
    return out, largest + jnp.log(totals)


def attention_backward(q, k, v, lse, d_out, heads, prefix):
    logits, allowed = attention_logits(q, k, heads, prefix)
    probs = jnp.where(allowed, jnp.exp(logits - lse), 0.0)
    d_probs = jnp.einsum("sqhe,skhe->shqk", d_out, v, preferred_element_type=F32)
    weighted = jnp.sum(probs * d_probs, axis=-1, keepdims=True)
    d_raw = (probs * (d_probs - weighted) * 0.125).astype(BF)
    low = probs.astype(BF)
    d_q = jnp.einsum("shqk,skhe->sqhe", d_raw, k, preferred_element_type=F32).astype(BF)
    d_k = jnp.einsum("shqk,sqhe->skhe", d_raw, q, preferred_element_type=F32).astype(BF)
    d_v = jnp.einsum("shqk,sqhe->skhe", low, d_out, preferred_element_type=F32).astype(BF)
    return d_q, d_k, d_v


def shards(
    sizes,
    inputs,
    prefix,
    joined_weight,
    query_bias,
    value_bias,
    dense_weight,
    dense_bias,
    expand_weight,
    expand_bias,
    shrink_weight,
    shrink_bias,
    first_gain,
    first_shift,
    second_gain,
    second_shift,
    cotangent,
):
    R, F, C = sizes
    N = R * C
    rep = lax.axis_index("rep")
    ctx = lax.axis_index("ctx")
    S, T, D = inputs.shape
    t = S * T
    B = joined_weight.shape[0]
    FFB = shrink_weight.shape[0]
    FF = FFB * F * C
    E = FFB // R
    W = D // N
    aligned = (B // R) % HD == 0

    def split_columns(weight, groups):
        n = weight.shape[1] // groups
        if aligned or groups == 1:
            pieces = weight.reshape(B, groups, F, C, R, n // (F * C * R))
            mine = lax.dynamic_index_in_dim(pieces, rep, 4, keepdims=False)
            mine = mine.transpose(3, 0, 1, 2, 4)
        else:
            pieces = weight.reshape(B, groups, R, C, n // (C * R))
            mine = lax.dynamic_index_in_dim(pieces, rep, 2, keepdims=False)
            mine = mine.transpose(2, 0, 1, 3)
        return mine.reshape(C, B, groups * n // N)

    def columns(weight, groups):
        blocks = lax.all_to_all(split_columns(weight, groups), "ctx", 0, 0, tiled=True)
        return lax.all_gather(blocks.reshape(C * B, -1), "fsdp", axis=0, tiled=True)

    def join_columns(grad, groups):
        part = lax.psum_scatter(grad.astype(BF), "fsdp", scatter_dimension=0, tiled=True)
        blocks = lax.all_to_all(part.reshape(C, B, -1), "ctx", 0, 0, tiled=True)
        both = lax.all_gather(blocks, "rep", axis=0, tiled=False)
        if aligned or groups == 1:
            both = both.reshape(R, C, B, groups, F, -1).transpose(2, 3, 4, 1, 0, 5)
        else:
            both = both.reshape(R, C, B, groups, -1).transpose(2, 3, 0, 1, 4)
        return both.reshape(B, -1).astype(F32)

    def half_rows(weight):
        n = weight.shape[0] // R
        return lax.dynamic_slice_in_dim(weight, rep * n, n, 0)

    def join_rows(part):
        return lax.all_gather(part, "rep", axis=0, tiled=True).astype(F32)

    small = jnp.concatenate(
        [first_gain, first_shift, second_gain, second_shift, dense_bias, shrink_bias, query_bias, value_bias, expand_bias]
    )
    small = lax.all_gather(small, ("fsdp", "ctx"), axis=0, tiled=False).astype(F32)
    gain_one, shift_one, gain_two, shift_two, dbias, sbias, qbias, vbias = [
        small[:, i * B : (i + 1) * B].reshape(D) for i in range(8)
    ]
    ebias = small[:, 8 * B :].reshape(F, C, R, E)
    ebias = lax.dynamic_index_in_dim(lax.dynamic_index_in_dim(ebias, ctx, 1, False), rep, 1, False).reshape(F * E)

    def my_features(vector):
        if aligned:
            v = vector.reshape(F, C, R, -1)
            return lax.dynamic_index_in_dim(lax.dynamic_index_in_dim(v, ctx, 1, False), rep, 1, False).reshape(W)
        return lax.dynamic_slice_in_dim(vector, (rep * C + ctx) * W, W, 0)

    my_heads = my_features(jnp.repeat(jnp.arange(H, dtype=jnp.int32), HD)).reshape(-1, HD)[:, 0]
    prefix_all = lax.all_gather(prefix, "rep", axis=0, tiled=True)

    joined_cols = columns(joined_weight, 3)
    dense_rows = lax.all_gather(half_rows(dense_weight), "fsdp", axis=0, tiled=True) if aligned else None
    expand_cols = columns(expand_weight, 1)
    shrink_rows = lax.all_gather(half_rows(shrink_weight), "fsdp", axis=0, tiled=True)
    if aligned:
        dense_all = gather_tp(dense_rows)
    else:
        dense_all = lax.all_gather(dense_weight, ("fsdp", "ctx"), axis=0, tiled=True)

    def to_sequences(a):
        return a.reshape(R, C, S, T, -1).transpose(0, 2, 1, 3, 4).reshape(R * S, C * T, -1)

    def from_sequences(a):
        return a.reshape(R, S, C, T, -1).transpose(0, 2, 1, 3, 4).reshape(N * t, -1)

    start = inputs.astype(F32).reshape(t, D)
    n1, inv1 = norm_stats(start)
    a1 = (n1 * gain_one + shift_one).astype(BF)
    a1_all = gather_tp(a1)
    g = cotangent.reshape(t, D)
    g_all = gather_tp(g)
    qkv = dot(a1_all, joined_cols, 1, 0)
    q = (qkv[:, :W] + my_features(qbias)).astype(BF)
    k = qkv[:, W : 2 * W].astype(BF)
    v = (qkv[:, 2 * W :] + my_features(vbias)).astype(BF)
    heads = lambda a: to_sequences(a).reshape(R * S, C * T, W // HD, HD)
    q, k, v = heads(q), heads(k), heads(v)
    out, lse = attention_forward(q, k, v, my_heads, prefix_all)
    o = swap_tp(from_sequences(out).reshape(N, t, W))
    o = o.transpose(1, 0, 2).reshape(t, D)
    midway = start + dot(o, dense_all, 1, 0) + dbias

    n2, inv2 = norm_stats(midway)
    a2 = (n2 * gain_two + shift_two).astype(BF)
    a2_all = gather_tp(a2)
    expanded = dot(a2_all, expand_cols, 1, 0) + ebias
    act = gelu(expanded).astype(BF)
    branch = scatter_tp(dot(act, shrink_rows, 1, 0).astype(BF))
    layer_output = midway + branch.astype(F32) + sbias

    g_float = g.astype(F32)
    d_act = dot(g_all, shrink_rows, 1, 1)
    d_exp = (d_act * gelu_slope(expanded)).astype(BF)
    d_a2 = scatter_tp(dot(d_exp, expand_cols, 1, 1).astype(BF)).astype(F32)
    shrink_grad = dot(act, g_all, 0, 0).astype(BF)
    expand_grad = dot(a2_all, d_exp, 0, 0)
    ebias_grad = jnp.sum(d_exp.astype(F32), axis=0)
    sbias_grad = jnp.sum(g_float, axis=0)
    d_mid = g_float + norm_back(n2, inv2, gain_two, d_a2)
    gain_two_grad = jnp.sum(d_a2 * n2, axis=0)
    shift_two_grad = jnp.sum(d_a2, axis=0)
    d_att = d_mid.astype(BF)

    dense_grad = dot(o, d_att, 0, 0)
    dbias_grad = jnp.sum(d_att.astype(F32), axis=0)
    d_o = dot(d_att, dense_all, 1, 1).astype(BF)
    d_o = swap_tp(d_o.reshape(t, N, W).transpose(1, 0, 2)).reshape(N * t, W)
    d_q, d_k, d_v = attention_backward(q, k, v, lse, heads(d_o), my_heads, prefix_all)
    d_qkv = jnp.concatenate([from_sequences(a.reshape(R * S, C * T, W)) for a in (d_q, d_k, d_v)], axis=1)
    d_a1 = scatter_tp(dot(d_qkv, joined_cols, 1, 1).astype(BF)).astype(F32)
    joined_grad = dot(a1_all, d_qkv, 0, 0)
    qkv_bias_grad = jnp.sum(d_qkv.astype(F32), axis=0)
    input_gradient = d_mid + norm_back(n1, inv1, gain_one, d_a1)
    gain_one_grad = jnp.sum(d_a1 * n1, axis=0)
    shift_one_grad = jnp.sum(d_a1, axis=0)

    shrink_out = join_rows(lax.psum_scatter(shrink_grad, "fsdp", scatter_dimension=0, tiled=True))
    expand_out = join_columns(expand_grad, 1)
    if aligned:
        part = scatter_tp(dense_grad.astype(BF))
        dense_out = join_rows(lax.psum_scatter(part, "fsdp", scatter_dimension=0, tiled=True))
    else:
        part = lax.psum_scatter(dense_grad.astype(BF), ("fsdp", "ctx"), scatter_dimension=0, tiled=True)
        dense_out = lax.psum(part, "rep").astype(F32)
    joined_out = join_columns(joined_grad, 3)

    def spread(vector, width):
        if aligned or width != D:
            full = jnp.zeros((F, C, R, width // (F * C * R)), F32)
            full = lax.dynamic_update_slice(full, vector.reshape(F, 1, 1, -1), (0, ctx, rep, 0))
        else:
            full = lax.dynamic_update_slice_in_dim(jnp.zeros((width,), F32), vector, (rep * C + ctx) * W, 0)
        return full.reshape(F * C, -1)

    tokens = [gain_one_grad, shift_one_grad, gain_two_grad, shift_two_grad, dbias_grad, sbias_grad]
    rows = [a.reshape(F * C, B) for a in tokens]
    rows += [spread(qkv_bias_grad[:W], D), spread(qkv_bias_grad[2 * W :], D), spread(ebias_grad, FF)]
    little = jnp.concatenate(rows, axis=1)
    little = lax.psum(lax.psum_scatter(little, ("fsdp", "ctx"), scatter_dimension=0, tiled=True), "rep").reshape(-1)
    gain_one_out, shift_one_out, gain_two_out, shift_two_out, dbias_out, sbias_out, qbias_out, vbias_out = [
        little[i * B : (i + 1) * B] for i in range(8)
    ]
    ebias_out = little[8 * B :]

    return (
        layer_output.reshape(S, T, D),
        input_gradient.reshape(S, T, D),
        joined_out,
        qbias_out,
        vbias_out,
        dense_out,
        dbias_out,
        expand_out,
        ebias_out,
        shrink_out,
        sbias_out,
        gain_one_out,
        shift_one_out,
        gain_two_out,
        shift_two_out,
    )


def solution(mesh):
    sizes = (mesh.shape["rep"], mesh.shape["fsdp"], mesh.shape["ctx"])
    tokens = P(("rep", "fsdp"), "ctx", None)
    matrix = P(("fsdp", "ctx"), None)
    vector = P(("fsdp", "ctx"))
    in_specs = (
        tokens,
        P(("rep", "fsdp")),
        matrix,
        vector,
        vector,
        matrix,
        vector,
        matrix,
        vector,
        matrix,
        vector,
        vector,
        vector,
        vector,
        vector,
        tokens,
    )
    out_specs = (
        tokens,
        tokens,
        matrix,
        vector,
        vector,
        matrix,
        vector,
        matrix,
        vector,
        matrix,
        vector,
        vector,
        vector,
        vector,
        vector,
    )

    def step(*arrays):
        return shards(sizes, *arrays)

    return jax.shard_map(step, mesh=mesh, in_specs=in_specs, out_specs=out_specs, check_vma=False)
```

time: 2960 us -> 1320 us (0.45)
  waiting for transfers between devices: 2190 us -> 699 us
  blocking collectives: 237 us -> 91.5 us
  matrix products: 424 us -> 322 us
  local copies, waits for them, and re-layouts: 25.5 us -> 112 us
    reduce_scatter x6 -> x8, waiting for transfers between devices: 1790 us -> 288 us  [the longest x4 245 us: scatter_tp(): return lax.psum_scatter(x, TP, scatter_dimension=0, tiled=True)]
    all_gather x9 -> x2, blocking collectives: 171 us -> 30 us  [the longest x1 21.2 us: shards(): lax.all_gather(small, ('fsdp', 'ctx'), axis=0, tiled=False).astype(F32)]
    dot_general x18, matrix products: 424 us -> 322 us  [the longest x12 138 us: dot(): lax.dot_general(a, b, (((ca,), (cb,)), ((), ())), preferred_element_type=...]
    unnamed x13 -> x21, waiting for transfers between devices: 2.41 us -> 80.7 us
    unnamed x1, blocking collectives: 60.8 us -> 4.25 us
    all_to_all x0 -> x3, blocking collectives: none -> 52.3 us  [the longest x1 18.8 us: join_columns(): blocks = lax.all_to_all(part.reshape(C, B, -1), 'ctx', 0, 0, tiled=True)]
    all_gather x6 -> x11, waiting for transfers between devices: 369 us -> 322 us  [the longest x4 166 us: gather_tp(): return lax.all_gather(x, TP, axis=0, tiled=True)]
    another operation x0 -> x13, local copies, waits for them, and re-layouts: none -> 30.8 us  [the longest x7 27 us: shards(): heads = lambda a: to_sequences(a).reshape(R * S, C * T, W // HD, HD)]
  transfers between devices with their start and end apart: 13 -> 23, of which waited for: 9 -> 18; matrix products, arithmetic and copies ran while one was open for 13% -> 35% of each run, Pallas kernels for 0% -> 0%
where the time goes in v1:
time: 1320 us; the launch traced here: 1310 us
  waiting for transfers between devices  699 us (53%)
  matrix products  322 us (24%)
  local copies, waits for them, and re-layouts  112 us (8%)
  blocking collectives  91.5 us (7%)
  other arithmetic  59.9 us (5%)
  between operations  15.9 us (1%)
    reduce_scatter x4, waiting for transfers between devices, scatter_tp(): return lax.psum_scatter(x, TP, scatter_dimension=0, tiled=True)  245 us
    all_gather x4, waiting for transfers between devices, gather_tp(): return lax.all_gather(x, TP, axis=0, tiled=True)  166 us
    dot_general x12, matrix products, dot(): lax.dot_general(a, b, (((ca,), (cb,)), ((), ())), preferred_element_type=...  138 us
    unnamed x21, waiting for transfers between devices  80.7 us
    all_gather x1, waiting for transfers between devices, shards(): lax.all_gather(half_rows(shrink_weight), 'fsdp', axis=0, tiled=True)  66.5 us
    dot_general x1, matrix products, attention_backward(): jnp.einsum('shqk,sqhe->skhe', d_raw, q, preferred_element_type=F32)  55.8 us
    dot_general x1, matrix products, attention_backward(): jnp.einsum('shqk,skhe->sqhe', d_raw, k, preferred_element_type=F32)  54.7 us
    all_gather x2, waiting for transfers between devices, join_columns(): both = lax.all_gather(blocks, 'rep', axis=0, tiled=False)  40.7 us
  transfers between devices with their start and end apart: 23, of which 18 were waited for; matrix products, arithmetic and copies ran while one was open for 35% of the time, Pallas kernels for 0%

profile of v1, /device:TPU:0, one launch (start us, length us, event | category | flops | bytes accessed | tf_op | source)
XLA Modules:
  0.0 1312.8 jit_solution(1803940489215172898)
XLA Ops:
  33.2 21.2 %all-gather.4 = bf16[16,1,1536]{2,1,0:T(2,128)(2,1)S(1)} all-gather(bf16[1,1,1536]{2,1,0:T(2,128)(2,1)S(1)} %reshape.335), channel_id=2, replica_groups=mesh['rep'=2,'fsdp'=4,'ctx'=4] {'fsdp','ctx'}, dimensions={0}, use_global_device_ids=true | all-gather | bytes 52224 | tf_op jit(solution)/shard_map/all_gather | solution.py:156
  106.2 55.5 %all-gather.17.cloned.1.call-done = bf16[2048,2048]{1,0:T(8,128)(2,1)} async-done(((bf16[256,2048]{1,0:T(8,128)(2,1)}), bf16[2048,2048]{1,0:T(8,128)(2,1)}) %all-gather.17.cloned.1.call-update) | async-done | bytes 8388624 | tf_op jit(solution)/shard_map/all_gather | solution.py:42
  200.1 22.8 %select_reduce_fusion = (f32[2,4,1024]{2,1,0:T(4,128)S(1)}, f32[2,4,1024,1024]{2,3,1,0:T(8,128)}) fusion(f32[4,1024,1024]{1,2,0:T(8,128)} %broadcast_multiply_fusion, pred[2,1024,1024]{1,2,0:T(8,128)(4,1)} %broadcast_or_fusion, bf16[2,1024,4,64]{1,3,2,0:T(8,128)(2,1)} %copy.112, bf16[2,1024,4,64]{1,3,2,0:T(8,128)(2,1)} %copy.113), kind=kOutput, calls=%fused_computation.8 | convolution fusion | flops 1107288064 | bytes 54558720 | tf_op jit(solution)/shard_map/sqhe,skhe->shqk/dot_general | solution.py:54
  222.9 19.0 %fusion.4 = f32[2,4,1024]{2,1,0:T(4,128)S(1)} fusion(f32[2,4,1024,1024]{2,3,1,0:T(8,128)} %get-tuple-element.92, f32[2,4,1024]{2,1,0:T(4,128)S(1)} %get-tuple-element.91, f32[4,1024,1024]{1,2,0:T(8,128)} %broadcast_multiply_fusion, pred[2,1024,1024]{1,2,0:T(8,128)(4,1)S(1)} %copy-done.2), kind=kLoop, calls=%fused_computation.9 | loop fusion | flops 41934848 | bytes 52494336 | tf_op jit(solution)/shard_map/reduce_sum | solution.py:69
  241.9 19.5 %fusion.72 = bf16[2,1024,4,64]{1,3,2,0:T(8,128)(2,1)S(1)} fusion(bf16[2,1024,4,64]{1,3,2,0:T(8,128)(2,1)S(1)} %copy-done.13, f32[2,4,1024,1024]{2,3,1,0:T(8,128)} %get-tuple-element.92, f32[2,4,1024]{2,1,0:T(4,128)S(1)} %fusion.4, f32[2,4,1024]{2,1,0:T(4,128)S(1)} %get-tuple-element.91, f32[4,1024,1024]{1,2,0:T(8,128)} %broadcast_multiply_fusion, ...), kind=kOutput, calls=%fused_computation.92 | convolution fusion | flops 1124597760 | bytes 54591488 | tf_op jit(solution)/shard_map/shqk,skhe->sqhe/dot_general | solution.py:71
  267.1 17.7 %all_to_all.31 = bf16[8,256,256]{1,2,0:T(8,128)(2,1)} all-to-all(bf16[8,256,256]{1,2,0:T(8,128)(2,1)S(1)} %copy.117), channel_id=1, replica_groups=mesh['rep'=2,'fsdp'=4,'ctx'=4] {'rep','ctx'}, dimensions={0} | all-to-all | bytes 2097152 | tf_op jit(solution)/shard_map/all_to_all | solution.py:50
  300.7 55.3 %all-gather.25.cloned.1.call-done = bf16[2048,2048]{1,0:T(8,128)(2,1)} async-done(((bf16[256,2048]{1,0:T(8,128)(2,1)}), bf16[2048,2048]{1,0:T(8,128)(2,1)}) %all-gather.25.cloned.1.call-update) | async-done | bytes 8388624 | tf_op jit(solution)/shard_map/all_gather | solution.py:42
  355.9 15.9 %multiply_convert_fusion.1 = (bf16[2048,1024]{1,0:T(8,128)(2,1)}, f32[2048,1024]{1,0:T(8,128)}) fusion(f32[1024]{0:T(1024)S(1)} %bitcast.232, bf16[2048,2048]{1,0:T(8,128)(2,1)} %all-gather.25.cloned.1.call-done, bf16[2048,1024]{1,0:T(8,128)(2,1)} %all-gather.27.cloned.1.call-done), kind=kOutput, calls=%fused_computation.22 | convolution fusion | flops 8602517504 | bytes 25169920 | tf_op jit(solution)/shard_map/dot_general | solution.py:14
  371.8 66.5 %all-gather.29.cloned.1.call-done = bf16[1024,2048]{1,0:T(8,128)(2,1)} async-done(((bf16[256,2048]{1,0:T(8,128)(2,1)}), bf16[1024,2048]{1,0:T(8,128)(2,1)}) %all-gather.29.cloned.1.call-update) | async-done | bytes 4194320 | tf_op jit(solution)/shard_map/all_gather | solution.py:175
  438.3 54.8 %all-gather.33.cloned.1.call-done = bf16[1,2048,2048]{2,1,0:T(8,128)(2,1)} async-done(((bf16[1,256,2048]{2,1,0:T(8,128)(2,1)}), bf16[1,2048,2048]{2,1,0:T(8,128)(2,1)}) %all-gather.33.cloned.1.call-update) | async-done | bytes 8388624 | tf_op jit(solution)/shard_map/all_gather | solution.py:42
  493.1 17.0 %convert_reduce_fusion = (f32[1024]{0:T(1024)}, bf16[2048,1024]{1,0:T(8,128)(2,1)S(1)}) fusion(f32[2048,1024]{1,0:T(8,128)} %get-tuple-element.96, f32[1024]{0:T(1024)S(1)} %bitcast.233, bf16[1024,2048]{1,0:T(8,128)(2,1)} %all-gather.29.cloned.1.call-done, bf16[1,2048,2048]{2,1,0:T(8,128)(2,1)} %all-gather.33.cloned.1.call-done), kind=kOutput, calls=%fused_computation.21 | convolution fusion | flops 8617196544 | bytes 25174016 | tf_op jit(solution)/shard_map/dot_general | solution.py:14
  552.3 42.2 %reduce-scatter.11.cloned.1.call-done = bf16[256,2048]{1,0:T(8,128)(2,1)} async-done(((bf16[2048,2048]{1,0:T(8,128)(2,1)}), bf16[256,2048]{1,0:T(8,128)(2,1)}) %reduce-scatter.11.cloned.1.call-update) | async-done | bytes 1048592 | tf_op jit(solution)/shard_map/reduce_scatter | solution.py:46
  597.3 72.2 %reduce-scatter.9.cloned.1.call-done = bf16[256,2048]{1,0:T(8,128)(2,1)} async-done(((bf16[2048,2048]{1,0:T(8,128)(2,1)}), bf16[256,2048]{1,0:T(8,128)(2,1)}) %reduce-scatter.9.cloned.1.call-update) | async-done | bytes 1048592 | tf_op jit(solution)/shard_map/reduce_scatter | solution.py:46
  704.2 18.3 %fusion.63 = bf16[2,1024,4,64]{1,3,2,0:T(8,128)(2,1)S(1)} fusion(bf16[2,1024,4,64]{1,0,3,2:T(2,128)(2,1)S(1)} %reshape_reshape_transpose_reshape_reshape.3, f32[2,4,1024,1024]{2,3,1,0:T(8,128)} %get-tuple-element.92, f32[2,4,1024]{2,1,0:T(4,128)S(1)} %bitcast.221, f32[4,1024,1024]{1,2,0:T(8,128)} %broadcast_multiply_fusion, ...), kind=kOutput, calls=%fused_computation.89 | convolution fusion | flops 1116209152 | bytes 54558720 | tf_op jit(solution)/shard_map/shqk,sqhe->skhe/dot_general | solution.py:84
  738.1 55.8 %fusion.66 = bf16[2,1024,4,64]{1,3,2,0:T(8,128)(2,1)} fusion(bf16[2,1024,4,64]{1,3,2,0:T(8,128)(2,1)} %copy.112, f32[2,4,1024,1024]{2,3,1,0:T(8,128)} %fusion.74, f32[2,4,1024,1024]{2,3,1,0:T(8,128)} %get-tuple-element.92, f32[2,4,1024]{2,1,0:T(4,128)S(1)} %bitcast.222, f32[4,1024,1024]{1,2,0:T(8,128)} %broadcast_multiply_fusion, ...), kind=kOutput, calls=%fused_computation.90 | convolution fusion | flops 1183327232 | bytes 88113152 | tf_op jit(solution)/shard_map/shqk,sqhe->skhe/dot_general | solution.py:83
  797.6 54.7 %fusion.69 = bf16[2,1024,4,64]{1,3,2,0:T(8,128)(2,1)} fusion(bf16[2,1024,4,64]{1,3,2,0:T(8,128)(2,1)S(1)} %copy-done.16, f32[2,4,1024,1024]{2,3,1,0:T(8,128)} %fusion.74, f32[2,4,1024,1024]{2,3,1,0:T(8,128)} %get-tuple-element.92, f32[2,4,1024]{2,1,0:T(4,128)S(1)} %bitcast.223, f32[4,1024,1024]{1,2,0:T(8,128)} %broadcast_multiply_fusion, ...), kind=kOutput, calls=%fused_computation.91 | convolution fusion | flops 1183327232 | bytes 88113152 | tf_op jit(solution)/shard_map/shqk,skhe->sqhe/dot_general | solution.py:82
  887.5 18.8 %all_to_all.32 = bf16[4,128,1024]{2,1,0:T(8,128)(2,1)} all-to-all(bf16[4,128,1024]{2,1,0:T(8,128)(2,1)} %bitcast.220), channel_id=1, replica_groups=mesh['rep'=2,'fsdp'=4,'ctx'=4] {'ctx'}, dimensions={0} | all-to-all | bytes 2097152 | tf_op jit(solution)/shard_map/all_to_all | solution.py:138
  906.3 22.6 %reduce-scatter.15.cloned.1.call-done = bf16[512,768]{1,0:T(8,128)(2,1)} async-done(((bf16[2048,768]{1,0:T(8,128)(2,1)}), bf16[512,768]{1,0:T(8,128)(2,1)}) %reduce-scatter.15.cloned.1.call-update) | async-done | bytes 786448 | tf_op jit(solution)/shard_map/reduce_scatter | solution.py:137
  945.1 58.4 %reduce-scatter.13.cloned.1.call-done = bf16[256,2048]{1,0:T(8,128)(2,1)} async-done(((bf16[2048,2048]{1,0:T(8,128)(2,1)}), bf16[256,2048]{1,0:T(8,128)(2,1)}) %reduce-scatter.13.cloned.1.call-update) | async-done | bytes 1048592 | tf_op jit(solution)/shard_map/reduce_scatter | solution.py:46
  1006.7 71.9 %reduce-scatter.17.cloned.1.call-done = bf16[256,2048]{1,0:T(8,128)(2,1)} async-done(((bf16[2048,2048]{1,0:T(8,128)(2,1)}), bf16[256,2048]{1,0:T(8,128)(2,1)}) %reduce-scatter.17.cloned.1.call-update) | async-done | bytes 1048592 | tf_op jit(solution)/shard_map/reduce_scatter | solution.py:46
  1079.2 33.9 %all-gather.31.cloned.1.call-done = bf16[512,2048]{1,0:T(8,128)(2,1)} async-done(((bf16[256,2048]{1,0:T(8,128)(2,1)}), bf16[512,2048]{1,0:T(8,128)(2,1)}) %all-gather.31.cloned.1.call-update) | async-done | bytes 2097168 | tf_op jit(solution)/shard_map/all_gather | solution.py:151
  1117.3 30.4 %all-gather.37.cloned.1.call-done = bf16[8,128,1024]{2,1,0:T(8,128)(2,1)} async-done(((bf16[4,128,1024]{2,1,0:T(8,128)(2,1)}), bf16[8,128,1024]{2,1,0:T(8,128)(2,1)}) %all-gather.37.cloned.1.call-update) | async-done | bytes 2097168 | tf_op jit(solution)/shard_map/all_gather | solution.py:139
  1188.8 78.7 %all-reduce.4.cloned.1.call-done = f32[16,1536]{1,0:T(8,128)} async-done(((f32[16,1536]{1,0:T(8,128)}), f32[16,1536]{1,0:T(8,128)}) %all-reduce.4.cloned.1.call-update) | async-done | bytes 98320
  1275.1 20.9 %reduce-scatter.19.cloned.1.call-done = bf16[64,2048]{1,0:T(8,128)(2,1)} async-done(((bf16[256,2048]{1,0:T(8,128)(2,1)}), bf16[64,2048]{1,0:T(8,128)(2,1)}) %reduce-scatter.19.cloned.1.call-update) | async-done | bytes 262160 | tf_op jit(solution)/shard_map/reduce_scatter | solution.py:242
  (277 shorter events, 352.8 us)
Async XLA Ops:
  7.2 286.6 %copy-start = (bf16[512,2048]{1,0:T(8,128)(2,1)S(1)}, bf16[512,2048]{1,0:T(8,128)(2,1)}, u32[]{:S(2)}) copy-start(bf16[512,2048]{1,0:T(8,128)(2,1)} %param.25) | copy-start | bytes 6291460
  7.2 50.6 %all-gather.21.cloned.1.call-start = ((), (), s32[]{:S(2)}) async-start(), calls=%async_computation.16 | async-start | bytes 1310720 | tf_op jit(solution)/shard_map/all_gather | solution.py:173
  9.1 97.1 %all-gather.19.cloned.1.call-start = ((), (), s32[]{:S(2)}) async-start(), calls=%async_computation.15 | async-start | bytes 3932160 | tf_op jit(solution)/shard_map/all_gather | solution.py:134
  31.3 130.4 %all-gather.17.cloned.1.call-start = ((), (), s32[]{:S(2)}) async-start(), calls=%async_computation.14 | async-start | bytes 9437184 | tf_op jit(solution)/shard_map/all_gather | solution.py:42
  57.7 227.1 %all-gather.23.cloned.1.call-start = ((), (), s32[]{:S(2)}) async-start(), calls=%async_computation.17 | async-start | bytes 9437184 | tf_op jit(solution)/shard_map/all_gather | solution.py:42
  69.2 24.2 %all-to-all-start.2 = ((bf16[4,128,1024]{1,2,0:T(8,128)(2,1)}), bf16[4,128,1024]{1,2,0:T(8,128)(2,1)}, u32[]{:S(2)}, u32[]{:S(2)}) async-start(bf16[4,128,1024]{1,2,0:T(8,128)(2,1)} %bitcast.209), calls=%async_computation.2 | async-start | bytes 2097152 | tf_op jit(solution)/shard_map/all_to_all | solution.py:133
  73.5 227.1 %all-gather.27.cloned.1.call-start = ((), (), s32[]{:S(2)}) async-start(), calls=%async_computation.19 | async-start | bytes 5242880 | tf_op jit(solution)/shard_map/all_gather | solution.py:134
  95.8 260.2 %all-gather.25.cloned.1.call-start = ((), (), s32[]{:S(2)}) async-start(), calls=%async_computation.18 | async-start | bytes 9437184 | tf_op jit(solution)/shard_map/all_gather | solution.py:42
  293.7 144.6 %all-gather.29.cloned.1.call-start = ((), (), s32[]{:S(2)}) async-start(), calls=%async_computation.20 | async-start | bytes 5242880 | tf_op jit(solution)/shard_map/all_gather | solution.py:175
  295.0 198.2 %all-gather.33.cloned.1.call-start = ((), (), s32[]{:S(2)}) async-start(), calls=%async_computation.30 | async-start | bytes 9437184 | tf_op jit(solution)/shard_map/all_gather | solution.py:42
  295.7 298.8 %reduce-scatter.11.cloned.1.call-start = ((), (), s32[]{:S(2)}) async-start(), calls=%async_computation.22 | async-start | bytes 9437184 | tf_op jit(solution)/shard_map/reduce_scatter | solution.py:46
  523.1 146.4 %reduce-scatter.9.cloned.1.call-start = ((), (), s32[]{:S(2)}) async-start(), calls=%async_computation.21 | async-start | bytes 9437184 | tf_op jit(solution)/shard_map/reduce_scatter | solution.py:46
  537.7 349.2 %reduce-scatter.23.cloned.1.call-start = ((), (), s32[]{:S(2)}) async-start(), calls=%async_computation.28 | async-start | bytes 5242880 | tf_op jit(solution)/shard_map/reduce_scatter | solution.py:238
  683.2 17.9 %all-to-all-start.3 = ((bf16[8,256,256]{1,2,0:T(8,128)(2,1)}), bf16[8,256,256]{1,2,0:T(8,128)(2,1)S(1)}, u32[]{:S(2)}, u32[]{:S(2)}) async-start(bf16[8,256,256]{1,2,0:T(8,128)(2,1)} %bitcast.29), calls=%async_computation.5 | async-start | bytes 2097152 | tf_op jit(solution)/shard_map/all_to_all | solution.py:50
  686.7 200.7 %reduce-scatter.21.cloned.1.call-start = ((), (), s32[]{:S(2)}) async-start(), calls=%async_computation.27 | async-start | bytes 5242880 | tf_op jit(solution)/shard_map/reduce_scatter | solution.py:137
  701.0 227.9 %reduce-scatter.15.cloned.1.call-start = ((), (), s32[]{:S(2)}) async-start(), calls=%async_computation.24 | async-start | bytes 3932160 | tf_op jit(solution)/shard_map/reduce_scatter | solution.py:137
  867.4 136.2 %reduce-scatter.13.cloned.1.call-start = ((), (), s32[]{:S(2)}) async-start(), calls=%async_computation.23 | async-start | bytes 9437184 | tf_op jit(solution)/shard_map/reduce_scatter | solution.py:46
  879.3 199.3 %reduce-scatter.17.cloned.1.call-start = ((), (), s32[]{:S(2)}) async-start(), calls=%async_computation.25 | async-start | bytes 9437184 | tf_op jit(solution)/shard_map/reduce_scatter | solution.py:46
  886.8 226.3 %all-gather.31.cloned.1.call-start = ((), (), s32[]{:S(2)}) async-start(), calls=%async_computation.29 | async-start | bytes 3145728 | tf_op jit(solution)/shard_map/all_gather | solution.py:151
  887.4 260.3 %all-gather.37.cloned.1.call-start = ((), (), s32[]{:S(2)}) async-start(), calls=%async_computation.32 | async-start | bytes 3145728 | tf_op jit(solution)/shard_map/all_gather | solution.py:139
  928.9 15.3 %all-to-all-start.4 = ((bf16[4,128,768]{2,1,0:T(8,128)(2,1)}), bf16[4,128,768]{2,1,0:T(8,128)(2,1)S(1)}, u32[]{:S(2)}, u32[]{:S(2)}) async-start(bf16[4,128,768]{2,1,0:T(8,128)(2,1)} %bitcast.224), calls=%async_computation.8 | async-start | bytes 1572864 | tf_op jit(solution)/shard_map/all_to_all | solution.py:138
  932.6 244.3 %all-gather.35.cloned.1.call-start = ((), (), s32[]{:S(2)}) async-start(), calls=%async_computation.31 | async-start | bytes 2359296 | tf_op jit(solution)/shard_map/all_gather | solution.py:139
  945.1 322.4 %all-reduce.4.cloned.1.call-start = ((), (), s32[]{:S(2)}) async-start(), calls=%async_computation.33 | async-start | bytes 196608
  1006.7 289.3 %reduce-scatter.19.cloned.1.call-start = ((), (), s32[]{:S(2)}) async-start(), calls=%async_computation.26 | async-start | bytes 1310720 | tf_op jit(solution)/shard_map/reduce_scatter | solution.py:242
  (44 other events, 1597.9 us)
Sparse Core Ops, SparseCore 0:
  10.2 30.7 all-gather.20
  43.1 63.0 all-gather.18
  108.6 53.0 all-gather.16
  163.5 54.3 all-gather.22
  219.9 80.7 all-gather.26
  303.0 52.9 all-gather.24
  357.5 80.7 all-gather.28
  440.2 52.9 all-gather.32
  523.2 71.2 reduce-scatter.10
  598.2 71.2 reduce-scatter.8
  671.8 76.7 reduce-scatter.22
  751.4 77.2 reduce-scatter.20
  867.5 61.3 reduce-scatter.14
  932.2 71.2 reduce-scatter.12
  1007.3 71.2 reduce-scatter.16
  1080.0 33.0 all-gather.30
  1114.5 33.1 all-gather.36
  1149.7 27.1 all-gather.34
  1180.3 87.1 all-reduce.3
  1269.8 26.1 reduce-scatter.18

commit v2 on v1

v2 whole, which is shorter than its diff:
```python
import functools

import jax
import jax.numpy as jnp
from jax import lax
from jax.experimental import pallas as pl
from jax.experimental.pallas import tpu as pltpu
from jax.sharding import PartitionSpec as P

H = 32
HD = 64
BF = jnp.bfloat16
F32 = jnp.float32
LONGEST = 512


def dot(a, b, ca, cb):
    return lax.dot_general(a, b, (((ca,), (cb,)), ((), ())), preferred_element_type=F32)


def head_probs(query, key, slope, place, prefix, lanes):
    raw = dot(jnp.where(lanes, query, jnp.zeros_like(query)), key, 1, 1)
    row = place + lax.broadcasted_iota(jnp.int32, raw.shape, 0)
    column = lax.broadcasted_iota(jnp.int32, raw.shape, 1)
    distance = jnp.abs(row - column).astype(F32)
    allowed = column <= jnp.maximum(row, prefix - 1)
    logits = jnp.where(allowed, raw - slope * distance, -1e30)
    largest = jnp.max(logits, axis=-1, keepdims=True)
    exponent = jnp.exp(logits - largest)
    return exponent * (1.0 / jnp.sum(exponent, axis=-1, keepdims=True))


def forward_kernel(W, order_ref, prefix_ref, slope_ref, qkv_ref, out_ref):
    C, T = qkv_ref.shape[1], qkv_ref.shape[2]
    seq, pair = pl.program_id(0), pl.program_id(1)
    at = lambda part: pl.ds(pl.multiple_of(part * W + pair * 128, 128), 128)
    first = lax.broadcasted_iota(jnp.int32, (T, 128), 1) < HD
    prefix = prefix_ref[seq]
    key = [qkv_ref[0, order_ref[c], :, at(1)] for c in range(C)]
    value = [qkv_ref[0, order_ref[c], :, at(2)] for c in range(C)]
    for c in range(C):
        n = min(C, max(c + 1, -(-LONGEST // T)))
        keys = jnp.concatenate(key[:n], axis=0)
        values = jnp.concatenate(value[:n], axis=0)
        query = qkv_ref[0, order_ref[c], :, at(0)] * 0.125
        out = []
        for h in range(2):
            probs = head_probs(query, keys, slope_ref[2 * pair + h], c * T, prefix, first if h == 0 else ~first)
            out.append(dot(probs.astype(BF), values, 1, 0))
        out_ref[0, order_ref[c], :, at(0)] = jnp.where(first, out[0], out[1]).astype(BF)


def backward_kernel(W, order_ref, prefix_ref, slope_ref, qkv_ref, d_out_ref, d_qkv_ref, d_key, d_value):
    C, T = qkv_ref.shape[1], qkv_ref.shape[2]
    seq, pair = pl.program_id(0), pl.program_id(1)
    at = lambda part: pl.ds(pl.multiple_of(part * W + pair * 128, 128), 128)
    first = lax.broadcasted_iota(jnp.int32, (T, 128), 1) < HD
    prefix = prefix_ref[seq]
    d_key[...] = jnp.zeros_like(d_key)
    d_value[...] = jnp.zeros_like(d_value)
    key = [qkv_ref[0, order_ref[c], :, at(1)] for c in range(C)]
    value = [qkv_ref[0, order_ref[c], :, at(2)] for c in range(C)]
    for c in range(C):
        n = min(C, max(c + 1, -(-LONGEST // T)))
        keys = jnp.concatenate(key[:n], axis=0)
        values = jnp.concatenate(value[:n], axis=0)
        query = qkv_ref[0, order_ref[c], :, at(0)]
        d_out = d_out_ref[0, order_ref[c], :, at(0)]
        d_query = []
        for h in range(2):
            lanes = first if h == 0 else ~first
            probs = head_probs(query * 0.125, keys, slope_ref[2 * pair + h], c * T, prefix, lanes)
            mine = jnp.where(lanes, d_out, jnp.zeros_like(d_out))
            d_probs = dot(mine, values, 1, 1)
            weighted = jnp.sum(probs * d_probs, axis=-1, keepdims=True)
            d_raw = (probs * (d_probs - weighted) * 0.125).astype(BF)
            d_query.append(dot(d_raw, keys, 1, 0))
            d_value[: n * T] += dot(probs.astype(BF), mine, 0, 0)
            d_key[: n * T] += dot(d_raw, jnp.where(lanes, query, jnp.zeros_like(query)), 0, 0)
        d_qkv_ref[0, order_ref[c], :, at(0)] = jnp.where(first, d_query[0], d_query[1]).astype(BF)
    for c in range(C):
        d_qkv_ref[0, order_ref[c], :, at(1)] = d_key[c * T : (c + 1) * T].astype(BF)
        d_qkv_ref[0, order_ref[c], :, at(2)] = d_value[c * T : (c + 1) * T].astype(BF)


def attention_call(kernel, widths, out_width, scratch, flops, order, prefix, slopes, *arrays):
    n, C, T = arrays[0].shape[:3]
    W = widths[-1]
    spec = lambda width: pl.BlockSpec((1, C, T, width), lambda s, p, *_: (s, 0, 0, 0))
    return pl.pallas_call(
        functools.partial(kernel, W),
        out_shape=jax.ShapeDtypeStruct((n, C, T, out_width), BF),
        grid_spec=pltpu.PrefetchScalarGridSpec(
            num_scalar_prefetch=3,
            grid=(n, W // 128),
            in_specs=[spec(a.shape[3]) for a in arrays],
            out_specs=spec(out_width),
            scratch_shapes=scratch,
        ),
        compiler_params=pltpu.CompilerParams(
            dimension_semantics=("arbitrary", "arbitrary"), vmem_limit_bytes=48 * 1024 * 1024
        ),
        cost_estimate=pl.CostEstimate(
            flops=flops * n * C * C * T * T * W, transcendentals=n * C * C * T * T * W // HD, bytes_accessed=sum(a.size * 2 for a in arrays)
        ),
    )(order, prefix, slopes, *arrays)


def attention_forward(order, prefix, slopes, qkv):
    W = qkv.shape[3] // 3
    return attention_call(forward_kernel, (W,), W, [], 4, order, prefix, slopes, qkv)


def attention_backward(order, prefix, slopes, qkv, d_out):
    W = qkv.shape[3] // 3
    L = qkv.shape[1] * qkv.shape[2]
    scratch = [pltpu.VMEM((L, 128), F32), pltpu.VMEM((L, 128), F32)]
    return attention_call(backward_kernel, (W,), 3 * W, scratch, 10, order, prefix, slopes, qkv, d_out)


def norm_stats(values):
    average = jnp.mean(values, axis=-1, keepdims=True)
    centred = values - average
    variance = jnp.mean(centred * centred, axis=-1, keepdims=True)
    inverse = lax.rsqrt(variance + 1e-05)
    return centred * inverse, inverse


def norm_back(normed, inverse, gain, grad):
    u = grad * gain
    mean_u = jnp.mean(u, axis=-1, keepdims=True)
    mean_un = jnp.mean(u * normed, axis=-1, keepdims=True)
    return (u - mean_u - normed * mean_un) * inverse


def gelu(values):
    return 0.5 * values * (1.0 + lax.erf(values * 0.7071067811865476))


def gelu_slope(values):
    density = jnp.exp(values * values * -0.5) * 0.3989422804014327
    return 0.5 * (1.0 + lax.erf(values * 0.7071067811865476)) + values * density


class Plain:
    def __init__(self, R, C):
        self.R, self.C, self.N = R, C, R * C
        self.axes = ("rep", "ctx")
        self.order = jnp.arange(C, dtype=jnp.int32)

    def gather(self, x):
        return lax.all_gather(x, self.axes, axis=0, tiled=False)

    def scatter(self, parts):
        out = lax.psum_scatter(parts.astype(BF), self.axes, scatter_dimension=0, tiled=True)
        return out.reshape(parts.shape[1:]).astype(F32)

    def swap(self, parts):
        return lax.all_to_all(parts, self.axes, 0, 0, tiled=True)

    def swap_ctx(self, blocks):
        return lax.all_to_all(blocks, "ctx", 0, 0, tiled=True)

    def prefixes(self, prefix):
        return lax.all_gather(prefix, "rep", axis=0, tiled=True)

    def both_reps(self, x):
        return lax.all_gather(x, "rep", axis=0, tiled=False)


class Near(Plain):
    def __init__(self, R, C):
        super().__init__(R, C)
        self.ctx = lax.axis_index("ctx")
        self.rep = lax.axis_index("rep")
        self.order = jnp.arange(C, dtype=jnp.int32) ^ self.ctx

    def over(self, x, d):
        return lax.ppermute(x, "ctx", [(i, i ^ d) for i in range(4)])

    def x(self, x):
        return lax.ppermute(x, "rep", [(0, 1), (1, 0)])

    def y(self, x):
        return self.over(x, 2)

    def core(self, x):
        return self.over(x, 1)

    def gather(self, x):
        half = x.shape[0] // 2
        from_x, from_y = self.x(x), self.y(x)
        far = jnp.concatenate([self.y(from_x[:half]), self.x(from_y[half:])], axis=0)
        quads = [x, from_y, from_x, far]
        return jnp.stack([piece for quad in quads for piece in (quad, self.core(quad))])

    def scatter(self, parts):
        sums = [parts[2 * i].astype(F32) + self.core(parts[2 * i + 1].astype(BF)).astype(F32) for i in range(4)]
        near, by_y, by_x, far = sums
        half = far.shape[0] // 2
        far = far.astype(BF)
        to_y = self.y(far[:half]).astype(F32)
        to_x = self.x(far[half:]).astype(F32)
        by_x = jnp.concatenate([by_x[:half] + to_y, by_x[half:]], axis=0)
        by_y = jnp.concatenate([by_y[:half], by_y[half:] + to_x], axis=0)
        return near + self.x(by_x.astype(BF)).astype(F32) + self.y(by_y.astype(BF)).astype(F32)

    def swap(self, parts):
        pairs = [[(i, i ^ d) for i in range(self.N)] for d in range(self.N)]
        moved = [lax.ppermute(parts[d], self.axes, pairs[d]) for d in range(1, self.N)]
        return jnp.stack([parts[0]] + moved)

    def swap_ctx(self, blocks):
        out = blocks
        for d in range(1, 4):
            moved = self.over(lax.dynamic_index_in_dim(blocks, self.ctx ^ d, 0, keepdims=False), d)
            out = lax.dynamic_update_index_in_dim(out, moved, self.ctx ^ d, 0)
        return out

    def prefixes(self, prefix):
        return jnp.concatenate([prefix, self.x(prefix)])

    def both_reps(self, x):
        other = self.x(x)
        first = self.rep == 0
        return jnp.stack([jnp.where(first, x, other), jnp.where(first, other, x)])


def gather_shifts(x, axis, size):
    me = lax.axis_index(axis)
    out = lax.dynamic_update_index_in_dim(jnp.zeros((size,) + x.shape, x.dtype), x, me, 0)
    for s in range(1, size):
        moved = lax.ppermute(x, axis, [(i, (i + s) % size) for i in range(size)])
        out = lax.dynamic_update_index_in_dim(out, moved, lax.rem(me - s + size, size), 0)
    return out


def scatter_shifts(x, axis, size):
    me = lax.axis_index(axis)
    total = lax.dynamic_index_in_dim(x, me, 0, keepdims=False)
    for s in range(1, size):
        mine = lax.dynamic_index_in_dim(x, lax.rem(me + s, size), 0, keepdims=False)
        total = total + lax.ppermute(mine, axis, [(i, (i + s) % size) for i in range(size)])
    return total


def shards(
    sizes,
    inputs,
    prefix,
    joined_weight,
    query_bias,
    value_bias,
    dense_weight,
    dense_bias,
    expand_weight,
    expand_bias,
    shrink_weight,
    shrink_bias,
    first_gain,
    first_shift,
    second_gain,
    second_shift,
    cotangent,
):
    R, F, C = sizes
    N = R * C
    rep = lax.axis_index("rep")
    ctx = lax.axis_index("ctx")
    S, T, D = inputs.shape
    t = S * T
    B = joined_weight.shape[0]
    FFB = shrink_weight.shape[0]
    FF = FFB * F * C
    E = FFB // R
    W = D // N
    aligned = (B // R) % HD == 0
    near = aligned and S == 1 and R == 2 and C == 4
    tp = Near(R, C) if near else Plain(R, C)

    def split_columns(weight, groups):
        n = weight.shape[1] // groups
        if aligned or groups == 1:
            pieces = weight.reshape(B, groups, F, C, R, n // (F * C * R))
            mine = lax.dynamic_index_in_dim(pieces, rep, 4, keepdims=False)
            mine = mine.transpose(3, 0, 1, 2, 4)
        else:
            pieces = weight.reshape(B, groups, R, C, n // (C * R))
            mine = lax.dynamic_index_in_dim(pieces, rep, 2, keepdims=False)
            mine = mine.transpose(2, 0, 1, 3)
        return mine.reshape(C, B, groups * n // N)

    def columns(weight, groups):
        blocks = tp.swap_ctx(split_columns(weight, groups))
        return lax.all_gather(blocks.reshape(C * B, -1), "fsdp", axis=0, tiled=True)

    def join_columns(grad, groups):
        part = lax.psum_scatter(grad.astype(BF), "fsdp", scatter_dimension=0, tiled=True)
        both = tp.both_reps(tp.swap_ctx(part.reshape(C, B, -1)))
        if aligned or groups == 1:
            both = both.reshape(R, C, B, groups, F, -1).transpose(2, 3, 4, 1, 0, 5)
        else:
            both = both.reshape(R, C, B, groups, -1).transpose(2, 3, 0, 1, 4)
        return both.reshape(B, -1).astype(F32)

    def half_rows(weight):
        n = weight.shape[0] // R
        return lax.dynamic_slice_in_dim(weight, rep * n, n, 0)

    def join_rows(part):
        both = tp.both_reps(part)
        return both.reshape(-1, both.shape[-1]).astype(F32)

    small = jnp.concatenate(
        [first_gain, first_shift, second_gain, second_shift, dense_bias, shrink_bias, query_bias, value_bias, expand_bias]
    )
    small = gather_shifts(gather_shifts(small, "ctx", C), "fsdp", F)
    small = small.reshape(F * C, -1).astype(F32)
    gain_one, shift_one, gain_two, shift_two, dbias, sbias, qbias, vbias = [
        small[:, i * B : (i + 1) * B].reshape(D) for i in range(8)
    ]
    ebias = small[:, 8 * B :].reshape(F, C, R, E)
    ebias = lax.dynamic_index_in_dim(lax.dynamic_index_in_dim(ebias, ctx, 1, False), rep, 1, False).reshape(F * E)

    def my_features(vector):
        if aligned:
            v = vector.reshape(F, C, R, -1)
            return lax.dynamic_index_in_dim(lax.dynamic_index_in_dim(v, ctx, 1, False), rep, 1, False).reshape(W)
        return lax.dynamic_slice_in_dim(vector, (rep * C + ctx) * W, W, 0)

    my_heads = my_features(jnp.repeat(jnp.arange(H, dtype=jnp.int32), HD)).reshape(-1, HD)[:, 0]
    slopes = jnp.exp2(-8.0 * (my_heads.astype(F32) + 1.0) / H)
    prefixes = tp.prefixes(prefix)

    joined_cols = columns(joined_weight, 3)
    if aligned:
        dense_all = tp.gather(lax.all_gather(half_rows(dense_weight), "fsdp", axis=0, tiled=True)).reshape(D, D)
    else:
        dense_all = lax.all_gather(dense_weight, ("fsdp", "ctx"), axis=0, tiled=True)
    expand_cols = columns(expand_weight, 1)
    shrink_rows = lax.all_gather(half_rows(shrink_weight), "fsdp", axis=0, tiled=True)

    def to_sequences(a):
        return a.reshape(R, C, S, T, -1).transpose(0, 2, 1, 3, 4).reshape(R * S, C, T, -1)

    def from_sequences(a):
        return a.reshape(R, S, C, T, -1).transpose(0, 2, 1, 3, 4).reshape(N, t, -1)

    start = inputs.astype(F32).reshape(t, D)
    n1, inv1 = norm_stats(start)
    a1 = (n1 * gain_one + shift_one).astype(BF)
    a1_all = tp.gather(a1).reshape(N * t, D)
    g = cotangent.reshape(t, D)
    g_all = tp.gather(g).reshape(N * t, D)
    qkv_bias = jnp.concatenate([my_features(qbias), jnp.zeros((W,), F32), my_features(vbias)])
    qkv = (dot(a1_all, joined_cols, 1, 0) + qkv_bias).astype(BF)
    qkv = to_sequences(qkv)
    out = attention_forward(tp.order, prefixes, slopes, qkv)
    o = tp.swap(from_sequences(out))
    o = o.transpose(1, 0, 2).reshape(t, D)
    midway = start + dot(o, dense_all, 1, 0) + dbias

    n2, inv2 = norm_stats(midway)
    a2 = (n2 * gain_two + shift_two).astype(BF)
    a2_all = tp.gather(a2).reshape(N * t, D)
    expanded = dot(a2_all, expand_cols, 1, 0) + ebias
    act = gelu(expanded).astype(BF)
    branch = tp.scatter(dot(act, shrink_rows, 1, 0).reshape(N, t, D))
    layer_output = midway + branch + sbias

    g_float = g.astype(F32)
    d_act = dot(g_all, shrink_rows, 1, 1)
    d_exp = (d_act * gelu_slope(expanded)).astype(BF)
    d_a2 = tp.scatter(dot(d_exp, expand_cols, 1, 1).reshape(N, t, D))
    shrink_grad = dot(act, g_all, 0, 0).astype(BF)
    expand_grad = dot(a2_all, d_exp, 0, 0)
    ebias_grad = jnp.sum(d_exp.astype(F32), axis=0)
    sbias_grad = jnp.sum(g_float, axis=0)
    d_mid = g_float + norm_back(n2, inv2, gain_two, d_a2)
    gain_two_grad = jnp.sum(d_a2 * n2, axis=0)
    shift_two_grad = jnp.sum(d_a2, axis=0)
    d_att = d_mid.astype(BF)

    dense_grad = dot(o, d_att, 0, 0)
    dbias_grad = jnp.sum(d_att.astype(F32), axis=0)
    d_o = dot(d_att, dense_all, 1, 1).astype(BF)
    d_o = tp.swap(d_o.reshape(t, N, W).transpose(1, 0, 2))
    d_qkv = attention_backward(tp.order, prefixes, slopes, qkv, to_sequences(d_o))
    d_qkv = from_sequences(d_qkv).reshape(N * t, 3 * W)
    d_a1 = tp.scatter(dot(d_qkv, joined_cols, 1, 1).reshape(N, t, D))
    joined_grad = dot(a1_all, d_qkv, 0, 0)
    qkv_bias_grad = jnp.sum(d_qkv.astype(F32), axis=0)
    input_gradient = d_mid + norm_back(n1, inv1, gain_one, d_a1)
    gain_one_grad = jnp.sum(d_a1 * n1, axis=0)
    shift_one_grad = jnp.sum(d_a1, axis=0)

    shrink_out = join_rows(lax.psum_scatter(shrink_grad, "fsdp", scatter_dimension=0, tiled=True))
    expand_out = join_columns(expand_grad, 1)
    if aligned:
        part = tp.scatter(dense_grad.reshape(N, W, D)).astype(BF)
        dense_out = join_rows(lax.psum_scatter(part, "fsdp", scatter_dimension=0, tiled=True))
    else:
        part = lax.psum_scatter(dense_grad.astype(BF), ("fsdp", "ctx"), scatter_dimension=0, tiled=True)
        dense_out = lax.psum(part, "rep").astype(F32)
    joined_out = join_columns(joined_grad, 3)

    tokens = jnp.stack([gain_one_grad, shift_one_grad, gain_two_grad, shift_two_grad, dbias_grad, sbias_grad])
    if near:
        tokens = tokens + tp.x(tokens)
        tokens = tokens + tp.y(tokens)
        tokens = tokens + tp.core(tokens)
    else:
        tokens = lax.psum(tokens, ("rep", "ctx"))
    tokens = lax.dynamic_index_in_dim(tokens.reshape(6, F, C, B), ctx, 2, keepdims=False)
    tokens = tokens.transpose(1, 0, 2).reshape(F, 6 * B)
    if aligned:
        own = [a.reshape(F, -1) for a in (qkv_bias_grad[:W], qkv_bias_grad[2 * W :], ebias_grad)]
    else:
        spread = jnp.zeros((2, N, W), F32)
        mine = jnp.stack([qkv_bias_grad[:W], qkv_bias_grad[2 * W :]])[:, None]
        spread = lax.psum(lax.dynamic_update_slice(spread, mine, (0, rep * C + ctx, 0)), ("rep", "ctx"))
        spread = lax.dynamic_index_in_dim(spread.reshape(2, F, C, R, -1), ctx, 2, keepdims=False)
        spread = lax.dynamic_index_in_dim(spread, rep, 2, keepdims=False)
        own = [spread[0], spread[1], ebias_grad.reshape(F, -1)]
    little = scatter_shifts(jnp.concatenate([tokens] + own, axis=1), "fsdp", F)
    gain_one_out, shift_one_out, gain_two_out, shift_two_out, dbias_out, sbias_out = [
        little[i * B : (i + 1) * B] for i in range(6)
    ]
    own = tp.both_reps(little[6 * B :])
    n = B // R
    qbias_out = own[:, :n].reshape(B)
    vbias_out = own[:, n : 2 * n].reshape(B)
    ebias_out = own[:, 2 * n :].reshape(FFB)

    return (
        layer_output.reshape(S, T, D),
        input_gradient.reshape(S, T, D),
        joined_out,
        qbias_out,
        vbias_out,
        dense_out,
        dbias_out,
        expand_out,
        ebias_out,
        shrink_out,
        sbias_out,
        gain_one_out,
        shift_one_out,
        gain_two_out,
        shift_two_out,
    )


def solution(mesh):
    sizes = (mesh.shape["rep"], mesh.shape["fsdp"], mesh.shape["ctx"])
    tokens = P(("rep", "fsdp"), "ctx", None)
    matrix = P(("fsdp", "ctx"), None)
    vector = P(("fsdp", "ctx"))
    weights = (matrix, vector, vector, matrix, vector, matrix, vector, matrix, vector, vector, vector, vector, vector)
    in_specs = (tokens, P(("rep", "fsdp")), *weights, tokens)
    out_specs = (tokens, tokens, *weights)

    def step(*arrays):
        return shards(sizes, *arrays)

    return jax.shard_map(step, mesh=mesh, in_specs=in_specs, out_specs=out_specs, check_vma=False)
```

time: 1320 us -> 830 us (0.63)
  waiting for transfers between devices: 699 us -> 334 us
  matrix products: 322 us -> 139 us
  blocking collectives: 91.5 us -> 0 us
  starting transfers between devices: 12.6 us -> 82.1 us
  Pallas kernels: 0 us -> 52.1 us
  local copies, waits for them, and re-layouts: 112 us -> 136 us
    ppermute x0 -> x108, waiting for transfers between devices: none -> 300 us  [the longest x62 159 us: over(): return lax.ppermute(x, 'ctx', [(i, i ^ d) for i in range(4)])]
    reduce_scatter x4 -> x0, waiting for transfers between devices: 245 us -> none  [scatter_tp(): return lax.psum_scatter(x, TP, scatter_dimension=0, tiled=True)]
    all_gather x7 -> x0, waiting for transfers between devices: 240 us -> none  [the longest x4 166 us: gather_tp(): return lax.all_gather(x, TP, axis=0, tiled=True)]
    dot_general x6 -> x0, matrix products: 184 us -> none  [the longest x1 55.8 us: attention_backward(): jnp.einsum('shqk,sqhe->skhe', d_raw, q, preferred_element_type=F32)]
    ppermute x0 -> x108, starting transfers between devices: none -> 81.3 us  [the longest x62 33.5 us: over(): return lax.ppermute(x, 'ctx', [(i, i ^ d) for i in range(4)])]
    unnamed x21 -> x8, waiting for transfers between devices: 80.7 us -> 0.13 us
    all_gather x1, waiting for transfers between devices: 66.5 us -> 0.01 us  [shards(): lax.all_gather(half_rows(shrink_weight), 'fsdp', axis=0, tiled=True)]
    all_to_all x3 -> x0, blocking collectives: 52.3 us -> none  [the longest x1 18.8 us: join_columns(): blocks = lax.all_to_all(part.reshape(C, B, -1), 'ctx', 0, 0, tiled=True)]
  transfers between devices with their start and end apart: 23 -> 116, of which waited for: 18 -> 60; matrix products, arithmetic and copies ran while one was open for 35% -> 33% of each run, Pallas kernels for 0% -> 6%
where the time goes in v2:
time: 830 us; the launch traced here: 823 us
  waiting for transfers between devices  334 us (40%)
  matrix products  139 us (17%)
  local copies, waits for them, and re-layouts  136 us (16%)
  starting transfers between devices  82.1 us (10%)
  other arithmetic  62.7 us (8%)
  Pallas kernels  52.1 us (6%)
  between operations  16.9 us (2%)
    ppermute x62, waiting for transfers between devices, over(): return lax.ppermute(x, 'ctx', [(i, i ^ d) for i in range(4)])  159 us
    dot_general x12, matrix products, dot(): lax.dot_general(a, b, (((ca,), (cb,)), ((), ())), preferred_element_type=...  139 us
    ppermute x23, waiting for transfers between devices, x(): return lax.ppermute(x, 'rep', [(0, 1), (1, 0)])  114 us
    unnamed x148, local copies, waits for them, and re-layouts  61.9 us
    pallas_call x2, Pallas kernels, attention_call(): pl.pallas_call(functools.partial(kernel, W), out_shape=jax.ShapeDtypeStru...  52.1 us
    ppermute x62, starting transfers between devices, over(): return lax.ppermute(x, 'ctx', [(i, i ^ d) for i in range(4)])  33.5 us
    reduce_scatter x2, waiting for transfers between devices, join_columns(): lax.psum_scatter(grad.astype(BF), 'fsdp', scatter_dimension=0, tiled=True)  33.5 us
    ppermute x14, waiting for transfers between devices, swap(): lax.ppermute(parts[d], self.axes, pairs[d])  22.7 us
  transfers between devices with their start and end apart: 116, of which 60 were waited for; matrix products, arithmetic and copies ran while one was open for 33% of the time, Pallas kernels for 6%

profile of v2, /device:TPU:0, one launch (start us, length us, event | category | flops | bytes accessed | tf_op | source)
XLA Modules:
  0.0 822.7 jit_solution(8367766464246241878)
XLA Ops:
  82.8 9.1 %collective-permute-done.55 = bf16[256,2048]{1,0:T(8,128)(2,1)} collective-permute-done((bf16[256,2048]{1,0:T(8,128)(2,1)S(1)}, bf16[256,2048]{1,0:T(8,128)(2,1)}, u32[]{:S(2)}, u32[]{:S(2)}) %collective-permute-start.55) | collective-permute-done | bytes 1048608 | tf_op jit(solution)/shard_map/ppermute | solution.py:182
  103.7 14.5 %collective-permute-done.10 = bf16[256,2048]{1,0:T(8,128)(2,1)S(1)} collective-permute-done((bf16[256,2048]{1,0:T(8,128)(2,1)}, bf16[256,2048]{1,0:T(8,128)(2,1)S(1)}, u32[]{:S(2)}, u32[]{:S(2)}) %collective-permute-start.10) | collective-permute-done | bytes 1048608 | tf_op jit(solution)/shard_map/ppermute | solution.py:182
  152.6 19.2 %collective-permute-done.28 = bf16[256,2048]{1,0:T(8,128)(2,1)S(1)} collective-permute-done((bf16[256,2048]{1,0:T(8,128)(2,1)S(1)}, bf16[256,2048]{1,0:T(8,128)(2,1)S(1)}, u32[]{:S(2)}, u32[]{:S(2)}) %collective-permute-start.28) | collective-permute-done | bytes 1048608 | tf_op jit(solution)/shard_map/ppermute | solution.py:182
  176.4 9.8 %collective-permute-done.30 = bf16[128,2048]{1,0:T(8,128)(2,1)S(1)} collective-permute-done((bf16[128,2048]{1,0:T(8,128)(2,1)S(1)}, bf16[128,2048]{1,0:T(8,128)(2,1)S(1)}, u32[]{:S(2)}, u32[]{:S(2)}) %collective-permute-start.30) | collective-permute-done | bytes 524320 | tf_op jit(solution)/shard_map/ppermute | solution.py:179
  193.4 10.9 %add_convert_fusion = bf16[2048,768]{1,0:T(8,128)(2,1)S(1)} fusion(f32[768]{0:T(1024)S(1)} %pad_maximum_fusion.10, bf16[2048,2048]{1,0:T(8,128)(2,1)} %bitcast.364, bf16[2048,768]{1,0:T(8,128)(2,1)} %all-gather.5.cloned.1.call-done), kind=kOutput, calls=%fused_computation.5 | convolution fusion | flops 6445596672 | bytes 14683136 | tf_op jit(solution)/shard_map/dot_general | solution.py:18
  204.4 19.8 %shard_map.271 = bf16[2,4,256,256]{3,2,1,0:T(8,128)(2,1)S(1)} custom-call(s32[4]{0:T(128)S(1)} %iota_xor_fusion.order_ref, s32[2]{0:T(128)S(1)} %pad_add_fusion.prefix_ref, f32[4]{0:T(128)S(1)} %fusion.61.slope_ref, bf16[2,4,256,768]{3,2,1,0:T(8,128)(2,1)S(1)} %bitcast.336), custom_call_target="tpu_custom_call" | custom-call | flops 2147483648 | bytes 3145728 | tf_op jit(solution)/shard_map/pallas_call | solution.py:90
  261.5 18.1 %collective-permute-done.36 = bf16[256,2048]{1,0:T(8,128)(2,1)S(1)} collective-permute-done((bf16[256,2048]{1,0:T(8,128)(2,1)S(1)}, bf16[256,2048]{1,0:T(8,128)(2,1)S(1)}, u32[]{:S(2)}, u32[]{:S(2)}) %collective-permute-start.36) | collective-permute-done | bytes 1048608 | tf_op jit(solution)/shard_map/ppermute | solution.py:182
  284.3 8.6 %collective-permute-done.38 = bf16[128,2048]{1,0:T(8,128)(2,1)S(1)} collective-permute-done((bf16[128,2048]{1,0:T(8,128)(2,1)S(1)}, bf16[128,2048]{1,0:T(8,128)(2,1)S(1)}, u32[]{:S(2)}, u32[]{:S(2)}) %collective-permute-start.38) | collective-permute-done | bytes 524320 | tf_op jit(solution)/shard_map/ppermute | solution.py:179
  298.7 16.2 %multiply_convert_fusion.1 = (bf16[2048,1024]{1,0:T(8,128)(2,1)}, f32[2048,1024]{1,0:T(8,128)}) fusion(f32[1024]{0:T(1024)S(1)} %bitcast.375, bf16[2048,2048]{1,0:T(8,128)(2,1)} %bitcast.65, bf16[2048,1024]{1,0:T(8,128)(2,1)} %all-gather.9.cloned.1.call-done), kind=kOutput, calls=%fused_computation.2 | convolution fusion | flops 8602517504 | bytes 25169920 | tf_op jit(solution)/shard_map/dot_general | solution.py:18
  314.9 18.2 %convert_reduce_fusion = (f32[1024]{0:T(1024)}, bf16[2048,1024]{1,0:T(8,128)(2,1)}) fusion(f32[2048,1024]{1,0:T(8,128)} %get-tuple-element.162, f32[1024]{0:T(1024)S(1)} %bitcast.376, bf16[2048,2048]{1,0:T(8,128)(2,1)} %bitcast.366, bf16[1024,2048]{1,0:T(8,128)(2,1)} %all-gather.11.cloned.1.call-done), kind=kOutput, calls=%fused_computation | convolution fusion | flops 8617196544 | bytes 25174016 | tf_op jit(solution)/shard_map/dot_general | solution.py:18
  333.1 14.1 %fusion.79 = (bf16[2048,2048]{1,0:T(8,128)(2,1)S(1)}, f32[2048,2048]{1,0:T(8,128)}) fusion(bf16[2048,1024]{1,0:T(8,128)(2,1)} %get-tuple-element.168, bf16[2048,1024]{1,0:T(8,128)(2,1)S(1)} %copy-done.45), kind=kOutput, calls=%fused_computation.295 | convolution fusion | flops 8594128896 | bytes 33554432 | tf_op jit(solution)/shard_map/dot_general | solution.py:18
  349.6 15.3 %fusion.80 = (bf16[2048,2048]{1,0:T(8,128)(2,1)S(1)}, f32[2048,2048]{1,0:T(8,128)}) fusion(bf16[2048,1024]{1,0:T(8,128)(2,1)} %get-tuple-element.161, bf16[1024,2048]{1,0:T(8,128)(2,1)} %all-gather.11.cloned.1.call-done), kind=kOutput, calls=%fused_computation.296 | convolution fusion | flops 8594128896 | bytes 33554432 | tf_op jit(solution)/shard_map/dot_general | solution.py:18
  406.8 17.3 %collective-permute-done.67 = bf16[256,2048]{1,0:T(8,128)(2,1)} collective-permute-done((bf16[256,2048]{1,0:T(8,128)(2,1)}, bf16[256,2048]{1,0:T(8,128)(2,1)}, u32[]{:S(2)}, u32[]{:S(2)}) %collective-permute-start.67) | collective-permute-done | bytes 1048608 | tf_op jit(solution)/shard_map/ppermute | solution.py:179
  428.0 16.7 %collective-permute-done.51 = bf16[256,2048]{1,0:T(8,128)(2,1)} collective-permute-done((bf16[256,2048]{1,0:T(8,128)(2,1)}, bf16[256,2048]{1,0:T(8,128)(2,1)}, u32[]{:S(2)}, u32[]{:S(2)}) %collective-permute-start.51) | collective-permute-done | bytes 1048608 | tf_op jit(solution)/shard_map/ppermute | solution.py:179
  464.3 11.9 %collective-permute-done.100 = bf16[128,2048]{1,0:T(8,128)(2,1)S(1)} collective-permute-done((bf16[128,2048]{1,0:T(8,128)(2,1)S(1)}, bf16[128,2048]{1,0:T(8,128)(2,1)S(1)}, u32[]{:S(2)}, u32[]{:S(2)}) %collective-permute-start.100) | collective-permute-done | bytes 524320 | tf_op jit(solution)/shard_map/ppermute | solution.py:182
  479.0 21.8 %collective-permute-done.101 = bf16[256,2048]{1,0:T(8,128)(2,1)S(1)} collective-permute-done((bf16[256,2048]{1,0:T(8,128)(2,1)S(1)}, bf16[256,2048]{1,0:T(8,128)(2,1)S(1)}, u32[]{:S(2)}, u32[]{:S(2)}) %collective-permute-start.101) | collective-permute-done | bytes 1048608 | tf_op jit(solution)/shard_map/ppermute | solution.py:179
  504.3 14.0 %convolution_convert_fusion.1 = bf16[2048,1024]{1,0:T(8,128)(2,1)} fusion(bf16[2048,2048]{1,0:T(8,128)(2,1)} %bitcast.65, bf16[2048,1024]{1,0:T(8,128)(2,1)} %get-tuple-element.168), kind=kOutput, calls=%fused_computation.8 | convolution fusion | flops 8592031744 | bytes 16777216 | tf_op jit(solution)/shard_map/dot_general | solution.py:18
  527.9 13.0 %convolution_convert_fusion = bf16[1024,2048]{1,0:T(8,128)(2,1)} fusion(bf16[2048,1024]{1,0:T(8,128)(2,1)S(1)} %copy-done.46, bf16[2048,2048]{1,0:T(8,128)(2,1)} %bitcast.367), kind=kOutput, calls=%fused_computation.7 | convolution fusion | flops 8592031744 | bytes 16777216 | tf_op jit(solution)/shard_map/dot_general | solution.py:18
  559.6 32.3 %shard_map.272 = bf16[2,4,256,768]{3,2,1,0:T(8,128)(2,1)S(1)} custom-call(s32[4]{0:T(128)S(1)} %copy-done.8, s32[2]{0:T(128)S(1)} %copy-done.6, f32[4]{0:T(128)S(1)} %copy-done.10, bf16[2,4,256,768]{3,2,1,0:T(8,128)(2,1)} %bitcast.337, bf16[2,4,256,256]{3,2,1,0:T(8,128)(2,1)S(1)} %bitcast.335), custom_call_target="tpu_custom_call" | custom-call | flops 5368709120 | bytes 4194304 | tf_op jit(solution)/shard_map/pallas_call | solution.py:90
  591.9 10.6 %fusion.81 = (bf16[2048,2048]{1,0:T(8,128)(2,1)}, f32[2048,2048]{1,0:T(8,128)S(1)}) fusion(bf16[2048,768]{1,0:T(8,128)(2,1)S(1)} %bitcast.332, bf16[2048,768]{1,0:T(8,128)(2,1)} %all-gather.5.cloned.1.call-done), kind=kOutput, calls=%fused_computation.297 | convolution fusion | flops 6446645248 | bytes 31457280 | tf_op jit(solution)/shard_map/dot_general | solution.py:18
  620.6 10.6 %convolution_convert_fusion.2 = bf16[2048,768]{1,0:T(8,128)(2,1)} fusion(bf16[2048,2048]{1,0:T(8,128)(2,1)} %bitcast.365, bf16[2048,768]{1,0:T(8,128)(2,1)S(1)} %bitcast.333), kind=kOutput, calls=%fused_computation.9 | convolution fusion | flops 6444023808 | bytes 14680064 | tf_op jit(solution)/shard_map/dot_general | solution.py:18
  638.6 10.3 %collective-permute-done.78 = bf16[128,2048]{1,0:T(8,128)(2,1)S(1)} collective-permute-done((bf16[128,2048]{1,0:T(8,128)(2,1)}, bf16[128,2048]{1,0:T(8,128)(2,1)S(1)}, u32[]{:S(2)}, u32[]{:S(2)}) %collective-permute-start.78) | collective-permute-done | bytes 524320 | tf_op jit(solution)/shard_map/ppermute | solution.py:179
  651.8 19.3 %collective-permute-done.82 = bf16[256,2048]{1,0:T(8,128)(2,1)} collective-permute-done((bf16[256,2048]{1,0:T(8,128)(2,1)}, bf16[256,2048]{1,0:T(8,128)(2,1)}, u32[]{:S(2)}, u32[]{:S(2)}) %collective-permute-start.82) | collective-permute-done | bytes 1048608 | tf_op jit(solution)/shard_map/ppermute | solution.py:179
  720.8 33.5 %reduce-scatter.5.cloned.1.call-done = bf16[512,768]{1,0:T(8,128)(2,1)} async-done(((bf16[2048,768]{1,0:T(8,128)(2,1)}), bf16[512,768]{1,0:T(8,128)(2,1)}) %reduce-scatter.5.cloned.1.call-update) | async-done | bytes 786448 | tf_op jit(solution)/shard_map/reduce_scatter | solution.py:298
  (555 shorter events, 420.8 us)
Async XLA Ops:
  7.2 122.0 %all-gather.7.cloned.1.call-start = ((), (), s32[]{:S(2)}) async-start(), calls=%async_computation.5 | async-start | bytes 1310720 | tf_op jit(solution)/shard_map/all_gather | solution.py:337
  9.1 184.3 %all-gather.5.cloned.1.call-start = ((), (), s32[]{:S(2)}) async-start(), calls=%async_computation.4 | async-start | bytes 3932160 | tf_op jit(solution)/shard_map/all_gather | solution.py:295
  27.8 270.9 %all-gather.9.cloned.1.call-start = ((), (), s32[]{:S(2)}) async-start(), calls=%async_computation.6 | async-start | bytes 5242880 | tf_op jit(solution)/shard_map/all_gather | solution.py:295
  53.5 261.4 %all-gather.11.cloned.1.call-start = ((), (), s32[]{:S(2)}) async-start(), calls=%async_computation.7 | async-start | bytes 5242880 | tf_op jit(solution)/shard_map/all_gather | solution.py:341
  60.1 36.1 %collective-permute-start.52 = (bf16[256,2048]{1,0:T(8,128)(2,1)}, bf16[256,2048]{1,0:T(8,128)(2,1)}, u32[]{:S(2)}, u32[]{:S(2)}) collective-permute-start(bf16[256,2048]{1,0:T(8,128)(2,1)} %bitcast.348), channel_id=1, source_target_pairs={{0,1},{1,0},{2,3},{3,2},{4,5},{5,4},{6,7},{7,6},{8,9},{9,8},{10,11... | collective-permute-start | bytes 3145736 | tf_op jit(solution)/shard_map/ppermute | solution.py:179
  61.2 642.5 %reduce-scatter.7.cloned.1.call-start = ((), (), s32[]{:S(2)}) async-start(), calls=%async_computation.9 | async-start | bytes 1310720 | tf_op jit(solution)/shard_map/reduce_scatter | solution.py:401
  80.2 39.8 %collective-permute-start.8 = (bf16[256,2048]{1,0:T(8,128)(2,1)}, bf16[256,2048]{1,0:T(8,128)(2,1)}, u32[]{:S(2)}, u32[]{:S(2)}) collective-permute-start(bf16[256,2048]{1,0:T(8,128)(2,1)} %fusion.10), channel_id=1, source_target_pairs={{0,2},{1,3},{2,0},{3,1},{4,6},{5,7},{6,4},{7,5},{8,10},{9,11},{10,... | collective-permute-start | bytes 3145736 | tf_op jit(solution)/shard_map/ppermute | solution.py:179
  102.4 37.8 %collective-permute-start.54 = (bf16[256,2048]{1,0:T(8,128)(2,1)}, bf16[256,2048]{1,0:T(8,128)(2,1)}, u32[]{:S(2)}, u32[]{:S(2)}) collective-permute-start(bf16[256,2048]{1,0:T(8,128)(2,1)} %collective-permute-done.53), channel_id=1, source_target_pairs={{0,1},{1,0},{2,3},{3,2},{4,5},{5,4},{6,7},{7,6},{8,9},{9,8},{10,11... | collective-permute-start | bytes 3145736 | tf_op jit(solution)/shard_map/ppermute | solution.py:179
  118.2 136.4 %collective-permute-start.56 = (bf16[256,2048]{1,0:T(8,128)(2,1)}, bf16[256,2048]{1,0:T(8,128)(2,1)}, u32[]{:S(2)}, u32[]{:S(2)}) collective-permute-start(bf16[256,2048]{1,0:T(8,128)(2,1)} %collective-permute-done.55), channel_id=1, source_target_pairs={{0,1},{1,0},{2,3},{3,2},{4,5},{5,4},{6,7},{7,6},{8,9},{9,8},{10,11... | collective-permute-start | bytes 3145736 | tf_op jit(solution)/shard_map/ppermute | solution.py:179
  139.1 32.7 %collective-permute-start.25 = (bf16[256,2048]{1,0:T(8,128)(2,1)S(1)}, bf16[256,2048]{1,0:T(8,128)(2,1)S(1)}, u32[]{:S(2)}, u32[]{:S(2)}) collective-permute-start(bf16[256,2048]{1,0:T(8,128)(2,1)S(1)} %copy-done.26), channel_id=1, source_target_pairs={{0,1},{1,0},{2,3},{3,2},{4,5},{5,4},{6,7},{7,6},{8,9},{9,8},{10,11... | collective-permute-start | bytes 3145736 | tf_op jit(solution)/shard_map/ppermute | solution.py:179
  171.8 87.4 %collective-permute-start.59 = (bf16[256,2048]{1,0:T(8,128)(2,1)}, bf16[256,2048]{1,0:T(8,128)(2,1)}, u32[]{:S(2)}, u32[]{:S(2)}) collective-permute-start(bf16[256,2048]{1,0:T(8,128)(2,1)} %constant_dynamic-update-slice_fusion.6), channel_id=1, source_target_pairs={{0,1},{1,0},{2,3},{3,2},{4,5},{5,4},{6,7},{7,6},{8,9},{9,8},{10,11... | collective-permute-start | bytes 3145736 | tf_op jit(solution)/shard_map/ppermute | solution.py:179
  189.1 35.8 %collective-permute-start.32 = (bf16[256,2048]{1,0:T(8,128)(2,1)S(1)}, bf16[256,2048]{1,0:T(8,128)(2,1)}, u32[]{:S(2)}, u32[]{:S(2)}) collective-permute-start(bf16[256,2048]{1,0:T(8,128)(2,1)S(1)} %constant_dynamic-update-slice_fusion.2), channel_id=1, source_target_pairs={{0,1},{1,0},{2,3},{3,2},{4,5},{5,4},{6,7},{7,6},{8,9},{9,8},{10,11... | collective-permute-start | bytes 3145736 | tf_op jit(solution)/shard_map/ppermute | solution.py:179
  349.6 54.7 %collective-permute-start.60 = (bf16[256,2048]{1,0:T(8,128)(2,1)S(1)}, bf16[256,2048]{1,0:T(8,128)(2,1)S(1)}, u32[]{:S(2)}, u32[]{:S(2)}) collective-permute-start(bf16[256,2048]{1,0:T(8,128)(2,1)S(1)} %get-tuple-element.83), channel_id=1, source_target_pairs={{0,1},{1,0},{2,3},{3,2},{4,5},{5,4},{6,7},{7,6},{8,9},{9,8},{10,11... | collective-permute-start | bytes 3145736 | tf_op jit(solution)/shard_map/ppermute | solution.py:179
  367.3 60.7 %collective-permute-start.44 = (bf16[256,2048]{1,0:T(8,128)(2,1)}, bf16[256,2048]{1,0:T(8,128)(2,1)}, u32[]{:S(2)}, u32[]{:S(2)}) collective-permute-start(bf16[256,2048]{1,0:T(8,128)(2,1)} %get-tuple-element.87), channel_id=1, source_target_pairs={{0,1},{1,0},{2,3},{3,2},{4,5},{5,4},{6,7},{7,6},{8,9},{9,8},{10,11... | collective-permute-start | bytes 3145736 | tf_op jit(solution)/shard_map/ppermute | solution.py:179
  389.5 34.7 %collective-permute-start.67 = (bf16[256,2048]{1,0:T(8,128)(2,1)}, bf16[256,2048]{1,0:T(8,128)(2,1)}, u32[]{:S(2)}, u32[]{:S(2)}) collective-permute-start(bf16[256,2048]{1,0:T(8,128)(2,1)} %pad_maximum_fusion.4), channel_id=1, source_target_pairs={{0,2},{1,3},{2,0},{3,1},{4,6},{5,7},{6,4},{7,5},{8,10},{9,11},{10,... | collective-permute-start | bytes 3145736 | tf_op jit(solution)/shard_map/ppermute | solution.py:179
  401.5 43.2 %collective-permute-start.51 = (bf16[256,2048]{1,0:T(8,128)(2,1)}, bf16[256,2048]{1,0:T(8,128)(2,1)}, u32[]{:S(2)}, u32[]{:S(2)}) collective-permute-start(bf16[256,2048]{1,0:T(8,128)(2,1)} %pad_maximum_fusion.2), channel_id=1, source_target_pairs={{0,2},{1,3},{2,0},{3,1},{4,6},{5,7},{6,4},{7,5},{8,10},{9,11},{10,... | collective-permute-start | bytes 3145736 | tf_op jit(solution)/shard_map/ppermute | solution.py:179
  404.3 40.6 %collective-permute-start.48 = (bf16[256,2048]{1,0:T(8,128)(2,1)}, bf16[256,2048]{1,0:T(8,128)(2,1)}, u32[]{:S(2)}, u32[]{:S(2)}) collective-permute-start(bf16[256,2048]{1,0:T(8,128)(2,1)} %pad_maximum_fusion.1), channel_id=1, source_target_pairs={{0,16},{16,0},{1,17},{17,1},{2,18},{18,2},{3,19},{19,3},{4,20},{20... | collective-permute-start | bytes 3145736 | tf_op jit(solution)/shard_map/ppermute | solution.py:182
  504.3 202.0 %reduce-scatter.9.cloned.1.call-start = ((), (), s32[]{:S(2)}) async-start(), calls=%async_computation.10 | async-start | bytes 5242880 | tf_op jit(solution)/shard_map/reduce_scatter | solution.py:298
  518.3 196.9 %reduce-scatter.11.cloned.1.call-start = ((), (), s32[]{:S(2)}) async-start(), calls=%async_computation.11 | async-start | bytes 5242880 | tf_op jit(solution)/shard_map/reduce_scatter | solution.py:397
  541.0 213.3 %reduce-scatter.5.cloned.1.call-start = ((), (), s32[]{:S(2)}) async-start(), calls=%async_computation.8 | async-start | bytes 3932160 | tf_op jit(solution)/shard_map/reduce_scatter | solution.py:298
  637.9 33.2 %collective-permute-start.82 = (bf16[256,2048]{1,0:T(8,128)(2,1)}, bf16[256,2048]{1,0:T(8,128)(2,1)}, u32[]{:S(2)}, u32[]{:S(2)}) collective-permute-start(bf16[256,2048]{1,0:T(8,128)(2,1)} %pad_maximum_fusion.6), channel_id=1, source_target_pairs={{0,2},{1,3},{2,0},{3,1},{4,6},{5,7},{6,4},{7,5},{8,10},{9,11},{10,... | collective-permute-start | bytes 3145736 | tf_op jit(solution)/shard_map/ppermute | solution.py:179
  715.3 56.9 %collective-permute-start.107 = (bf16[256,2048]{1,0:T(8,128)(2,1)}, bf16[256,2048]{1,0:T(8,128)(2,1)S(1)}, u32[]{:S(2)}, u32[]{:S(2)}) collective-permute-start(bf16[256,2048]{1,0:T(8,128)(2,1)} %reduce-scatter.11.cloned.1.call-done), channel_id=1, source_target_pairs={{0,16},{16,0},{1,17},{17,1},{2,18},{18,2},{3,19},{19,3},{4,20},{20... | collective-permute-start | bytes 3145736 | tf_op jit(solution)/shard_map/ppermute | solution.py:182
  716.2 39.5 %collective-permute-start.105 = (bf16[128,1024]{1,0:T(8,128)(2,1)S(1)}, bf16[128,1024]{1,0:T(8,128)(2,1)S(1)}, u32[]{:S(2)}, u32[]{:S(2)}) collective-permute-start(bf16[128,1024]{1,0:T(8,128)(2,1)S(1)} %get-tuple-element.98), channel_id=1, source_target_pairs={{0,3},{1,2},{2,1},{3,0},{4,7},{5,6},{6,5},{7,4},{8,11},{9,10},{10,... | collective-permute-start | bytes 786440 | tf_op jit(solution)/shard_map/ppermute | solution.py:179
  771.6 36.6 %collective-permute-start.86 = (bf16[4,128,768]{1,2,0:T(8,128)(2,1)}, bf16[4,128,768]{1,2,0:T(8,128)(2,1)}, u32[]{:S(2)}, u32[]{:S(2)}) collective-permute-start(bf16[4,128,768]{1,2,0:T(8,128)(2,1)} %bitcast_dynamic-update-slice_fusion.36), channel_id=1, source_target_pairs={{0,16},{16,0},{1,17},{17,1},{2,18},{18,2},{3,19},{19,3},{4,20},{20... | collective-permute-start | bytes 2359304 | tf_op jit(solution)/shard_map/ppermute | solution.py:182
  (139 other events, 2409.6 us)
Sparse Core Ops, SparseCore 0:
  9.6 30.6 all-gather.6
  42.4 63.9 all-gather.4
  108.6 79.2 all-gather.8
  189.9 79.2 all-gather.10
  504.4 28.1 reduce-scatter.6
  534.9 75.4 reduce-scatter.8
  613.2 77.2 reduce-scatter.10
  693.5 60.7 reduce-scatter.4

commit v3 on v2

v3 whole, which is shorter than its diff:
```python
import functools

import jax
import jax.numpy as jnp
from jax import lax
from jax.experimental import pallas as pl
from jax.experimental.pallas import tpu as pltpu
from jax.sharding import PartitionSpec as P

H = 32
HD = 64
BF = jnp.bfloat16
F32 = jnp.float32
LONGEST = 512
CHEAP = pl.CostEstimate(flops=1, transcendentals=0, bytes_accessed=1)


def dot(a, b, ca, cb):
    return lax.dot_general(a, b, (((ca,), (cb,)), ((), ())), preferred_element_type=F32)


def head_probs(query, key, slope, place, prefix, lanes):
    raw = dot(jnp.where(lanes, query, jnp.zeros_like(query)), key, 1, 1)
    row = place + lax.broadcasted_iota(jnp.int32, raw.shape, 0)
    column = lax.broadcasted_iota(jnp.int32, raw.shape, 1)
    distance = jnp.abs(row - column).astype(F32)
    allowed = column <= jnp.maximum(row, prefix - 1)
    logits = jnp.where(allowed, raw - slope * distance, -1e30)
    largest = jnp.max(logits, axis=-1, keepdims=True)
    exponent = jnp.exp(logits - largest)
    return exponent * (1.0 / jnp.sum(exponent, axis=-1, keepdims=True))


def forward_kernel(order_ref, prefix_ref, slope_ref, qkv_ref, out_ref):
    C, T = qkv_ref.shape[0] * qkv_ref.shape[2], qkv_ref.shape[3]
    seq, pair = pl.program_id(0), pl.program_id(1)
    at = lambda part: slice(part * 128, part * 128 + 128)
    first = lax.broadcasted_iota(jnp.int32, (T, 128), 1) < HD
    prefix = prefix_ref[seq]
    key = [qkv_ref[order_ref[0, c], 0, order_ref[1, c], :, at(1)] for c in range(C)]
    value = [qkv_ref[order_ref[0, c], 0, order_ref[1, c], :, at(2)] for c in range(C)]
    for c in range(C):
        n = min(C, max(c + 1, -(-LONGEST // T)))
        keys = jnp.concatenate(key[:n], axis=0)
        values = jnp.concatenate(value[:n], axis=0)
        query = qkv_ref[order_ref[0, c], 0, order_ref[1, c], :, at(0)] * 0.125
        out = []
        for h in range(2):
            probs = head_probs(query, keys, slope_ref[2 * pair + h], c * T, prefix, first if h == 0 else ~first)
            out.append(dot(probs.astype(BF), values, 1, 0))
        out_ref[0, c] = jnp.where(first, out[0], out[1]).astype(BF)


def backward_kernel(order_ref, prefix_ref, slope_ref, qkv_ref, d_out_ref, d_qkv_ref, d_key, d_value):
    C, T = qkv_ref.shape[0] * qkv_ref.shape[2], qkv_ref.shape[3]
    seq, pair = pl.program_id(0), pl.program_id(1)
    at = lambda part: slice(part * 128, part * 128 + 128)
    first = lax.broadcasted_iota(jnp.int32, (T, 128), 1) < HD
    prefix = prefix_ref[seq]
    d_key[...] = jnp.zeros_like(d_key)
    d_value[...] = jnp.zeros_like(d_value)
    key = [qkv_ref[order_ref[0, c], 0, order_ref[1, c], :, at(1)] for c in range(C)]
    value = [qkv_ref[order_ref[0, c], 0, order_ref[1, c], :, at(2)] for c in range(C)]
    for c in range(C):
        n = min(C, max(c + 1, -(-LONGEST // T)))
        keys = jnp.concatenate(key[:n], axis=0)
        values = jnp.concatenate(value[:n], axis=0)
        query = qkv_ref[order_ref[0, c], 0, order_ref[1, c], :, at(0)]
        d_out = d_out_ref[0, c]
        d_query = []
        for h in range(2):
            lanes = first if h == 0 else ~first
            probs = head_probs(query * 0.125, keys, slope_ref[2 * pair + h], c * T, prefix, lanes)
            mine = jnp.where(lanes, d_out, jnp.zeros_like(d_out))
            d_probs = dot(mine, values, 1, 1)
            weighted = jnp.sum(probs * d_probs, axis=-1, keepdims=True)
            d_raw = (probs * (d_probs - weighted) * 0.125).astype(BF)
            d_query.append(dot(d_raw, keys, 1, 0))
            d_value[: n * T] += dot(probs.astype(BF), mine, 0, 0)
            d_key[: n * T] += dot(d_raw, jnp.where(lanes, query, jnp.zeros_like(query)), 0, 0)
        d_qkv_ref[order_ref[0, c], 0, order_ref[1, c], :, at(0)] = jnp.where(first, d_query[0], d_query[1]).astype(BF)
    for c in range(C):
        d_qkv_ref[order_ref[0, c], 0, order_ref[1, c], :, at(1)] = d_key[c * T : (c + 1) * T].astype(BF)
        d_qkv_ref[order_ref[0, c], 0, order_ref[1, c], :, at(2)] = d_value[c * T : (c + 1) * T].astype(BF)


def attention_specs(order_ndim, K, n, Y, C, T, pair):
    near = pl.BlockSpec((K, 1, Y, T, 384), lambda s, p, *_: (0, s, 0, 0, p + pair))
    true = pl.BlockSpec((1, C, T, 128), lambda s, p, order, *_: (s ^ order[2, 0], 0, 0, p + pair))
    return near, true


def attention_forward(order, prefix, slopes, qkv):
    K, n, Y, T = qkv.shape[:4]
    C, pairs = K * Y, qkv.shape[4] // 384
    near, true = attention_specs(0, K, n, Y, C, T, 0)
    return pl.pallas_call(
        forward_kernel,
        out_shape=jax.ShapeDtypeStruct((n, C, T, pairs * 128), BF),
        grid_spec=pltpu.PrefetchScalarGridSpec(num_scalar_prefetch=3, grid=(n, pairs), in_specs=[near], out_specs=true),
        compiler_params=vmem(32),
        cost_estimate=CHEAP,
    )(order, prefix, slopes, qkv)


def attention_backward(pair, order, prefix, slopes, qkv, d_out, before=None):
    K, n, Y, T = qkv.shape[:4]
    C = K * Y
    near, true = attention_specs(0, K, n, Y, C, T, pair)
    kernel = backward_kernel
    more, aliases = [], {}
    if before is not None:
        kernel = lambda a, b, c, d, e, _, *rest: backward_kernel(a, b, c, d, e, *rest)
        more, aliases = [before], {5: 0}
    return pl.pallas_call(
        kernel,
        out_shape=jax.ShapeDtypeStruct(qkv.shape, BF),
        grid_spec=pltpu.PrefetchScalarGridSpec(
            num_scalar_prefetch=3,
            grid=(n, 1),
            in_specs=[near, true] + [pl.BlockSpec(memory_space=pl.ANY)] * len(more),
            out_specs=near,
            scratch_shapes=[pltpu.VMEM((C * T, 128), F32), pltpu.VMEM((C * T, 128), F32)],
        ),
        input_output_aliases=aliases,
        compiler_params=vmem(32),
        cost_estimate=CHEAP,
    )(order, prefix, slopes, qkv, d_out, *more)


def whole(shape):
    return pl.BlockSpec(shape, lambda *_: (0,) * len(shape))


def vmem(megabytes):
    return pltpu.CompilerParams(vmem_limit_bytes=megabytes * 1024 * 1024)


def half_turn(tile):
    return jnp.concatenate([tile[:, 64:], tile[:, :64]], axis=1)


def pack_kernel(F, C, rep_ref, joined_ref, expand_ref, out_ref):
    B = joined_ref.shape[0]
    E = expand_ref.shape[1] // (2 * F * C)
    D = joined_ref.shape[1] // 3
    first = lax.broadcasted_iota(jnp.int32, (B, 128), 1) < HD
    rep = rep_ref[0]
    keep = first == (rep == 0)
    for c in range(C):
        for p in range(F // 2):
            for q in range(3):
                one, two = [joined_ref[:, q * D + (f * C + c) * 128 :][:, :128] for f in (2 * p, 2 * p + 1)]
                mine = jnp.where(keep, jnp.where(first, one, two), half_turn(jnp.where(first, two, one)))
                out_ref[c, :, (p * 3 + q) * 128 : (p * 3 + q + 1) * 128] = mine
        for f in range(F):
            from_ = pl.multiple_of((f * C + c) * 2 * E + rep * E, 128)
            to = 3 * F * 64 + f * E
            out_ref[c, :, to : to + E] = expand_ref[:, pl.ds(from_, E)]


def pack(F, C, rep, joined, expand):
    B = joined.shape[0]
    width = 3 * F * 64 + expand.shape[1] // (2 * C)
    return pl.pallas_call(
        functools.partial(pack_kernel, F, C),
        out_shape=jax.ShapeDtypeStruct((C, B, width), BF),
        grid_spec=pltpu.PrefetchScalarGridSpec(
            num_scalar_prefetch=1,
            grid=(1,),
            in_specs=[whole(joined.shape), whole(expand.shape)],
            out_specs=whole((C, B, width)),
        ),
        compiler_params=vmem(24),
        cost_estimate=CHEAP,
    )(rep.reshape(1), joined, expand)


def unpack_joined_kernel(F, rep_ref, own_ref, other_ref, out_ref):
    C, B = own_ref.shape[:2]
    D = out_ref.shape[1] // 3
    first = lax.broadcasted_iota(jnp.int32, (B, 128), 1) < HD
    swap = rep_ref[0] == 1
    for c in range(C):
        for p in range(F // 2):
            for q in range(3):
                at = slice((p * 3 + q) * 128, (p * 3 + q + 1) * 128)
                own, other = own_ref[c, :, at].astype(F32), other_ref[c, :, at].astype(F32)
                one, two = jnp.where(swap, other, own), jnp.where(swap, own, other)
                for i, f in enumerate((2 * p, 2 * p + 1)):
                    if i == 0:
                        tile = jnp.where(first, one, half_turn(two))
                    else:
                        tile = jnp.where(first, half_turn(one), two)
                    out_ref[:, q * D + (f * C + c) * 128 : q * D + (f * C + c + 1) * 128] = tile


def unpack_expand_kernel(F, rep_ref, own_ref, other_ref, out_ref):
    C = own_ref.shape[0]
    E = own_ref.shape[2] // F
    for c in range(C):
        for f in range(F):
            at = (f * C + c) * 2 * E
            mine = pl.multiple_of(at + rep_ref[0] * E, 128)
            theirs = pl.multiple_of(at + (1 - rep_ref[0]) * E, 128)
            out_ref[:, pl.ds(mine, E)] = own_ref[c, :, f * E : (f + 1) * E].astype(F32)
            out_ref[:, pl.ds(theirs, E)] = other_ref[c, :, f * E : (f + 1) * E].astype(F32)


def unpack(kernel, F, rep, own, other):
    C, B, width = own.shape
    return pl.pallas_call(
        functools.partial(kernel, F),
        out_shape=jax.ShapeDtypeStruct((B, 2 * C * width), F32),
        grid_spec=pltpu.PrefetchScalarGridSpec(
            num_scalar_prefetch=1,
            grid=(1,),
            in_specs=[whole(own.shape), whole(own.shape)],
            out_specs=whole((B, 2 * C * width)),
        ),
        compiler_params=vmem(32),
        cost_estimate=CHEAP,
    )(rep.reshape(1), own, other)


def normed(values):
    average = jnp.mean(values, axis=-1, keepdims=True)
    centred = values - average
    variance = jnp.mean(centred * centred, axis=-1, keepdims=True)
    inverse = lax.rsqrt(variance + 1e-05)
    return centred * inverse, inverse


def norm_kernel(x_ref, gain_ref, shift_ref, out_ref):
    n, _ = normed(x_ref[...].astype(F32))
    out_ref[...] = (n * gain_ref[...] + shift_ref[...]).astype(BF)


def norm(x, gain, shift):
    rows, D = x.shape
    step = min(rows, 256)
    return pl.pallas_call(
        norm_kernel,
        out_shape=jax.ShapeDtypeStruct((rows, D), BF),
        grid=(rows // step,),
        in_specs=[pl.BlockSpec((step, D), lambda i: (i, 0)), whole((1, D)), whole((1, D))],
        out_specs=pl.BlockSpec((step, D), lambda i: (i, 0)),
        compiler_params=vmem(24),
        cost_estimate=CHEAP,
    )(x, gain.reshape(1, D), shift.reshape(1, D))


def attended_kernel(table_ref, o_ref, w_ref, v_ref, x_ref, bias_ref, gain_ref, shift_ref, mid_ref, out_ref):
    d = pl.program_id(0)
    half = pl.num_programs(0) // 2
    weight = jnp.where(d < half, w_ref[0], v_ref[0])
    product = dot(o_ref[0], weight, 1, 0)

    @pl.when(d == 0)
    def _():
        mid_ref[...] = product + x_ref[...].astype(F32) + bias_ref[...]

    @pl.when(d > 0)
    def _():
        mid_ref[...] += product

    @pl.when(d == pl.num_programs(0) - 1)
    def _():
        n, _ = normed(mid_ref[...])
        out_ref[...] = (n * gain_ref[...] + shift_ref[...]).astype(BF)


def attended(table, o, weights, x, bias, gain, shift):
    N, t, W = o.shape
    D = x.shape[1]
    half = N // 2
    weights = [w.reshape(half, W, D) for w in weights]
    return pl.pallas_call(
        attended_kernel,
        out_shape=(jax.ShapeDtypeStruct((t, D), F32), jax.ShapeDtypeStruct((t, D), BF)),
        grid_spec=pltpu.PrefetchScalarGridSpec(
            num_scalar_prefetch=1,
            grid=(N,),
            in_specs=[
                pl.BlockSpec((1, t, W), lambda d, table: (table[d], 0, 0)),
                pl.BlockSpec((1, W, D), lambda d, table: (jnp.minimum(d, half - 1), 0, 0)),
                pl.BlockSpec((1, W, D), lambda d, table: (jnp.maximum(d - half, 0), 0, 0)),
                whole((t, D)),
                whole((1, D)),
                whole((1, D)),
                whole((1, D)),
            ],
            out_specs=(whole((t, D)), whole((t, D))),
        ),
        compiler_params=vmem(32),
        cost_estimate=CHEAP,
    )(table, o, *weights, x, bias.reshape(1, D), gain.reshape(1, D), shift.reshape(1, D))


def turned_kernel(table_ref, a_ref, b_ref, c_ref, mid_ref, g_ref, gain_ref, w_ref, v_ref, d_mid_ref, d_att_ref, sums_ref, d_o_ref):
    d = pl.program_id(0)
    half = pl.num_programs(0) // 2

    @pl.when(d == 0)
    def _():
        grad = a_ref[...] + b_ref[...].astype(F32) + c_ref[...].astype(F32)
        n, inverse = normed(mid_ref[...])
        g = g_ref[...].astype(F32)
        u = grad * gain_ref[...]
        mean_u = jnp.mean(u, axis=-1, keepdims=True)
        mean_un = jnp.mean(u * n, axis=-1, keepdims=True)
        d_mid = g + (u - mean_u - n * mean_un) * inverse
        d_att = d_mid.astype(BF)
        d_mid_ref[...] = d_mid
        d_att_ref[...] = d_att
        rows = (grad * n, grad, d_att.astype(F32), g)
        for i, row in enumerate(rows):
            sums_ref[i : i + 1] = jnp.sum(row, axis=0, keepdims=True)

    weight = jnp.where(d < half, w_ref[0], v_ref[0])
    d_o_ref[0] = dot(d_att_ref[...], weight, 1, 1).astype(BF)


def turned(table, parts, mid, g, gain, weights):
    t, D = mid.shape
    N = table.shape[0]
    half = N // 2
    W = D // N
    weights = [w.reshape(half, W, D) for w in weights]
    full = whole((t, D))
    return pl.pallas_call(
        turned_kernel,
        out_shape=(
            jax.ShapeDtypeStruct((t, D), F32),
            jax.ShapeDtypeStruct((t, D), BF),
            jax.ShapeDtypeStruct((4, D), F32),
            jax.ShapeDtypeStruct((N, t, W), BF),
        ),
        grid_spec=pltpu.PrefetchScalarGridSpec(
            num_scalar_prefetch=1,
            grid=(N,),
            in_specs=[
                full,
                full,
                full,
                full,
                full,
                whole((1, D)),
                pl.BlockSpec((1, W, D), lambda d, table: (jnp.minimum(d, half - 1), 0, 0)),
                pl.BlockSpec((1, W, D), lambda d, table: (jnp.maximum(d - half, 0), 0, 0)),
            ],
            out_specs=(full, full, whole((4, D)), pl.BlockSpec((1, t, W), lambda d, table: (table[d], 0, 0))),
        ),
        compiler_params=vmem(48),
        cost_estimate=CHEAP,
    )(table, *parts, mid, g, gain.reshape(1, D), *weights)


def outer_kernel(table_ref, o_ref, d_att_ref, own_ref, oth_ref):
    d = pl.program_id(0)
    product = dot(o_ref[0], d_att_ref[...], 0, 0).astype(BF)

    @pl.when(d < pl.num_programs(0) // 2)
    def _():
        own_ref[0] = product

    @pl.when(d >= pl.num_programs(0) // 2)
    def _():
        oth_ref[0] = product


def outer(table, o, d_att):
    N, t, W = o.shape
    D = d_att.shape[1]
    half = N // 2
    return pl.pallas_call(
        outer_kernel,
        out_shape=(jax.ShapeDtypeStruct((half, W, D), BF), jax.ShapeDtypeStruct((half, W, D), BF)),
        grid_spec=pltpu.PrefetchScalarGridSpec(
            num_scalar_prefetch=1,
            grid=(N,),
            in_specs=[pl.BlockSpec((1, t, W), lambda d, table: (table[d], 0, 0)), whole((t, D))],
            out_specs=(
                pl.BlockSpec((1, W, D), lambda d, table: (jnp.minimum(d, half - 1), 0, 0)),
                pl.BlockSpec((1, W, D), lambda d, table: (jnp.maximum(d - half, 0), 0, 0)),
            ),
        ),
        compiler_params=vmem(24),
        cost_estimate=CHEAP,
    )(table, o, d_att)


def last_kernel(a_ref, b_ref, c_ref, x_ref, d_mid_ref, gain_ref, out_ref):
    grad = a_ref[...] + b_ref[...].astype(F32) + c_ref[...].astype(F32)
    n, inverse = normed(x_ref[...].astype(F32))
    u = grad * gain_ref[...]
    mean_u = jnp.mean(u, axis=-1, keepdims=True)
    mean_un = jnp.mean(u * n, axis=-1, keepdims=True)
    out_ref[...] = d_mid_ref[...] + (u - mean_u - n * mean_un) * inverse


def last(parts, x, d_mid, gain):
    t, D = x.shape
    full = whole((t, D))
    return pl.pallas_call(
        last_kernel,
        out_shape=jax.ShapeDtypeStruct((t, D), F32),
        grid=(1,),
        in_specs=[full] * 5 + [whole((1, D))],
        out_specs=full,
        compiler_params=vmem(48),
        cost_estimate=CHEAP,
    )(*parts, x, d_mid, gain.reshape(1, D))


def pair_up_kernel(rep_ref, own_ref, other_ref, out_ref):
    m = own_ref.shape[0]
    mine = pl.multiple_of(rep_ref[0] * m, 8)
    theirs = pl.multiple_of((1 - rep_ref[0]) * m, 8)
    out_ref[pl.ds(mine, m)] = own_ref[...].astype(F32)
    out_ref[pl.ds(theirs, m)] = other_ref[...].astype(F32)


def pair_up(rep, own, other):
    m, D = own.shape
    return pl.pallas_call(
        pair_up_kernel,
        out_shape=jax.ShapeDtypeStruct((2 * m, D), F32),
        grid_spec=pltpu.PrefetchScalarGridSpec(
            num_scalar_prefetch=1,
            grid=(1,),
            in_specs=[whole((m, D)), whole((m, D))],
            out_specs=whole((2 * m, D)),
        ),
        compiler_params=vmem(24),
        cost_estimate=CHEAP,
    )(rep.reshape(1), own, other)


def columns_kernel(count, *refs):
    grads, w_ref, sums_ref, gain_ref, shift_ref, rest_ref, out_ref = refs[:count], *refs[count:]
    width = grads[0].shape[1]
    by_d = jnp.zeros((w_ref.shape[0], 1), F32)
    by_g = jnp.zeros((w_ref.shape[0], 1), F32)
    for p, grad_ref in enumerate(grads):
        w = w_ref[:, p * width : (p + 1) * width].astype(F32)
        by_d += jnp.sum(w * sums_ref[:, p * width : (p + 1) * width], axis=1, keepdims=True)
        by_g += jnp.sum(w * grad_ref[...].astype(F32), axis=1, keepdims=True)
    by_n = (by_g - shift_ref[:, :1] * by_d) / gain_ref[:, :1]
    lane = lax.broadcasted_iota(jnp.int32, (w_ref.shape[0], 128), 1)
    small = jnp.where(lane == 0, by_n, jnp.where(lane == 1, by_d, rest_ref[...]))
    out_ref[:, :width] = grads[-1][...]
    out_ref[:, width:] = small.astype(BF)


def with_columns(grads, weight, sums, gain, shift, rest):
    D, width = grads[0].shape
    step = 512
    rows = lambda w: pl.BlockSpec((step, w), lambda i: (i, 0))
    return pl.pallas_call(
        functools.partial(columns_kernel, len(grads)),
        out_shape=jax.ShapeDtypeStruct((D, width + 128), BF),
        grid=(D // step,),
        in_specs=[rows(width)] * len(grads) + [rows(weight.shape[1]), whole(sums.shape), rows(128), rows(128), rows(128)],
        out_specs=rows(width + 128),
        compiler_params=vmem(32),
        cost_estimate=CHEAP,
    )(*grads, weight, sums, gain, shift, rest)


def part_weights_kernel(m, rows, early_ref, late_ref, expand_ref, shrink_ref):
    half = shrink_ref.shape[0] // 2
    width = late_ref.shape[2]
    expand_ref[...] = late_ref[0, :rows]
    shrink_ref[:half] = early_ref[0, m : m + half]
    shrink_ref[half:, :width] = late_ref[0, rows : rows + half]
    shrink_ref[half:, width:] = late_ref[0, rows + half : rows + 2 * half]


def part_weights(early, late, m, rows):
    F, _, D = early.shape
    width = late.shape[2]
    half = (late.shape[1] - rows) // 2
    return pl.pallas_call(
        functools.partial(part_weights_kernel, m, rows),
        out_shape=(jax.ShapeDtypeStruct((F * rows, width), BF), jax.ShapeDtypeStruct((F * 2 * half, D), BF)),
        grid=(F,),
        in_specs=[
            pl.BlockSpec((1,) + early.shape[1:], lambda f: (f, 0, 0)),
            pl.BlockSpec((1,) + late.shape[1:], lambda f: (f, 0, 0)),
        ],
        out_specs=(pl.BlockSpec((rows, width), lambda f: (f, 0)), pl.BlockSpec((2 * half, D), lambda f: (f, 0))),
        compiler_params=vmem(32),
        cost_estimate=CHEAP,
    )(early, late)


def gelu_and_slope(values):
    half = 0.5 + 0.5 * lax.erf(values * 0.7071067811865476)
    density = jnp.exp(values * values * -0.5) * 0.3989422804014327
    return (values * half).astype(BF), (half + values * density).astype(BF)


def together(*values):
    return lax.optimization_barrier(values)


class Plain:
    def __init__(self, R, C):
        self.R, self.C, self.N = R, C, R * C
        self.axes = ("rep", "ctx")
        self.groups = (1, R, C)
        place = jnp.arange(C, dtype=jnp.int32)
        self.order = jnp.stack([place * 0, place, place * 0])
        self.table = jnp.arange(self.N, dtype=jnp.int32)

    def gather(self, x, beside=()):
        out, beside = together(lax.all_gather(x, self.axes, axis=0, tiled=True), beside)
        return [out], beside

    def scatter_core(self, rows, part):
        return part(0, 0, self.N * rows).astype(BF)

    def scatter_far(self, state):
        return state

    def scatter_near(self, state):
        return lax.psum_scatter(state, self.axes, scatter_dimension=0, tiled=True)

    def scatter_end(self, state):
        return state.astype(F32), jnp.zeros_like(state), jnp.zeros_like(state)

    def swap(self, parts):
        return lax.all_to_all(parts, self.axes, 0, 0, tiled=True)

    def swap_ctx(self, blocks):
        return lax.all_to_all(blocks, "ctx", 0, 0, tiled=True)

    def prefixes(self, prefix):
        return lax.all_gather(prefix, "rep", axis=0, tiled=True)


class Near(Plain):
    def __init__(self, R, F, C):
        super().__init__(R, C)
        self.F = F
        self.ctx = lax.axis_index("ctx")
        self.rep = lax.axis_index("rep")
        self.fsdp = lax.axis_index("fsdp")
        self.groups = (2, 2, 2)
        place = jnp.arange(C, dtype=jnp.int32) ^ self.ctx
        self.order = jnp.stack([place & 1, place >> 1, place * 0 + self.rep])
        d = jnp.arange(8, dtype=jnp.int32)
        self.table = (self.rep * 4 + self.ctx) ^ ((d & 2) * 2 + (d & 1) * 2 + (d >> 2))

    def over(self, x, d):
        return lax.ppermute(x, "ctx", [(i, i ^ d) for i in range(4)])

    def x(self, x):
        return lax.ppermute(x, "rep", [(0, 1), (1, 0)])

    def y(self, x):
        return self.over(x, 2)

    def core(self, x):
        return self.over(x, 1)

    def gather(self, x, beside=()):
        half = x.shape[0] // 2
        from_x, from_y = self.x(x), self.y(x)
        if beside:
            from_x, from_y, beside = together(from_x, from_y, beside)
        own = jnp.concatenate([x, from_y, from_x, self.y(from_x[:half]), self.x(from_y[half:])], axis=0)
        return [own, self.core(own)], beside

    def scatter_core(self, rows, part):
        far_x = part(1, 2 * rows, 4 * rows).astype(BF)
        near_x = part(1, 0, 2 * rows).astype(BF)
        far_x = part(0, 2 * rows, 4 * rows) + self.core(far_x).astype(F32)
        near_x = part(0, 0, 2 * rows) + self.core(near_x).astype(F32)
        return far_x, near_x

    def scatter_given(self, own, oth):
        total = (own.astype(F32) + self.core(oth).astype(F32)).astype(BF)
        return total[total.shape[0] // 2 :], total[: total.shape[0] // 2]

    def scatter_far(self, state):
        far_x, near_x = state
        rows = far_x.shape[0] // 2
        far = far_x[rows:].astype(BF)
        return far_x[:rows].astype(F32), near_x.astype(F32), self.y(far[: rows // 2]), self.x(far[rows // 2 :])

    def scatter_near(self, state):
        by_x, near_x, to_y, to_x = state
        rows = by_x.shape[0]
        half = rows // 2
        by_x = jnp.concatenate([by_x[:half] + to_y.astype(F32), by_x[half:]], axis=0)
        by_y = jnp.concatenate([near_x[rows : rows + half], near_x[rows + half :] + to_x.astype(F32)], axis=0)
        return near_x[:rows], self.x(by_x.astype(BF)), self.y(by_y.astype(BF))

    def scatter_end(self, state):
        return state

    def prefixes(self, prefix):
        return jnp.concatenate([prefix, self.x(prefix)])

    def gather_ctx(self, x):
        x = jnp.stack([x, self.y(x)])
        x = jnp.stack([x, self.core(x)], axis=1).reshape(4, *x.shape[1:])
        x = jnp.take(x, jnp.arange(4) ^ self.ctx, axis=0)
        return x.transpose(1, 0, 2).reshape(-1, x.shape[2])


def added(parts):
    return sum(a.astype(F32) for a in parts)


def scatter_shifts(x, axis, size):
    me = lax.axis_index(axis)
    total = lax.dynamic_index_in_dim(x, me, 0, keepdims=False)
    for s in range(1, size):
        mine = lax.dynamic_index_in_dim(x, lax.rem(me + s, size), 0, keepdims=False)
        total = total.astype(F32) + lax.ppermute(mine, axis, [(i, (i + s) % size) for i in range(size)]).astype(F32)
    return total.astype(x.dtype)


def shards(
    sizes,
    inputs,
    prefix,
    joined_weight,
    query_bias,
    value_bias,
    dense_weight,
    dense_bias,
    expand_weight,
    expand_bias,
    shrink_weight,
    shrink_bias,
    first_gain,
    first_shift,
    second_gain,
    second_shift,
    cotangent,
):
    R, F, C = sizes
    N = R * C
    rep = lax.axis_index("rep")
    ctx = lax.axis_index("ctx")
    S, t, D = inputs.shape
    assert S == 1
    B = joined_weight.shape[0]
    FFB = shrink_weight.shape[0]
    FF = FFB * F * C
    E = FFB // R
    W = D // N
    near = R == 2 and C == 4 and B == 2 * HD
    tp = Near(R, F, C) if near else Plain(R, C)
    K, _, Y = tp.groups
    G = range(K)
    n = N // K
    pairs = W // 128

    def half_rows(weight):
        m = weight.shape[0] // R
        return lax.dynamic_slice_in_dim(weight, rep * m, m, 0)

    def widen(blocks):
        return lax.all_gather(blocks.reshape(C * B, -1), "fsdp", axis=0, tiled=True)

    def over_rep(x):
        return lax.ppermute(x, "rep", [(0, 1), (1, 0)])

    x = inputs.reshape(t, D)
    g = cotangent.reshape(t, D)
    small = jnp.concatenate(
        [first_gain, first_shift, second_gain, second_shift, dense_bias, shrink_bias, query_bias, value_bias, expand_bias]
    )
    if near:
        low, high = jnp.split(half_rows(shrink_weight), 2)
        m = B // R
        small = jnp.pad(small.reshape(1, -1), ((0, 15), (0, D - small.shape[0])))
        early = lax.all_gather(jnp.concatenate([half_rows(dense_weight), low, small]), "fsdp", axis=0, tiled=False)
        dense_rows = early[:, :m].reshape(F * m, D)
        small = tp.gather_ctx(early[:, m + low.shape[0], : 8 * B + FFB])
        blocks = lax.all_to_all(pack(F, C, rep, joined_weight, expand_weight), "ctx", 0, 0, tiled=True)
        joined_blocks, expand_blocks = blocks[:, :, : 3 * W], blocks[:, :, 3 * W :]
    else:
        dense_rows = lax.all_gather(dense_weight, ("fsdp", "ctx"), axis=0, tiled=True)
        small = lax.all_gather(small, ("fsdp", "ctx"), axis=0, tiled=False)
        pieces = joined_weight.reshape(B, 3, R, C, pairs, 128)
        pieces = lax.dynamic_index_in_dim(pieces, rep, 2, keepdims=False).transpose(2, 0, 3, 1, 4)
        joined_blocks = lax.all_to_all(pieces.reshape(C, B, 3 * W), "ctx", 0, 0, tiled=True)
        pieces = expand_weight.reshape(B, F, C, R, E)
        pieces = lax.dynamic_index_in_dim(pieces, rep, 3, keepdims=False).transpose(2, 0, 1, 3)
        expand_blocks = lax.all_to_all(pieces.reshape(C, B, F * E), "ctx", 0, 0, tiled=True)
    joined_cols = widen(joined_blocks)
    if near:
        late = jnp.concatenate([expand_blocks.reshape(C * B, -1), high[:, : D // 2], high[:, D // 2 :]])
        late = lax.all_gather(late, "fsdp", axis=0, tiled=False)
        expand_cols, shrink_rows = part_weights(early, late, m, C * B)
    else:
        expand_cols = widen(expand_blocks)
        shrink_rows = lax.all_gather(half_rows(shrink_weight), "fsdp", axis=0, tiled=True)
    prefixes = tp.prefixes(prefix)
    x_all, _ = tp.gather(x)

    small = small.astype(F32)
    gain_one, shift_one, gain_two, shift_two, dbias, sbias, qbias, vbias = [
        small[:, i * B : (i + 1) * B].reshape(D) for i in range(8)
    ]
    ebias = small[:, 8 * B :].reshape(F, C, R, E)
    ebias = lax.dynamic_index_in_dim(lax.dynamic_index_in_dim(ebias, ctx, 1, False), rep, 1, False)
    ebias = ebias.reshape(F * E)

    def my_features(vector):
        if near:
            v = vector.reshape(F, C, R, -1)
            return lax.dynamic_index_in_dim(lax.dynamic_index_in_dim(v, ctx, 1, False), rep, 1, False).reshape(W)
        return lax.dynamic_slice_in_dim(vector, (rep * C + ctx) * W, W, 0)

    my_heads = my_features(jnp.repeat(jnp.arange(H, dtype=jnp.int32), HD)).reshape(-1, HD)[:, 0]
    slopes = jnp.exp2(-8.0 * (my_heads.astype(F32) + 1.0) / H)

    a1_all = [norm(a, gain_one, shift_one) for a in x_all]
    if near:
        a1_all, dense_rows = together(a1_all, dense_rows)
        dense_all, _ = tp.gather(dense_rows)
        own, g = together(dense_all[0], g)
        dense_all[0] = own
    else:
        dense_all = [dense_rows[: D // 2], dense_rows[D // 2 :]]
    g_all, _ = tp.gather(g)
    qkv_bias = jnp.stack([my_features(qbias), jnp.zeros((W,), F32), my_features(vbias)])
    qkv_bias = qkv_bias.reshape(3, pairs, 128).transpose(1, 0, 2).reshape(3 * W)
    qkv = jnp.stack([(dot(a, joined_cols, 1, 0) + qkv_bias).astype(BF) for a in a1_all])
    qkv = qkv.reshape(K, R, Y, t, 3 * W)
    out = attention_forward(tp.order, prefixes, slopes, qkv)
    o = tp.swap(out.reshape(N, t, W))
    o, g_all = together(o, g_all)
    midway, a2 = attended(tp.table, o, dense_all, x, dbias, gain_two, shift_two)

    a2_all, _ = tp.gather(a2)
    act, slope = zip(*[gelu_and_slope(dot(a, expand_cols, 1, 0) + ebias) for a in a2_all])
    shrink_grad = sum(dot(act[i], g_all[i], 0, 0) for i in G).astype(BF)
    slope, shrink_grad, act = together(slope, shrink_grad, act)
    shrink_part = lax.psum_scatter(shrink_grad, "fsdp", scatter_dimension=0, tiled=True)
    d_exp = [(dot(g_all[i], shrink_rows, 1, 1) * slope[i].astype(F32)).astype(BF) for i in G]

    d_a2 = tp.scatter_core(t, lambda i, a, b: dot(d_exp[i][a:b], expand_cols, 1, 1))
    d_a2, d_exp = together(tp.scatter_far(d_a2), d_exp)
    d_a2 = tp.scatter_near(d_a2)
    expand_grad = sum(dot(a2_all[i], d_exp[i], 0, 0) for i in G).astype(BF)
    d_a2, expand_grad = together(d_a2, expand_grad)
    d_mid, d_att, sums_two, d_o = turned(tp.table, tp.scatter_end(d_a2), midway, g, gain_two, dense_all)
    d_o, expand_grad, shrink_part = together(d_o, expand_grad, shrink_part)
    expand_part = lax.psum_scatter(expand_grad, "fsdp", scatter_dimension=0, tiled=True)

    d_o = tp.swap(d_o).reshape(R, C, t, W)
    shrink_other = over_rep(shrink_part)
    dense_part = outer(tp.table, o, d_att) if near else ()
    d_o, dense_part = together(d_o, dense_part)
    if near:
        dense_part = tp.scatter_given(*[a.reshape(n * W, D) for a in dense_part])
    d_qkv, joined_grad = None, []
    for p in range(pairs):
        d_qkv = attention_backward(p, tp.order, prefixes, slopes[2 * p : 2 * p + 2], qkv, d_o, d_qkv)
        mine = d_qkv.reshape(K, n * t, 3 * W)[:, :, 384 * p : 384 * (p + 1)]
        grad = sum(dot(a1_all[i], mine[i], 0, 0) for i in G).astype(BF)
        d_qkv, grad, d_o, act, dense_part = together(d_qkv, grad, d_o, act, dense_part)
        joined_grad.append(grad)
        if p == 0 and near:
            dense_part = tp.scatter_far(dense_part)
    d_qkv = d_qkv.reshape(K, n * t, 3 * W)

    d_qkv_sum = jnp.sum(d_qkv.astype(F32), axis=(0, 1))
    d_exp_sum = sum(jnp.sum(d.astype(F32), axis=0) for d in d_exp)

    def place(vector, width):
        if near or width != D:
            full = jnp.zeros((F, C, R, width // (F * C * R)), F32)
            full = lax.dynamic_update_slice(full, vector.reshape(F, 1, 1, -1), (0, ctx, rep, 0))
            return full.reshape(F * C, width // D, B).transpose(0, 2, 1).reshape(D, width // D)
        return lax.dynamic_update_slice_in_dim(jnp.zeros((width,), F32), vector, (rep * C + ctx) * W, 0).reshape(D, 1)

    by_part = d_qkv_sum.reshape(pairs, 3, 128)
    rest = [jnp.zeros((D, 2), F32), sums_two.T, place(by_part[:, 0].reshape(W), D), place(by_part[:, 2].reshape(W), D)]
    rest.append(place(d_exp_sum, FF))
    rest = jnp.concatenate(rest, axis=1)
    used = rest.shape[1]
    rest = jnp.pad(rest, ((0, 0), (0, 128 - used)))
    lanes = lambda a: jnp.broadcast_to(a[:, None], (D, 128))
    grad = with_columns(joined_grad, joined_cols, d_qkv_sum.reshape(1, 3 * W), lanes(gain_one), lanes(shift_one), rest)
    expand_part, shrink_other, joined_grad = together(expand_part, shrink_other, joined_grad[:-1] + [grad])
    joined_part = [lax.psum_scatter(a, "fsdp", scatter_dimension=0, tiled=True) for a in joined_grad]
    expand_own = lax.all_to_all(expand_part.reshape(C, B, -1), "ctx", 0, 0, tiled=True)

    d_a1 = tp.scatter_core(t, lambda i, a, b: dot(d_qkv[i, a:b], joined_cols, 1, 1))
    if near:
        dense_part = tp.scatter_near(dense_part)
    d_a1, expand_own, dense_part, act = together(d_a1, expand_own, dense_part, act)
    d_a1 = tp.scatter_far(d_a1)
    expand_other = over_rep(expand_own)
    if near:
        shrink_out = pair_up(rep, shrink_part, shrink_other)
        dense_part = added(tp.scatter_end(dense_part)).astype(BF).reshape(F, W // F, D)
        dense_part = scatter_shifts(dense_part, "fsdp", F)

    branch = tp.scatter_core(t, lambda i, a, b: dot(act[i][a:b], shrink_rows, 1, 0))
    d_a1, branch, dense_part = together(d_a1, branch, dense_part)
    d_a1 = tp.scatter_near(d_a1)
    branch = tp.scatter_far(branch)
    d_a1, branch, expand_other = together(d_a1, branch, expand_other)
    if near:
        expand_out = unpack(unpack_expand_kernel, F, rep, expand_own, expand_other)
    branch = tp.scatter_near(branch)
    input_gradient = last(tp.scatter_end(d_a1), x, d_mid, gain_one)
    branch, input_gradient = together(branch, input_gradient)
    layer_output = midway + added(tp.scatter_end(branch)) + sbias

    def both_reps(own, other):
        first = rep == 0
        return jnp.stack([jnp.where(first, own, other), jnp.where(first, other, own)])

    joined_own = [lax.all_to_all(a.reshape(C, B, -1), "ctx", 0, 0, tiled=True) for a in joined_part]
    joined_other = [over_rep(a) for a in joined_own]
    little = jnp.sum((joined_own[-1][:, :, 384:].astype(F32) + joined_other[-1][:, :, 384:].astype(F32)), axis=0).T
    joined_own = jnp.concatenate([a[:, :, :384] for a in joined_own], axis=2)
    joined_other = jnp.concatenate([a[:, :, :384] for a in joined_other], axis=2)
    if near:
        joined_out = unpack(unpack_joined_kernel, F, rep, joined_own, joined_other)
        dense_out = pair_up(rep, dense_part, over_rep(dense_part))
    else:
        both = both_reps(expand_own, expand_other).reshape(R, C, B, F, E).transpose(2, 3, 1, 0, 4)
        expand_out = both.reshape(B, FF).astype(F32)
        both = both_reps(joined_own, joined_other).reshape(R, C, B, pairs, 3, 128).transpose(2, 4, 0, 1, 3, 5)
        joined_out = both.reshape(B, 3 * D).astype(F32)
        shrink_out = both_reps(shrink_part, shrink_other).reshape(FFB, D).astype(F32)
        part = dot(o.transpose(1, 0, 2).reshape(t, D), d_att, 0, 0).astype(BF)
        part = lax.psum_scatter(part, ("fsdp", "ctx"), scatter_dimension=0, tiled=True)
        dense_out = lax.psum(part, "rep").astype(F32)
    gain_one_out, shift_one_out, gain_two_out, shift_two_out, dbias_out, sbias_out, qbias_out, vbias_out = [
        little[i] for i in range(8)
    ]
    ebias_out = little[8:used].reshape(FFB)

    return (
        layer_output.reshape(S, t, D),
        input_gradient.reshape(S, t, D),
        joined_out,
        qbias_out,
        vbias_out,
        dense_out,
        dbias_out,
        expand_out,
        ebias_out,
        shrink_out,
        sbias_out,
        gain_one_out,
        shift_one_out,
        gain_two_out,
        shift_two_out,
    )


def solution(mesh):
    sizes = (mesh.shape["rep"], mesh.shape["fsdp"], mesh.shape["ctx"])
    tokens = P(("rep", "fsdp"), "ctx", None)
    matrix = P(("fsdp", "ctx"), None)
    vector = P(("fsdp", "ctx"))
    weights = (matrix, vector, vector, matrix, vector, matrix, vector, matrix, vector, vector, vector, vector, vector)
    in_specs = (tokens, P(("rep", "fsdp")), *weights, tokens)
    out_specs = (tokens, tokens, *weights)

    def step(*arrays):
        return shards(sizes, *arrays)

    return jax.shard_map(step, mesh=mesh, in_specs=in_specs, out_specs=out_specs, check_vma=False)
```

time: 830 us -> 806 us (0.971)
  Pallas kernels: 52.1 us -> 116 us
  local copies, waits for them, and re-layouts: 136 us -> 87 us
  blocking collectives: 0 us -> 27.1 us
  waiting for transfers between devices: 334 us -> 308 us
  other arithmetic: 62.7 us -> 36.9 us
    ppermute x62 -> x29, waiting for transfers between devices: 159 us -> 58.8 us  [over(): return lax.ppermute(x, 'ctx', [(i, i ^ d) for i in range(4)])]
    pallas_call x2 -> x16, Pallas kernels: 52.1 us -> 116 us  [the longest x2 34.8 us: attention_backward(): pl.pallas_call(kernel, out_shape=jax.ShapeDtypeStruct(qkv.shape, BF), gri...]
    all_gather x4 -> x3, waiting for transfers between devices: 0.01 us -> 34.4 us  [the longest x1 24.4 us: shards(): lax.all_gather(jnp.concatenate([half_rows(dense_weight), low, small]), 'f...]
    reduce_scatter x3, waiting for transfers between devices: 33.5 us -> 0.01 us  [the longest x2 0.01 us: shards(): lax.psum_scatter(a, 'fsdp', scatter_dimension=0, tiled=True)]
    ppermute x3, waiting for transfers between devices: 1.1 us -> 33.4 us  [scatter_shifts(): lax.ppermute(mine, axis, [(i, (i + s) % size) for i in range(size)])]
    all_to_all x0 -> x1, blocking collectives: none -> 27.1 us  [shards(): lax.all_to_all(a.reshape(C, B, -1), 'ctx', 0, 0, tiled=True)]
    all_to_all x0 -> x5, waiting for transfers between devices: none -> 26.3 us  [the longest x2 16.3 us: swap(): return lax.all_to_all(parts, self.axes, 0, 0, tiled=True)]
    all_to_all x0 -> x5, starting transfers between devices: none -> 20.5 us  [the longest x2 8.5 us: swap(): return lax.all_to_all(parts, self.axes, 0, 0, tiled=True)]
  transfers between devices with their start and end apart: 116 -> 66, of which waited for: 60 -> 33; matrix products, arithmetic and copies ran while one was open for 33% -> 23% of each run, Pallas kernels for 6% -> 14%
where the time goes in v3:
time: 806 us; the launch traced here: 799 us
  waiting for transfers between devices  308 us (38%)
  matrix products  132 us (16%)
  Pallas kernels  116 us (14%)
  local copies, waits for them, and re-layouts  87 us (11%)
  starting transfers between devices  75.7 us (9%)
  other arithmetic  36.9 us (5%)
  blocking collectives  27.1 us (3%)
  between operations  16.5 us (2%)
    dot_general x26, matrix products, dot(): lax.dot_general(a, b, (((ca,), (cb,)), ((), ())), preferred_element_type=...  132 us
    ppermute x17, waiting for transfers between devices, x(): return lax.ppermute(x, 'rep', [(0, 1), (1, 0)])  127 us
    unnamed x167, local copies, waits for them, and re-layouts  60.1 us
    ppermute x29, waiting for transfers between devices, over(): return lax.ppermute(x, 'ctx', [(i, i ^ d) for i in range(4)])  58.8 us
    pallas_call x2, Pallas kernels, attention_backward(): pl.pallas_call(kernel, out_shape=jax.ShapeDtypeStruct(qkv.shape, BF), gri...  34.8 us
    ppermute x3, waiting for transfers between devices, scatter_shifts(): lax.ppermute(mine, axis, [(i, (i + s) % size) for i in range(size)])  33.4 us
    ppermute x5, waiting for transfers between devices, over_rep(): return lax.ppermute(x, 'rep', [(0, 1), (1, 0)])  27.9 us
    all_to_all x1, blocking collectives, shards(): lax.all_to_all(a.reshape(C, B, -1), 'ctx', 0, 0, tiled=True)  27.1 us
  transfers between devices with their start and end apart: 66, of which 33 were waited for; matrix products, arithmetic and copies ran while one was open for 23% of the time, Pallas kernels for 14%

profile of v3, /device:TPU:0, one launch (start us, length us, event | category | flops | bytes accessed | tf_op | source)
XLA Modules:
  0.0 799.2 jit_solution(9677392507765723994)
XLA Ops:
  21.3 12.3 %collective-permute-done.2 = bf16[256,2048]{1,0:T(8,128)(2,1)S(1)} collective-permute-done((bf16[256,2048]{1,0:T(8,128)(2,1)}, bf16[256,2048]{1,0:T(8,128)(2,1)S(1)}, u32[]{:S(2)}, u32[]{:S(2)}) %collective-permute-start.2) | collective-permute-done | bytes 1048608 | tf_op jit(solution)/shard_map/ppermute | solution.py:560
  36.6 9.6 %collective-permute-done.1 = bf16[256,2048]{1,0:T(8,128)(2,1)S(1)} collective-permute-done((bf16[256,2048]{1,0:T(8,128)(2,1)}, bf16[256,2048]{1,0:T(8,128)(2,1)S(1)}, u32[]{:S(2)}, u32[]{:S(2)}) %collective-permute-start.1) | collective-permute-done | bytes 1048608 | tf_op jit(solution)/shard_map/ppermute | solution.py:557
  63.7 24.4 %all-gather.8.cloned.1.call-done = bf16[832,2048]{1,0:T(8,128)(2,1)} async-done(((bf16[208,2048]{1,0:T(8,128)(2,1)}), bf16[832,2048]{1,0:T(8,128)(2,1)}) %all-gather.8.cloned.1.call-update) | async-done | bytes 3407888 | tf_op jit(solution)/shard_map/all_gather | solution.py:683
  114.5 21.6 %collective-permute-done.9 = bf16[256,2048]{1,0:T(8,128)(2,1)S(1)} collective-permute-done((bf16[256,2048]{1,0:T(8,128)(2,1)}, bf16[256,2048]{1,0:T(8,128)(2,1)S(1)}, u32[]{:S(2)}, u32[]{:S(2)}) %collective-permute-start.9) | collective-permute-done | bytes 1048608 | tf_op jit(solution)/shard_map/ppermute | solution.py:560
  159.4 19.9 %collective-permute-done.13 = bf16[256,2048]{1,0:T(8,128)(2,1)} collective-permute-done((bf16[256,2048]{1,0:T(8,128)(2,1)S(1)}, bf16[256,2048]{1,0:T(8,128)(2,1)}, u32[]{:S(2)}, u32[]{:S(2)}) %collective-permute-start.13) | collective-permute-done | bytes 1048608 | tf_op jit(solution)/shard_map/ppermute | solution.py:560
  213.7 20.3 %shard_map.274 = bf16[2,4,256,256]{3,2,1,0:T(8,128)(2,1)S(1)} custom-call(s32[3,4]{1,0:T(4,128)S(1)} %add_add_fusion.1.order_ref.a, s32[2]{0:T(128)S(1)} %pad_add_fusion.prefix_ref.b, f32[4]{0:T(128)S(1)} %fusion.84.slope_ref, bf16[2,2,2,256,768]{4,3,2,1,0:T(8,128)(2,1)S(1)} %pad_maximum_fusion.qkv_ref.d), custom_call_target="tpu_custom_call" | custom-call | flops 1 | bytes 1 | tf_op jit(solution)/shard_map/pallas_call | solution.py:97
  239.4 14.2 %all-to-all-done.1.o_ref = bf16[8,256,256]{2,1,0:T(8,128)(2,1)} async-done(((bf16[8,256,256]{2,1,0:T(8,128)(2,1)}), bf16[8,256,256]{2,1,0:T(8,128)(2,1)}, u32[]{:S(2)}, u32[]{:S(2)}) %all-to-all-start.1) | async-done | bytes 1048608 | tf_op jit(solution)/shard_map/all_to_all | solution.py:534
  254.9 10.4 %shard_map.275 = (f32[256,2048]{1,0:T(8,128)S(1)}, bf16[256,2048]{1,0:T(8,128)(2,1)S(1)}) custom-call(s32[8]{0:T(128)S(1)} %fusion.31.table_ref, bf16[8,256,256]{2,1,0:T(8,128)(2,1)} %all-to-all-done.1.o_ref, bf16[4,256,2048]{2,1,0:T(8,128)(2,1)} %bitcast.20.w_ref, bf16[4,256,2048]{2,1,0:T(8,128)(2,1)} %bitcast.21.v_ref, bf16[256,2048]{1,0:T(8,128)(2,1)S(1)} %bitcast.159, ...), custom_call_target="tpu_custom_call" | custom-call | flops 1 | bytes 1 | tf_op jit(solution)/shard_map/pallas_call | solution.py:278
  267.3 22.7 %collective-permute-done.19 = bf16[256,2048]{1,0:T(8,128)(2,1)S(1)} collective-permute-done((bf16[256,2048]{1,0:T(8,128)(2,1)S(1)}, bf16[256,2048]{1,0:T(8,128)(2,1)S(1)}, u32[]{:S(2)}, u32[]{:S(2)}) %collective-permute-start.19) | collective-permute-done | bytes 1048608 | tf_op jit(solution)/shard_map/ppermute | solution.py:560
  306.1 10.0 %all-gather.10.cloned.1.call-done = bf16[3072,1024]{1,0:T(8,128)(2,1)} async-done(((bf16[768,1024]{1,0:T(8,128)(2,1)}), bf16[3072,1024]{1,0:T(8,128)(2,1)}) %all-gather.10.cloned.1.call-update) | async-done | bytes 6291472 | tf_op jit(solution)/shard_map/all_gather | solution.py:700
  329.4 10.7 %multiply_convert_fusion.3 = (bf16[1024,1024]{1,0:T(8,128)(2,1)S(1)}, bf16[1024,1024]{1,0:T(8,128)(2,1)}, bf16[1024,1024]{1,0:T(8,128)(2,1)}, bf16[1024,1024]{1,0:T(8,128)(2,1)S(1)}) fusion(f32[1024]{0:T(1024)S(1)} %bitcast.202, f32[1024,1024]{1,0:T(8,128)S(1)} %fusion.45, bf16[1024,2048]{1,0:T(8,128)(2,1)} %constant_dynamic-update-slice_fusion.15, ...), kind=kOutput, calls=%fused_computation.17 | convolution fusion | flops 4320133120 | bytes 20975616 | tf_op jit(solution)/shard_map/dot_general | solution.py:19
  348.1 8.7 %add_convert_fusion.1 = bf16[1024,2048]{1,0:T(8,128)(2,1)} fusion(f32[1024,2048]{1,0:T(8,128)S(1)} %fusion.46, bf16[1024,1024]{1,0:T(8,128)(2,1)S(1)} %get-tuple-element.156, bf16[1024,2048]{1,0:T(8,128)(2,1)} %constant_dynamic-update-slice_fusion.10), kind=kOutput, calls=%fused_computation.4 | convolution fusion | flops 4299161600 | bytes 18874368 | tf_op jit(solution)/shard_map/dot_general | solution.py:19
  356.8 8.7 %multiply_convert_fusion = bf16[1024,1024]{1,0:T(8,128)(2,1)S(1)} fusion(bf16[1024,1024]{1,0:T(8,128)(2,1)} %get-tuple-element.113, bf16[1024,2048]{1,0:T(8,128)(2,1)} %collective-permute-done.16, bf16[1024,2048]{1,0:T(8,128)(2,1)} %copy-done.45), kind=kOutput, calls=%fused_computation.14 | convolution fusion | flops 4298113024 | bytes 12582912 | tf_op jit(solution)/shard_map/dot_general | solution.py:19
  408.6 8.7 %add_convert_fusion = bf16[2048,1024]{1,0:T(8,128)(2,1)} fusion(f32[2048,1024]{1,0:T(8,128)S(1)} %fusion.47, bf16[1024,2048]{1,0:T(8,128)(2,1)} %constant_dynamic-update-slice_fusion.15, bf16[1024,1024]{1,0:T(8,128)(2,1)S(1)} %multiply_convert_fusion.1), kind=kOutput, calls=%fused_computation.3 | convolution fusion | flops 4299161600 | bytes 18874368 | tf_op jit(solution)/shard_map/dot_general | solution.py:19
  426.9 14.5 %shard_map.277 = (f32[256,2048]{1,0:T(8,128)}, bf16[256,2048]{1,0:T(8,128)(2,1)S(1)}, f32[4,2048]{1,0:T(4,128)S(1)}, bf16[8,256,256]{2,1,0:T(8,128)(2,1)S(1)}) custom-call(s32[8]{0:T(128)S(1)} %fusion.31.table_ref, f32[256,2048]{1,0:T(8,128)} %slice.344.a_ref, bf16[256,2048]{1,0:T(8,128)(2,1)} %collective-permute-done.27.b_ref, ...), custom_call_target="tpu_custom_call" | custom-call | flops 1 | bytes 1 | tf_op jit(solution)/shard_map/pallas_call | solution.py:331
  467.9 17.4 %shard_map.279._ = bf16[2,2,2,256,768]{4,3,2,1,0:T(8,128)(2,1)S(1)} custom-call(s32[3,4]{1,0:T(4,128)S(1)} %add_add_fusion.1.order_ref.a, s32[2]{0:T(128)S(1)} %pad_add_fusion.prefix_ref.b, f32[2]{0:T(128)S(1)} %get-tuple-element.230.slope_ref, bf16[2,2,2,256,768]{4,3,2,1,0:T(8,128)(2,1)S(1)} %pad_maximum_fusion.qkv_ref.d, ...), custom_call_target="tpu_custom_call" | custom-call | flops 1 | bytes 1 | tf_op jit(solution)/shard_map/pallas_call | solution.py:115
  500.6 17.5 %shard_map.280 = bf16[2,2,2,256,768]{4,3,2,1,0:T(8,128)(2,1)S(1)} custom-call(s32[3,4]{1,0:T(4,128)S(1)} %add_add_fusion.1.order_ref.a, s32[2]{0:T(128)S(1)} %pad_add_fusion.prefix_ref.b, f32[2]{0:T(128)S(1)} %get-tuple-element.231.c, bf16[2,2,2,256,768]{4,3,2,1,0:T(8,128)(2,1)S(1)} %pad_maximum_fusion.qkv_ref.d, ...), custom_call_target="tpu_custom_call", output_to_operand_aliasing={{}: (5, {})} | custom-call | flops 1 | bytes 1 | tf_op jit(solution)/shard_map/pallas_call | solution.py:115
  584.2 10.0 %all-to-all-done.3.own_ref = bf16[4,128,1024]{2,1,0:T(8,128)(2,1)} async-done(((bf16[4,128,1024]{2,1,0:T(8,128)(2,1)}), bf16[4,128,1024]{2,1,0:T(8,128)(2,1)}, u32[]{:S(2)}, u32[]{:S(2)}) %all-to-all-start.3) | async-done | bytes 1048608 | tf_op jit(solution)/shard_map/all_to_all | solution.py:796
  608.9 14.3 %collective-permute-done.43 = bf16[64,2048]{1,0:T(8,128)(2,1)S(1)} collective-permute-done((bf16[64,2048]{1,0:T(8,128)(2,1)S(1)}, bf16[64,2048]{1,0:T(8,128)(2,1)S(1)}, u32[]{:S(2)}, u32[]{:S(2)}) %collective-permute-start.43) | collective-permute-done | bytes 262176 | tf_op jit(solution)/shard_map/ppermute | solution.py:623
  624.6 19.1 %collective-permute-done.42 = bf16[64,2048]{1,0:T(8,128)(2,1)S(1)} collective-permute-done((bf16[64,2048]{1,0:T(8,128)(2,1)S(1)}, bf16[64,2048]{1,0:T(8,128)(2,1)S(1)}, u32[]{:S(2)}, u32[]{:S(2)}) %collective-permute-start.42) | collective-permute-done | bytes 262176 | tf_op jit(solution)/shard_map/ppermute | solution.py:623
  664.2 16.7 %collective-permute-done.48.other_ref = bf16[4,128,1024]{2,1,0:T(8,128)(2,1)S(1)} collective-permute-done((bf16[4,128,1024]{2,1,0:T(8,128)(2,1)}, bf16[4,128,1024]{2,1,0:T(8,128)(2,1)S(1)}, u32[]{:S(2)}, u32[]{:S(2)}) %collective-permute-start.48) | collective-permute-done | bytes 1048608 | tf_op jit(solution)/shard_map/ppermute | solution.py:672
  681.0 14.2 %collective-permute-done.46 = bf16[128,2048]{1,0:T(8,128)(2,1)S(1)} collective-permute-done((bf16[128,2048]{1,0:T(8,128)(2,1)S(1)}, bf16[128,2048]{1,0:T(8,128)(2,1)S(1)}, u32[]{:S(2)}, u32[]{:S(2)}) %collective-permute-start.46) | collective-permute-done | bytes 524320 | tf_op jit(solution)/shard_map/ppermute | solution.py:557
  695.1 18.7 %collective-permute-done.47 = bf16[128,2048]{1,0:T(8,128)(2,1)S(1)} collective-permute-done((bf16[128,2048]{1,0:T(8,128)(2,1)S(1)}, bf16[128,2048]{1,0:T(8,128)(2,1)S(1)}, u32[]{:S(2)}, u32[]{:S(2)}) %collective-permute-start.47) | collective-permute-done | bytes 524320 | tf_op jit(solution)/shard_map/ppermute | solution.py:560
  720.4 27.1 %all_to_all.30 = bf16[4,128,384]{2,1,0:T(8,128)(2,1)} all-to-all(bf16[4,128,384]{2,1,0:T(8,128)(2,1)} %bitcast.192), channel_id=1, replica_groups=mesh['rep'=2,'fsdp'=4,'ctx'=4] {'ctx'}, dimensions={0} | all-to-all | bytes 786432 | tf_op jit(solution)/shard_map/all_to_all | solution.py:825
  (459 shorter events, 411.3 us)
Async XLA Ops:
  7.2 80.9 %all-gather.8.cloned.1.call-start = ((), (), s32[]{:S(2)}) async-start(), calls=%async_computation.15 | async-start | bytes 4259840 | tf_op jit(solution)/shard_map/all_gather | solution.py:683
  58.2 45.3 %collective-permute-start.7 = (bf16[1024,2048]{1,0:T(8,128)(2,1)}, bf16[1024,2048]{1,0:T(8,128)(2,1)}, u32[]{:S(2)}, u32[]{:S(2)}) collective-permute-start(bf16[1024,2048]{1,0:T(8,128)(2,1)} %constant_dynamic-update-slice_fusion.x_ref), channel_id=1, source_target_pairs={{0,1},{1,0},{2,3},{3,2},{4,5},{5,4},{6,7},{7,6},{8,9},{9,8},{10,11... | collective-permute-start | bytes 12582920 | tf_op jit(solution)/shard_map/ppermute | solution.py:557
  60.0 53.3 %all-to-all-start = ((bf16[4,128,1792]{2,1,0:T(8,128)(2,1)}), bf16[4,128,1792]{2,1,0:T(8,128)(2,1)S(1)}, u32[]{:S(2)}, u32[]{:S(2)}) async-start(bf16[4,128,1792]{2,1,0:T(8,128)(2,1)} %shard_map.273), calls=%async_computation | async-start | bytes 3670016 | tf_op jit(solution)/shard_map/all_to_all | solution.py:686
  63.6 139.6 %all-gather.6.cloned.1.call-start = ((), (), s32[]{:S(2)}) async-start(), calls=%async_computation.10 | async-start | bytes 3932160 | tf_op jit(solution)/shard_map/all_gather | solution.py:669
  114.3 201.9 %all-gather.10.cloned.1.call-start = ((), (), s32[]{:S(2)}) async-start(), calls=%async_computation.16 | async-start | bytes 7864320 | tf_op jit(solution)/shard_map/all_gather | solution.py:700
  158.1 42.5 %collective-permute-start = (s32[1]{0:T(128)}, s32[1]{0:T(128)}, u32[]{:S(2)}, u32[]{:S(2)}) collective-permute-start(s32[1]{0:T(128)} %param.17), channel_id=1, source_target_pairs={{0,16},{16,0},{1,17},{17,1},{2,18},{18,2},{3,19},{19,3},{4,20},{20... | collective-permute-start | bytes 20 | tf_op jit(solution)/shard_map/ppermute | solution.py:560
  183.1 70.5 %collective-permute-start.17 = (bf16[1024,2048]{1,0:T(8,128)(2,1)}, bf16[1024,2048]{1,0:T(8,128)(2,1)}, u32[]{:S(2)}, u32[]{:S(2)}) collective-permute-start(bf16[1024,2048]{1,0:T(8,128)(2,1)} %constant_dynamic-update-slice_fusion.5), channel_id=1, source_target_pairs={{0,1},{1,0},{2,3},{3,2},{4,5},{5,4},{6,7},{7,6},{8,9},{9,8},{10,11... | collective-permute-start | bytes 12582920 | tf_op jit(solution)/shard_map/ppermute | solution.py:557
  199.4 54.2 %collective-permute-start.16 = (bf16[1024,2048]{1,0:T(8,128)(2,1)}, bf16[1024,2048]{1,0:T(8,128)(2,1)}, u32[]{:S(2)}, u32[]{:S(2)}) collective-permute-start(bf16[1024,2048]{1,0:T(8,128)(2,1)} %constant_dynamic-update-slice_fusion.10), channel_id=1, source_target_pairs={{0,1},{1,0},{2,3},{3,2},{4,5},{5,4},{6,7},{7,6},{8,9},{9,8},{10,11... | collective-permute-start | bytes 12582920 | tf_op jit(solution)/shard_map/ppermute | solution.py:557
  239.2 204.2 %reduce-scatter.5.cloned.1.call-start = ((), (), s32[]{:S(2)}) async-start(), calls=%async_computation.11 | async-start | bytes 5242880 | tf_op jit(solution)/shard_map/reduce_scatter | solution.py:747
  447.7 96.7 %reduce-scatter.7.cloned.1.call-start = ((), (), s32[]{:S(2)}) async-start(), calls=%async_computation.12 | async-start | bytes 5242880 | tf_op jit(solution)/shard_map/reduce_scatter | solution.py:757
  462.1 258.2 %reduce-scatter.9.cloned.1.call-start = ((), (), s32[]{:S(2)}) async-start(), calls=%async_computation.13 | async-start | bytes 1966080 | tf_op jit(solution)/shard_map/reduce_scatter | solution.py:795
  466.4 78.0 %collective-permute-start.34 = (bf16[256,2048]{1,0:T(8,128)(2,1)}, bf16[256,2048]{1,0:T(8,128)(2,1)}, u32[]{:S(2)}, u32[]{:S(2)}) collective-permute-start(bf16[256,2048]{1,0:T(8,128)(2,1)} %reduce-scatter.5.cloned.1.call-done.own_ref), channel_id=1, source_target_pairs={{0,16},{16,0},{1,17},{17,1},{2,18},{18,2},{3,19},{19,3},{4,20},{20... | collective-permute-start | bytes 3145736 | tf_op jit(solution)/shard_map/ppermute | solution.py:672
  559.3 34.8 %all-to-all-start.3 = ((bf16[4,128,1024]{2,1,0:T(8,128)(2,1)}), bf16[4,128,1024]{2,1,0:T(8,128)(2,1)}, u32[]{:S(2)}, u32[]{:S(2)}) async-start(bf16[4,128,1024]{2,1,0:T(8,128)(2,1)} %bitcast.190), calls=%async_computation.5 | async-start | bytes 2097152 | tf_op jit(solution)/shard_map/all_to_all | solution.py:796
  563.6 183.8 %reduce-scatter.11.cloned.1.call-start = ((), (), s32[]{:S(2)}) async-start(), calls=%async_computation.14 | async-start | bytes 2621440 | tf_op jit(solution)/shard_map/reduce_scatter | solution.py:795
  599.2 46.7 %collective-permute-start.39 = (bf16[512,2048]{1,0:T(8,128)(2,1)S(1)}, bf16[512,2048]{1,0:T(8,128)(2,1)S(1)}, u32[]{:S(2)}, u32[]{:S(2)}) collective-permute-start(bf16[512,2048]{1,0:T(8,128)(2,1)S(1)} %convolution_convert_fusion.1), channel_id=1, source_target_pairs={{0,1},{1,0},{2,3},{3,2},{4,5},{5,4},{6,7},{7,6},{8,9},{9,8},{10,11... | collective-permute-start | bytes 6291464 | tf_op jit(solution)/shard_map/ppermute | solution.py:557
  601.6 46.6 %collective-permute-start.40 = (bf16[512,2048]{1,0:T(8,128)(2,1)S(1)}, bf16[512,2048]{1,0:T(8,128)(2,1)S(1)}, u32[]{:S(2)}, u32[]{:S(2)}) collective-permute-start(bf16[512,2048]{1,0:T(8,128)(2,1)S(1)} %convolution_convert_fusion), channel_id=1, source_target_pairs={{0,1},{1,0},{2,3},{3,2},{4,5},{5,4},{6,7},{7,6},{8,9},{9,8},{10,11... | collective-permute-start | bytes 6291464 | tf_op jit(solution)/shard_map/ppermute | solution.py:557
  605.8 37.9 %collective-permute-start.42 = (bf16[64,2048]{1,0:T(8,128)(2,1)S(1)}, bf16[64,2048]{1,0:T(8,128)(2,1)S(1)}, u32[]{:S(2)}, u32[]{:S(2)}) collective-permute-start(bf16[64,2048]{1,0:T(8,128)(2,1)S(1)} %get-tuple-element.213), channel_id=1, source_target_pairs={{0,8},{4,12},{8,0},{12,4},{1,9},{5,13},{9,1},{13,5},{2,10},{6,14},... | collective-permute-start | bytes 786440 | tf_op jit(solution)/shard_map/ppermute | solution.py:623
  606.7 38.5 %collective-permute-start.41 = (bf16[64,2048]{1,0:T(8,128)(2,1)S(1)}, bf16[64,2048]{1,0:T(8,128)(2,1)S(1)}, u32[]{:S(2)}, u32[]{:S(2)}) collective-permute-start(bf16[64,2048]{1,0:T(8,128)(2,1)S(1)} %get-tuple-element.211), channel_id=1, source_target_pairs={{0,4},{4,8},{8,12},{12,0},{1,5},{5,9},{9,13},{13,1},{2,6},{6,10},{... | collective-permute-start | bytes 786440 | tf_op jit(solution)/shard_map/ppermute | solution.py:623
  645.2 35.8 %collective-permute-start.48 = (bf16[4,128,1024]{2,1,0:T(8,128)(2,1)}, bf16[4,128,1024]{2,1,0:T(8,128)(2,1)S(1)}, u32[]{:S(2)}, u32[]{:S(2)}) collective-permute-start(bf16[4,128,1024]{2,1,0:T(8,128)(2,1)} %all-to-all-done.3.own_ref), channel_id=1, source_target_pairs={{0,16},{16,0},{1,17},{17,1},{2,18},{18,2},{3,19},{19,3},{4,20},{20... | collective-permute-start | bytes 3145736 | tf_op jit(solution)/shard_map/ppermute | solution.py:672
  658.8 55.0 %collective-permute-start.44 = (bf16[256,2048]{1,0:T(8,128)(2,1)S(1)}, bf16[256,2048]{1,0:T(8,128)(2,1)S(1)}, u32[]{:S(2)}, u32[]{:S(2)}) collective-permute-start(bf16[256,2048]{1,0:T(8,128)(2,1)S(1)} %pad_maximum_fusion.6), channel_id=1, source_target_pairs={{0,16},{16,0},{1,17},{17,1},{2,18},{18,2},{3,19},{19,3},{4,20},{20... | collective-permute-start | bytes 3145736 | tf_op jit(solution)/shard_map/ppermute | solution.py:560
  660.7 54.1 %collective-permute-start.45 = (bf16[256,2048]{1,0:T(8,128)(2,1)S(1)}, bf16[256,2048]{1,0:T(8,128)(2,1)S(1)}, u32[]{:S(2)}, u32[]{:S(2)}) collective-permute-start(bf16[256,2048]{1,0:T(8,128)(2,1)S(1)} %pad_maximum_fusion.7), channel_id=1, source_target_pairs={{0,2},{1,3},{2,0},{3,1},{4,6},{5,7},{6,4},{7,5},{8,10},{9,11},{10,... | collective-permute-start | bytes 3145736 | tf_op jit(solution)/shard_map/ppermute | solution.py:557
  663.3 50.5 %collective-permute-start.47 = (bf16[128,2048]{1,0:T(8,128)(2,1)S(1)}, bf16[128,2048]{1,0:T(8,128)(2,1)S(1)}, u32[]{:S(2)}, u32[]{:S(2)}) collective-permute-start(bf16[128,2048]{1,0:T(8,128)(2,1)S(1)} %get-tuple-element.201), channel_id=1, source_target_pairs={{0,16},{16,0},{1,17},{17,1},{2,18},{18,2},{3,19},{19,3},{4,20},{20... | collective-permute-start | bytes 1572872 | tf_op jit(solution)/shard_map/ppermute | solution.py:560
  716.1 59.1 %collective-permute-start.49 = (bf16[256,2048]{1,0:T(8,128)(2,1)}, bf16[256,2048]{1,0:T(8,128)(2,1)}, u32[]{:S(2)}, u32[]{:S(2)}) collective-permute-start(bf16[256,2048]{1,0:T(8,128)(2,1)} %pad_maximum_fusion.8), channel_id=1, source_target_pairs={{0,16},{16,0},{1,17},{17,1},{2,18},{18,2},{3,19},{19,3},{4,20},{20... | collective-permute-start | bytes 3145736 | tf_op jit(solution)/shard_map/ppermute | solution.py:560
  718.9 56.4 %collective-permute-start.50 = (bf16[256,2048]{1,0:T(8,128)(2,1)}, bf16[256,2048]{1,0:T(8,128)(2,1)}, u32[]{:S(2)}, u32[]{:S(2)}) collective-permute-start(bf16[256,2048]{1,0:T(8,128)(2,1)} %pad_maximum_fusion.9), channel_id=1, source_target_pairs={{0,2},{1,3},{2,0},{3,1},{4,6},{5,7},{6,4},{7,5},{8,10},{9,11},{10,... | collective-permute-start | bytes 3145736 | tf_op jit(solution)/shard_map/ppermute | solution.py:557
  (114 other events, 1522.4 us)
Sparse Core Ops, SparseCore 0:
  19.9 68.1 all-gather.7
  114.4 60.2 all-gather.5
  202.9 113.2 all-gather.9
  356.9 74.9 reduce-scatter.4
  462.3 74.3 reduce-scatter.6
  544.5 32.8 reduce-scatter.8
  579.6 54.5 reduce-scatter.10

commit v4 on v3

--- a/solution.py
+++ b/solution.py
@@ -19,13 +19,21 @@
     return lax.dot_general(a, b, (((ca,), (cb,)), ((), ())), preferred_element_type=F32)
 
 
-def head_probs(query, key, slope, place, prefix, lanes):
+def places(c, n, T, prefix):
+    before = lax.broadcasted_iota(jnp.int32, (1, c * T), 1).astype(F32) - c * T if c else None
+    row = lax.broadcasted_iota(jnp.int32, (T, (n - c) * T), 0)
+    column = lax.broadcasted_iota(jnp.int32, (T, (n - c) * T), 1)
+    allowed = column <= jnp.maximum(row, prefix - 1 - c * T)
+    return before, jnp.minimum(column, 2 * row - column).astype(F32), allowed
+
+
+def head_probs(query, key, slope, place, lanes):
+    before, near, allowed = place
     raw = dot(jnp.where(lanes, query, jnp.zeros_like(query)), key, 1, 1)
-    row = place + lax.broadcasted_iota(jnp.int32, raw.shape, 0)
-    column = lax.broadcasted_iota(jnp.int32, raw.shape, 1)
-    distance = jnp.abs(row - column).astype(F32)
-    allowed = column <= jnp.maximum(row, prefix - 1)
-    logits = jnp.where(allowed, raw - slope * distance, -1e30)
+    split = raw.shape[1] - near.shape[1]
+    logits = jnp.where(allowed, raw[:, split:] + slope * near, -1e30)
+    if split:
+        logits = jnp.concatenate([raw[:, :split] + slope * before, logits], axis=1)
     largest = jnp.max(logits, axis=-1, keepdims=True)
     exponent = jnp.exp(logits - largest)
     return exponent * (1.0 / jnp.sum(exponent, axis=-1, keepdims=True))
@@ -36,7 +44,6 @@
     seq, pair = pl.program_id(0), pl.program_id(1)
     at = lambda part: slice(part * 128, part * 128 + 128)
     first = lax.broadcasted_iota(jnp.int32, (T, 128), 1) < HD
-    prefix = prefix_ref[seq]
     key = [qkv_ref[order_ref[0, c], 0, order_ref[1, c], :, at(1)] for c in range(C)]
     value = [qkv_ref[order_ref[0, c], 0, order_ref[1, c], :, at(2)] for c in range(C)]
     for c in range(C):
@@ -44,9 +51,10 @@
         keys = jnp.concatenate(key[:n], axis=0)
         values = jnp.concatenate(value[:n], axis=0)
         query = qkv_ref[order_ref[0, c], 0, order_ref[1, c], :, at(0)] * 0.125
+        place = places(c, n, T, prefix_ref[seq])
         out = []
         for h in range(2):
-            probs = head_probs(query, keys, slope_ref[2 * pair + h], c * T, prefix, first if h == 0 else ~first)
+            probs = head_probs(query, keys, slope_ref[2 * pair + h], place, first if h == 0 else ~first)
             out.append(dot(probs.astype(BF), values, 1, 0))
         out_ref[0, c] = jnp.where(first, out[0], out[1]).astype(BF)
 
@@ -56,7 +64,6 @@
     seq, pair = pl.program_id(0), pl.program_id(1)
     at = lambda part: slice(part * 128, part * 128 + 128)
     first = lax.broadcasted_iota(jnp.int32, (T, 128), 1) < HD
-    prefix = prefix_ref[seq]
     d_key[...] = jnp.zeros_like(d_key)
     d_value[...] = jnp.zeros_like(d_value)
     key = [qkv_ref[order_ref[0, c], 0, order_ref[1, c], :, at(1)] for c in range(C)]
@@ -67,10 +74,11 @@
         values = jnp.concatenate(value[:n], axis=0)
         query = qkv_ref[order_ref[0, c], 0, order_ref[1, c], :, at(0)]
         d_out = d_out_ref[0, c]
+        place = places(c, n, T, prefix_ref[seq])
         d_query = []
         for h in range(2):
             lanes = first if h == 0 else ~first
-            probs = head_probs(query * 0.125, keys, slope_ref[2 * pair + h], c * T, prefix, lanes)
+            probs = head_probs(query * 0.125, keys, slope_ref[2 * pair + h], place, lanes)
             mine = jnp.where(lanes, d_out, jnp.zeros_like(d_out))
             d_probs = dot(mine, values, 1, 1)
             weighted = jnp.sum(probs * d_probs, axis=-1, keepdims=True)
@@ -99,7 +107,7 @@
         out_shape=jax.ShapeDtypeStruct((n, C, T, pairs * 128), BF),
         grid_spec=pltpu.PrefetchScalarGridSpec(num_scalar_prefetch=3, grid=(n, pairs), in_specs=[near], out_specs=true),
         compiler_params=vmem(32),
-        cost_estimate=CHEAP,
+        cost_estimate=pl.CostEstimate(flops=12 * 10**9, transcendentals=0, bytes_accessed=1),
     )(order, prefix, slopes, qkv)
 
 
@@ -124,7 +132,7 @@
         ),
         input_output_aliases=aliases,
         compiler_params=vmem(32),
-        cost_estimate=CHEAP,
+        cost_estimate=pl.CostEstimate(flops=12 * 10**9, transcendentals=0, bytes_accessed=1),
     )(order, prefix, slopes, qkv, d_out, *more)
 
 
@@ -176,51 +184,42 @@
     )(rep.reshape(1), joined, expand)
 
 
-def unpack_joined_kernel(F, rep_ref, own_ref, other_ref, out_ref):
-    C, B = own_ref.shape[:2]
+def unpack_joined_kernel(F, ref, out_ref):
+    C, B = ref.shape[1:3]
     D = out_ref.shape[1] // 3
     first = lax.broadcasted_iota(jnp.int32, (B, 128), 1) < HD
-    swap = rep_ref[0] == 1
     for c in range(C):
         for p in range(F // 2):
             for q in range(3):
                 at = slice((p * 3 + q) * 128, (p * 3 + q + 1) * 128)
-                own, other = own_ref[c, :, at].astype(F32), other_ref[c, :, at].astype(F32)
-                one, two = jnp.where(swap, other, own), jnp.where(swap, own, other)
+                one, two = ref[0, c, :, at].astype(F32), ref[1, c, :, at].astype(F32)
                 for i, f in enumerate((2 * p, 2 * p + 1)):
-                    if i == 0:
-                        tile = jnp.where(first, one, half_turn(two))
-                    else:
-                        tile = jnp.where(first, half_turn(one), two)
+                    tile = jnp.where(first, half_turn(one) if i else one, two if i else half_turn(two))
                     out_ref[:, q * D + (f * C + c) * 128 : q * D + (f * C + c + 1) * 128] = tile
 
 
-def unpack_expand_kernel(F, rep_ref, own_ref, other_ref, out_ref):
-    C = own_ref.shape[0]
-    E = own_ref.shape[2] // F
+def unpack_expand_kernel(F, ref, out_ref):
+    C = ref.shape[1]
+    E = ref.shape[3] // F
     for c in range(C):
         for f in range(F):
-            at = (f * C + c) * 2 * E
-            mine = pl.multiple_of(at + rep_ref[0] * E, 128)
-            theirs = pl.multiple_of(at + (1 - rep_ref[0]) * E, 128)
-            out_ref[:, pl.ds(mine, E)] = own_ref[c, :, f * E : (f + 1) * E].astype(F32)
-            out_ref[:, pl.ds(theirs, E)] = other_ref[c, :, f * E : (f + 1) * E].astype(F32)
-
-
-def unpack(kernel, F, rep, own, other):
-    C, B, width = own.shape
+            for r in range(2):
+                at = ((f * C + c) * 2 + r) * E
+                out_ref[:, at : at + E] = ref[r, c, :, f * E : (f + 1) * E].astype(F32)
+
+
+def unpack(kernel, F, parts, extra=0):
+    R, C, B, width = parts.shape
+    width -= extra
     return pl.pallas_call(
         functools.partial(kernel, F),
-        out_shape=jax.ShapeDtypeStruct((B, 2 * C * width), F32),
-        grid_spec=pltpu.PrefetchScalarGridSpec(
-            num_scalar_prefetch=1,
-            grid=(1,),
-            in_specs=[whole(own.shape), whole(own.shape)],
-            out_specs=whole((B, 2 * C * width)),
-        ),
+        out_shape=jax.ShapeDtypeStruct((B, R * C * width), F32),
+        grid=(1,),
+        in_specs=[whole((R, C, B, width))],
+        out_specs=whole((B, R * C * width)),
         compiler_params=vmem(32),
         cost_estimate=CHEAP,
-    )(rep.reshape(1), own, other)
+    )(parts)
 
 
 def normed(values):
@@ -409,7 +408,7 @@
         in_specs=[full] * 5 + [whole((1, D))],
         out_specs=full,
         compiler_params=vmem(48),
-        cost_estimate=CHEAP,
+        cost_estimate=pl.CostEstimate(flops=4 * 10**9, transcendentals=0, bytes_accessed=1),
     )(*parts, x, d_mid, gain.reshape(1, D))
 
 
@@ -514,12 +513,15 @@
         self.order = jnp.stack([place * 0, place, place * 0])
         self.table = jnp.arange(self.N, dtype=jnp.int32)
 
-    def gather(self, x, beside=()):
-        out, beside = together(lax.all_gather(x, self.axes, axis=0, tiled=True), beside)
-        return [out], beside
-
-    def scatter_core(self, rows, part):
-        return part(0, 0, self.N * rows).astype(BF)
+    def gather(self, x):
+        return [lax.all_gather(x, self.axes, axis=0, tiled=True)]
+
+    def gather_two(self, x, g, ready):
+        return self.gather(x), self.gather(g), ready
+
+    def scatter_core(self, rows, part, ready=None):
+        out = part(0, 0, self.N * rows).astype(BF)
+        return out if ready is None else (out, ready)
 
     def scatter_far(self, state):
         return state
@@ -565,20 +567,35 @@
     def core(self, x):
         return self.over(x, 1)
 
-    def gather(self, x, beside=()):
+    def gather(self, x):
+        return self.gather_core(self.gather_far(x, self.x(x), self.y(x)))
+
+    def gather_far(self, x, from_x, from_y):
         half = x.shape[0] // 2
-        from_x, from_y = self.x(x), self.y(x)
-        if beside:
-            from_x, from_y, beside = together(from_x, from_y, beside)
-        own = jnp.concatenate([x, from_y, from_x, self.y(from_x[:half]), self.x(from_y[half:])], axis=0)
-        return [own, self.core(own)], beside
-
-    def scatter_core(self, rows, part):
+        return x, from_y, from_x, self.y(from_x[:half]), self.x(from_y[half:])
+
+    def gather_core(self, pieces):
+        own = jnp.concatenate(pieces, axis=0)
+        return [own, self.core(own)]
+
+    def gather_two(self, x, g, ready):
+        t = x.shape[0]
+        both = jnp.concatenate([x, g], axis=0)
+        from_x = self.x(both)
+        both, ready = together(both, ready)
+        from_y = self.y(both)
+        far_x, far_g = together(self.y(from_x[:t]), self.x(from_y[t:]))
+        x = jnp.concatenate([x, from_y[:t], from_x[:t], far_x], axis=0)
+        g = jnp.concatenate([g, from_y[t:], from_x[t:], far_g], axis=0)
+        return [x, self.core(x)], [g, self.core(g)], ready
+
+    def scatter_core(self, rows, part, ready=None):
         far_x = part(1, 2 * rows, 4 * rows).astype(BF)
         near_x = part(1, 0, 2 * rows).astype(BF)
+        far_x, near_x, halfway = together(far_x, near_x, () if ready is None else ready)
         far_x = part(0, 2 * rows, 4 * rows) + self.core(far_x).astype(F32)
         near_x = part(0, 0, 2 * rows) + self.core(near_x).astype(F32)
-        return far_x, near_x
+        return (far_x, near_x) if ready is None else ((far_x, near_x), halfway)
 
     def scatter_given(self, own, oth):
         total = (own.astype(F32) + self.core(oth).astype(F32)).astype(BF)
@@ -588,15 +605,16 @@
         far_x, near_x = state
         rows = far_x.shape[0] // 2
         far = far_x[rows:].astype(BF)
-        return far_x[:rows].astype(F32), near_x.astype(F32), self.y(far[: rows // 2]), self.x(far[rows // 2 :])
+        return far_x, near_x, self.y(far[: rows // 2]), self.x(far[rows // 2 :])
 
     def scatter_near(self, state):
-        by_x, near_x, to_y, to_x = state
-        rows = by_x.shape[0]
+        far_x, near_x, to_y, to_x = state
+        rows = far_x.shape[0] // 2
         half = rows // 2
+        by_x, near_y = far_x[:rows].astype(F32), near_x[rows:].astype(F32)
         by_x = jnp.concatenate([by_x[:half] + to_y.astype(F32), by_x[half:]], axis=0)
-        by_y = jnp.concatenate([near_x[rows : rows + half], near_x[rows + half :] + to_x.astype(F32)], axis=0)
-        return near_x[:rows], self.x(by_x.astype(BF)), self.y(by_y.astype(BF))
+        by_y = jnp.concatenate([near_y[:half], near_y[half:] + to_x.astype(F32)], axis=0)
+        return near_x, self.x(by_x.astype(BF)), self.y(by_y.astype(BF))
 
     def scatter_end(self, state):
         return state
@@ -612,7 +630,8 @@
 
 
 def added(parts):
-    return sum(a.astype(F32) for a in parts)
+    rows = parts[-1].shape[0]
+    return sum(a[:rows].astype(F32) for a in parts)
 
 
 def scatter_shifts(x, axis, size):
@@ -668,6 +687,10 @@
     def widen(blocks):
         return lax.all_gather(blocks.reshape(C * B, -1), "fsdp", axis=0, tiled=True)
 
+    def to_owners(part):
+        blocks = jnp.concatenate([part.reshape(C, B, -1)] * R)
+        return lax.all_to_all(blocks, ("rep", "ctx"), 0, 0, tiled=True).reshape(R, C, B, -1)
+
     def over_rep(x):
         return lax.ppermute(x, "rep", [(0, 1), (1, 0)])
 
@@ -694,16 +717,15 @@
         pieces = expand_weight.reshape(B, F, C, R, E)
         pieces = lax.dynamic_index_in_dim(pieces, rep, 3, keepdims=False).transpose(2, 0, 1, 3)
         expand_blocks = lax.all_to_all(pieces.reshape(C, B, F * E), "ctx", 0, 0, tiled=True)
+    x_all, g_all, (joined_blocks, expand_blocks) = tp.gather_two(x, g, (joined_blocks, expand_blocks))
     joined_cols = widen(joined_blocks)
     if near:
         late = jnp.concatenate([expand_blocks.reshape(C * B, -1), high[:, : D // 2], high[:, D // 2 :]])
         late = lax.all_gather(late, "fsdp", axis=0, tiled=False)
-        expand_cols, shrink_rows = part_weights(early, late, m, C * B)
     else:
         expand_cols = widen(expand_blocks)
         shrink_rows = lax.all_gather(half_rows(shrink_weight), "fsdp", axis=0, tiled=True)
     prefixes = tp.prefixes(prefix)
-    x_all, _ = tp.gather(x)
 
     small = small.astype(F32)
     gain_one, shift_one, gain_two, shift_two, dbias, sbias, qbias, vbias = [
@@ -722,56 +744,80 @@
     my_heads = my_features(jnp.repeat(jnp.arange(H, dtype=jnp.int32), HD)).reshape(-1, HD)[:, 0]
     slopes = jnp.exp2(-8.0 * (my_heads.astype(F32) + 1.0) / H)
 
+    if near:
+        own, dense_rows = together(x_all[0], dense_rows)
+        x_all[0] = own
     a1_all = [norm(a, gain_one, shift_one) for a in x_all]
     if near:
-        a1_all, dense_rows = together(a1_all, dense_rows)
-        dense_all, _ = tp.gather(dense_rows)
-        own, g = together(dense_all[0], g)
-        dense_all[0] = own
+        a1_all, joined_cols = together(a1_all, joined_cols)
     else:
         dense_all = [dense_rows[: D // 2], dense_rows[D // 2 :]]
-    g_all, _ = tp.gather(g)
     qkv_bias = jnp.stack([my_features(qbias), jnp.zeros((W,), F32), my_features(vbias)])
     qkv_bias = qkv_bias.reshape(3, pairs, 128).transpose(1, 0, 2).reshape(3 * W)
     qkv = jnp.stack([(dot(a, joined_cols, 1, 0) + qkv_bias).astype(BF) for a in a1_all])
     qkv = qkv.reshape(K, R, Y, t, 3 * W)
+    if near:
+        from_x, from_y, qkv = together(tp.x(dense_rows), tp.y(dense_rows), qkv)
+        dense_all = tp.gather_far(dense_rows, from_x, from_y)
     out = attention_forward(tp.order, prefixes, slopes, qkv)
+    out, g_all, dense_all = together(out, g_all, dense_all)
+    if near:
+        dense_all = tp.gather_core(dense_all)
     o = tp.swap(out.reshape(N, t, W))
-    o, g_all = together(o, g_all)
     midway, a2 = attended(tp.table, o, dense_all, x, dbias, gain_two, shift_two)
 
-    a2_all, _ = tp.gather(a2)
-    act, slope = zip(*[gelu_and_slope(dot(a, expand_cols, 1, 0) + ebias) for a in a2_all])
+    if near:
+        pieces, late = together(tp.gather_far(a2, tp.x(a2), tp.y(a2)), late)
+        a2_all = tp.gather_core(pieces)
+        expand_cols, shrink_rows = part_weights(early, late, m, C * B)
+    else:
+        a2_all = tp.gather(a2)
+    act, slope = [], []
+    for i in G:
+        got = gelu_and_slope(dot(a2_all[i], expand_cols, 1, 0) + ebias)
+        if i + 1 < K:
+            got, a2_all[i + 1] = together(got, a2_all[i + 1])
+        act.append(got[0])
+        slope.append(got[1])
     shrink_grad = sum(dot(act[i], g_all[i], 0, 0) for i in G).astype(BF)
     slope, shrink_grad, act = together(slope, shrink_grad, act)
     shrink_part = lax.psum_scatter(shrink_grad, "fsdp", scatter_dimension=0, tiled=True)
     d_exp = [(dot(g_all[i], shrink_rows, 1, 1) * slope[i].astype(F32)).astype(BF) for i in G]
 
     d_a2 = tp.scatter_core(t, lambda i, a, b: dot(d_exp[i][a:b], expand_cols, 1, 1))
-    d_a2, d_exp = together(tp.scatter_far(d_a2), d_exp)
+    d_a2, act = together(d_a2, act)
+    d_a2 = tp.scatter_far(d_a2)
+    branch = tp.scatter_core(t, lambda i, a, b: dot(act[i][a:b], shrink_rows, 1, 0))
+    d_a2, d_exp, branch = together(d_a2, d_exp, branch)
     d_a2 = tp.scatter_near(d_a2)
     expand_grad = sum(dot(a2_all[i], d_exp[i], 0, 0) for i in G).astype(BF)
-    d_a2, expand_grad = together(d_a2, expand_grad)
+    d_a2, expand_grad, branch = together(d_a2, expand_grad, branch)
+    expand_part = lax.psum_scatter(expand_grad, "fsdp", scatter_dimension=0, tiled=True)
+    branch = tp.scatter_far(branch)
     d_mid, d_att, sums_two, d_o = turned(tp.table, tp.scatter_end(d_a2), midway, g, gain_two, dense_all)
-    d_o, expand_grad, shrink_part = together(d_o, expand_grad, shrink_part)
-    expand_part = lax.psum_scatter(expand_grad, "fsdp", scatter_dimension=0, tiled=True)
-
+
+    d_o, shrink_part, branch = together(d_o, shrink_part, branch)
     d_o = tp.swap(d_o).reshape(R, C, t, W)
+    dense_part = outer(tp.table, o, d_att) if near else ()
+    d_o, dense_part, branch, shrink_part = together(d_o, dense_part, branch, shrink_part)
+    branch = tp.scatter_near(branch)
     shrink_other = over_rep(shrink_part)
-    dense_part = outer(tp.table, o, d_att) if near else ()
-    d_o, dense_part = together(d_o, dense_part)
     if near:
         dense_part = tp.scatter_given(*[a.reshape(n * W, D) for a in dense_part])
-    d_qkv, joined_grad = None, []
+    d_qkv, joined_grad, expand_all = None, [], ()
     for p in range(pairs):
         d_qkv = attention_backward(p, tp.order, prefixes, slopes[2 * p : 2 * p + 2], qkv, d_o, d_qkv)
+        d_qkv, dense_part, branch, expand_all = together(d_qkv, dense_part, branch, expand_all)
         mine = d_qkv.reshape(K, n * t, 3 * W)[:, :, 384 * p : 384 * (p + 1)]
         grad = sum(dot(a1_all[i], mine[i], 0, 0) for i in G).astype(BF)
-        d_qkv, grad, d_o, act, dense_part = together(d_qkv, grad, d_o, act, dense_part)
+        d_qkv, grad, d_o, expand_part, shrink_other = together(d_qkv, grad, d_o, expand_part, shrink_other)
         joined_grad.append(grad)
-        if p == 0 and near:
-            dense_part = tp.scatter_far(dense_part)
+        if p == 0:
+            expand_all = to_owners(expand_part)
+            if near:
+                dense_part = tp.scatter_far(dense_part)
     d_qkv = d_qkv.reshape(K, n * t, 3 * W)
+    layer_output = midway + added(tp.scatter_end(branch)) + sbias
 
     d_qkv_sum = jnp.sum(d_qkv.astype(F32), axis=(0, 1))
     d_exp_sum = sum(jnp.sum(d.astype(F32), axis=0) for d in d_exp)
@@ -791,49 +837,42 @@
     rest = jnp.pad(rest, ((0, 0), (0, 128 - used)))
     lanes = lambda a: jnp.broadcast_to(a[:, None], (D, 128))
     grad = with_columns(joined_grad, joined_cols, d_qkv_sum.reshape(1, 3 * W), lanes(gain_one), lanes(shift_one), rest)
-    expand_part, shrink_other, joined_grad = together(expand_part, shrink_other, joined_grad[:-1] + [grad])
-    joined_part = [lax.psum_scatter(a, "fsdp", scatter_dimension=0, tiled=True) for a in joined_grad]
-    expand_own = lax.all_to_all(expand_part.reshape(C, B, -1), "ctx", 0, 0, tiled=True)
-
-    d_a1 = tp.scatter_core(t, lambda i, a, b: dot(d_qkv[i, a:b], joined_cols, 1, 1))
+    joined_part = [lax.psum_scatter(a, "fsdp", scatter_dimension=0, tiled=True) for a in joined_grad[:-1]]
+    grad, joined_part = together(grad, joined_part)
+    joined_part.append(lax.psum_scatter(grad, "fsdp", scatter_dimension=0, tiled=True))
     if near:
         dense_part = tp.scatter_near(dense_part)
-    d_a1, expand_own, dense_part, act = together(d_a1, expand_own, dense_part, act)
-    d_a1 = tp.scatter_far(d_a1)
-    expand_other = over_rep(expand_own)
+    d_a1, dense_part = tp.scatter_core(t, lambda i, a, b: dot(d_qkv[i, a:b], joined_cols, 1, 1), dense_part)
+    expand_out = shrink_out = ()
     if near:
         shrink_out = pair_up(rep, shrink_part, shrink_other)
+        expand_out = unpack(unpack_expand_kernel, F, expand_all)
         dense_part = added(tp.scatter_end(dense_part)).astype(BF).reshape(F, W // F, D)
+    d_a1, shrink_out, expand_out, layer_output, dense_part, joined_part = together(
+        d_a1, shrink_out, expand_out, layer_output, dense_part, joined_part
+    )
+    if near:
         dense_part = scatter_shifts(dense_part, "fsdp", F)
-
-    branch = tp.scatter_core(t, lambda i, a, b: dot(act[i][a:b], shrink_rows, 1, 0))
-    d_a1, branch, dense_part = together(d_a1, branch, dense_part)
+    d_a1 = together(*tp.scatter_far(d_a1)) if near else d_a1
+    joined_all = to_owners(jnp.concatenate(joined_part, axis=1))
     d_a1 = tp.scatter_near(d_a1)
-    branch = tp.scatter_far(branch)
-    d_a1, branch, expand_other = together(d_a1, branch, expand_other)
-    if near:
-        expand_out = unpack(unpack_expand_kernel, F, rep, expand_own, expand_other)
-    branch = tp.scatter_near(branch)
+    d_a1, dense_part = together(d_a1, dense_part)
+    dense_other = over_rep(dense_part) if near else ()
     input_gradient = last(tp.scatter_end(d_a1), x, d_mid, gain_one)
-    branch, input_gradient = together(branch, input_gradient)
-    layer_output = midway + added(tp.scatter_end(branch)) + sbias
+    if near:
+        dense_out = pair_up(rep, dense_part, dense_other)
+        input_gradient, dense_out, joined_all = together(input_gradient, dense_out, joined_all)
 
     def both_reps(own, other):
         first = rep == 0
         return jnp.stack([jnp.where(first, own, other), jnp.where(first, other, own)])
 
-    joined_own = [lax.all_to_all(a.reshape(C, B, -1), "ctx", 0, 0, tiled=True) for a in joined_part]
-    joined_other = [over_rep(a) for a in joined_own]
-    little = jnp.sum((joined_own[-1][:, :, 384:].astype(F32) + joined_other[-1][:, :, 384:].astype(F32)), axis=0).T
-    joined_own = jnp.concatenate([a[:, :, :384] for a in joined_own], axis=2)
-    joined_other = jnp.concatenate([a[:, :, :384] for a in joined_other], axis=2)
-    if near:
-        joined_out = unpack(unpack_joined_kernel, F, rep, joined_own, joined_other)
-        dense_out = pair_up(rep, dense_part, over_rep(dense_part))
+    little = jnp.sum(joined_all[:, :, :, 3 * W :].astype(F32), axis=(0, 1)).T
+    if near:
+        joined_out = unpack(unpack_joined_kernel, F, joined_all, 128)
     else:
-        both = both_reps(expand_own, expand_other).reshape(R, C, B, F, E).transpose(2, 3, 1, 0, 4)
-        expand_out = both.reshape(B, FF).astype(F32)
-        both = both_reps(joined_own, joined_other).reshape(R, C, B, pairs, 3, 128).transpose(2, 4, 0, 1, 3, 5)
+        expand_out = expand_all.reshape(R, C, B, F, E).transpose(2, 3, 1, 0, 4).reshape(B, FF).astype(F32)
+        both = joined_all[:, :, :, : 3 * W].reshape(R, C, B, pairs, 3, 128).transpose(2, 4, 0, 1, 3, 5)
         joined_out = both.reshape(B, 3 * D).astype(F32)
         shrink_out = both_reps(shrink_part, shrink_other).reshape(FFB, D).astype(F32)
         part = dot(o.transpose(1, 0, 2).reshape(t, D), d_att, 0, 0).astype(BF)

time: 806 us -> 715 us (0.89)
  waiting for transfers between devices: 308 us -> 219 us
  blocking collectives: 27.1 us -> 0 us
  local copies, waits for them, and re-layouts: 87 us -> 106 us
  other arithmetic: 36.9 us -> 52.5 us
  Pallas kernels: 116 us -> 106 us
  starting transfers between devices: 75.7 us -> 66.2 us
    ppermute x17 -> x15, waiting for transfers between devices: 127 us -> 72.8 us  [x(): return lax.ppermute(x, 'rep', [(0, 1), (1, 0)])]
    all_to_all x1 -> x0, blocking collectives: 27.1 us -> none  [shards(): lax.all_to_all(a.reshape(C, B, -1), 'ctx', 0, 0, tiled=True)]
    all_gather x1, waiting for transfers between devices: 24.4 us -> 0.01 us  [shards(): lax.all_gather(jnp.concatenate([half_rows(dense_weight), low, small]), 'f...]
    all_to_all x1, waiting for transfers between devices: 0.01 us -> 19.1 us  [shards(): lax.all_to_all(pack(F, C, rep, joined_weight, expand_weight), 'ctx', 0, 0...]
    ppermute x5 -> x2, waiting for transfers between devices: 27.9 us -> 10.9 us  [over_rep(): return lax.ppermute(x, 'rep', [(0, 1), (1, 0)])]
    ppermute x3, waiting for transfers between devices: 33.4 us -> 18.2 us  [scatter_shifts(): lax.ppermute(mine, axis, [(i, (i + s) % size) for i in range(size)])]
    another operation x10 -> x11, other arithmetic: 2.76 us -> 14.1 us
    concatenate x6 -> x10, other arithmetic: 5.45 us -> 16.5 us  [the longest x2 4.86 us: to_owners(): blocks = jnp.concatenate([part.reshape(C, B, -1)] * R)]
  transfers between devices with their start and end apart: 66 -> 59, of which waited for: 33 -> 28; matrix products, arithmetic and copies ran while one was open for 23% -> 27% of each run, Pallas kernels for 14% -> 15%
where the time goes in v4:
time: 715 us; the launch traced here: 704 us
  waiting for transfers between devices  219 us (31%)
  matrix products  138 us (19%)
  local copies, waits for them, and re-layouts  106 us (15%)
  Pallas kernels  106 us (15%)
  starting transfers between devices  66.2 us (9%)
  other arithmetic  52.5 us (7%)
  between operations  16.4 us (2%)
    dot_general x26, matrix products, dot(): lax.dot_general(a, b, (((ca,), (cb,)), ((), ())), preferred_element_type=...  138 us
    ppermute x15, waiting for transfers between devices, x(): return lax.ppermute(x, 'rep', [(0, 1), (1, 0)])  72.8 us
    ppermute x27, waiting for transfers between devices, over(): return lax.ppermute(x, 'ctx', [(i, i ^ d) for i in range(4)])  66.9 us
    unnamed x183, local copies, waits for them, and re-layouts  61.6 us
    pallas_call x2, Pallas kernels, attention_backward(): pl.pallas_call(kernel, out_shape=jax.ShapeDtypeStruct(qkv.shape, BF), gri...  31 us
    ppermute x15, starting transfers between devices, x(): return lax.ppermute(x, 'rep', [(0, 1), (1, 0)])  20.8 us
    all_to_all x1, waiting for transfers between devices, shards(): lax.all_to_all(pack(F, C, rep, joined_weight, expand_weight), 'ctx', 0, 0...  19.1 us
    pallas_call x1, Pallas kernels, attention_forward(): pl.pallas_call(forward_kernel, out_shape=jax.ShapeDtypeStruct((n, C, T, p...  18.9 us
  transfers between devices with their start and end apart: 59, of which 28 were waited for; matrix products, arithmetic and copies ran while one was open for 27% of the time, Pallas kernels for 15%

profile of v4, /device:TPU:0, one launch (start us, length us, event | category | flops | bytes accessed | tf_op | source)
XLA Modules:
  0.0 703.7 jit_solution(3658588511912977574)
XLA Ops:
  30.5 19.1 %all-to-all-done = bf16[4,128,1792]{2,1,0:T(8,128)(2,1)} async-done(((bf16[4,128,1792]{2,1,0:T(8,128)(2,1)}), bf16[4,128,1792]{2,1,0:T(8,128)(2,1)}, u32[]{:S(2)}, u32[]{:S(2)}) %all-to-all-start) | async-done | bytes 1835040 | tf_op jit(solution)/shard_map/all_to_all | solution.py:709
  54.6 22.4 %collective-permute-done.2 = bf16[512,2048]{1,0:T(8,128)(2,1)} collective-permute-done((bf16[512,2048]{1,0:T(8,128)(2,1)}, bf16[512,2048]{1,0:T(8,128)(2,1)}, u32[]{:S(2)}, u32[]{:S(2)}) %collective-permute-start.2) | collective-permute-done | bytes 2097184 | tf_op jit(solution)/shard_map/ppermute | solution.py:562
  81.4 21.4 %collective-permute-done.1 = bf16[512,2048]{1,0:T(8,128)(2,1)} collective-permute-done((bf16[512,2048]{1,0:T(8,128)(2,1)}, bf16[512,2048]{1,0:T(8,128)(2,1)}, u32[]{:S(2)}, u32[]{:S(2)}) %collective-permute-start.1) | collective-permute-done | bytes 2097184 | tf_op jit(solution)/shard_map/ppermute | solution.py:559
  107.8 15.6 %collective-permute-done.3 = bf16[256,2048]{1,0:T(8,128)(2,1)S(1)} collective-permute-done((bf16[256,2048]{1,0:T(8,128)(2,1)S(1)}, bf16[256,2048]{1,0:T(8,128)(2,1)S(1)}, u32[]{:S(2)}, u32[]{:S(2)}) %collective-permute-start.3) | collective-permute-done | bytes 1048608 | tf_op jit(solution)/shard_map/ppermute | solution.py:559
  165.0 6.7 add_convert_fusion.6
  179.6 18.9 %shard_map.274 = bf16[2,4,256,256]{3,2,1,0:T(8,128)(2,1)S(1)} custom-call(s32[3,4]{1,0:T(4,128)S(1)} %add_add_fusion.2.order_ref.a, s32[2]{0:T(128)S(1)} %pad_add_fusion.prefix_ref.b, f32[4]{0:T(128)S(1)} %fusion.88.slope_ref, bf16[2,2,2,256,768]{4,3,2,1,0:T(8,128)(2,1)S(1)} %pad_maximum_fusion.2.qkv_ref.d), custom_call_target="tpu_custom_call" | custom-call | flops 12000000000 | bytes 1 | tf_op jit(solution)/shard_map/pallas_call | solution.py:105
  209.8 14.3 %all-to-all-done.1.o_ref = bf16[8,256,256]{2,1,0:T(8,128)(2,1)S(1)} async-done(((bf16[8,256,256]{2,1,0:T(8,128)(2,1)}), bf16[8,256,256]{2,1,0:T(8,128)(2,1)S(1)}, u32[]{:S(2)}, u32[]{:S(2)}) %all-to-all-start.1) | async-done | bytes 1048608 | tf_op jit(solution)/shard_map/all_to_all | solution.py:536
  224.1 9.9 %shard_map.275 = (f32[256,2048]{1,0:T(8,128)S(1)}, bf16[256,2048]{1,0:T(8,128)(2,1)S(1)}) custom-call(s32[8]{0:T(128)S(1)} %fusion.35.table_ref, bf16[8,256,256]{2,1,0:T(8,128)(2,1)S(1)} %all-to-all-done.1.o_ref, bf16[4,256,2048]{2,1,0:T(8,128)(2,1)} %bitcast.22.w_ref, bf16[4,256,2048]{2,1,0:T(8,128)(2,1)} %bitcast.23.v_ref, ...), custom_call_target="tpu_custom_call" | custom-call | flops 1 | bytes 1 | tf_op jit(solution)/shard_map/pallas_call | solution.py:277
  237.8 22.4 %collective-permute-done.15 = bf16[256,2048]{1,0:T(8,128)(2,1)S(1)} collective-permute-done((bf16[256,2048]{1,0:T(8,128)(2,1)S(1)}, bf16[256,2048]{1,0:T(8,128)(2,1)S(1)}, u32[]{:S(2)}, u32[]{:S(2)}) %collective-permute-start.15) | collective-permute-done | bytes 1048608 | tf_op jit(solution)/shard_map/ppermute | solution.py:562
  267.4 6.6 collective-permute-done.16
  291.0 12.2 %add_convert_fusion.3 = (bf16[1024,1024]{1,0:T(8,128)(2,1)}, bf16[1024,1024]{1,0:T(8,128)(2,1)S(1)}) fusion(f32[1024]{0:T(1024)S(1)} %bitcast.203, bf16[1024,2048]{1,0:T(8,128)(2,1)} %constant_dynamic-update-slice_fusion.5, bf16[2048,1024]{1,0:T(8,128)(2,1)S(1)} %get-tuple-element.173), kind=kOutput, calls=%fused_computation.21 | convolution fusion | flops 4307550208 | bytes 12587008 | tf_op jit(solution)/shard_map/dot_general | solution.py:19
  303.2 10.0 %multiply_convert_fusion.2 = (bf16[1024,1024]{1,0:T(8,128)(2,1)S(1)}, bf16[1024,1024]{1,0:T(8,128)(2,1)}) fusion(f32[1024]{0:T(1024)S(1)} %bitcast.204, bf16[1024,2048]{1,0:T(8,128)(2,1)} %collective-permute-done.18, bf16[2048,1024]{1,0:T(8,128)(2,1)S(1)} %get-tuple-element.173), kind=kOutput, calls=%fused_computation.18 | convolution fusion | flops 4307550208 | bytes 12587008 | tf_op jit(solution)/shard_map/dot_general | solution.py:19
  320.9 8.5 %add_convert_fusion.1 = bf16[1024,2048]{1,0:T(8,128)(2,1)} fusion(f32[1024,2048]{1,0:T(8,128)S(1)} %fusion.50, bf16[1024,1024]{1,0:T(8,128)(2,1)S(1)} %get-tuple-element.186, bf16[1024,2048]{1,0:T(8,128)(2,1)} %pad_maximum_fusion.1), kind=kOutput, calls=%fused_computation.4 | convolution fusion | flops 4299161600 | bytes 18874368 | tf_op jit(solution)/shard_map/dot_general | solution.py:19
  329.4 8.7 %multiply_convert_fusion = bf16[1024,1024]{1,0:T(8,128)(2,1)S(1)} fusion(bf16[1024,1024]{1,0:T(8,128)(2,1)} %get-tuple-element.179, bf16[1024,2048]{1,0:T(8,128)(2,1)} %collective-permute-done.10, bf16[1024,2048]{1,0:T(8,128)(2,1)} %copy-done.51), kind=kOutput, calls=%fused_computation.16 | convolution fusion | flops 4298113024 | bytes 12582912 | tf_op jit(solution)/shard_map/dot_general | solution.py:19
  346.6 8.7 %multiply_convert_fusion.1 = bf16[1024,1024]{1,0:T(8,128)(2,1)S(1)} fusion(bf16[1024,1024]{1,0:T(8,128)(2,1)} %get-tuple-element.178, bf16[1024,2048]{1,0:T(8,128)(2,1)} %pad_maximum_fusion.1, bf16[1024,2048]{1,0:T(8,128)(2,1)} %copy-done.51), kind=kOutput, calls=%fused_computation.17 | convolution fusion | flops 4298113024 | bytes 12582912 | tf_op jit(solution)/shard_map/dot_general | solution.py:19
  395.7 8.5 %add_convert_fusion = bf16[2048,1024]{1,0:T(8,128)(2,1)} fusion(f32[2048,1024]{1,0:T(8,128)S(1)} %fusion.51, bf16[1024,2048]{1,0:T(8,128)(2,1)} %constant_dynamic-update-slice_fusion.5, bf16[1024,1024]{1,0:T(8,128)(2,1)S(1)} %multiply_convert_fusion.1), kind=kOutput, calls=%fused_computation.3 | convolution fusion | flops 4299161600 | bytes 18874368 | tf_op jit(solution)/shard_map/dot_general | solution.py:19
  404.1 6.6 collective-permute-done.25.b_ref
  421.9 14.4 %shard_map.277 = (f32[256,2048]{1,0:T(8,128)}, bf16[256,2048]{1,0:T(8,128)(2,1)S(1)}, f32[4,2048]{1,0:T(4,128)S(1)}, bf16[8,256,256]{2,1,0:T(8,128)(2,1)S(1)}) custom-call(s32[8]{0:T(128)S(1)} %fusion.35.table_ref, f32[512,2048]{1,0:T(8,128)} %copy-done.60, bf16[256,2048]{1,0:T(8,128)(2,1)S(1)} %copy-done.40, ...), custom_call_target="tpu_custom_call" | custom-call | flops 1 | bytes 1 | tf_op jit(solution)/shard_map/pallas_call | solution.py:330
  467.4 15.3 %shard_map.279._ = bf16[2,2,2,256,768]{4,3,2,1,0:T(8,128)(2,1)S(1)} custom-call(s32[3,4]{1,0:T(4,128)S(1)} %add_add_fusion.2.order_ref.a, s32[2]{0:T(128)S(1)} %pad_add_fusion.prefix_ref.b, f32[2]{0:T(128)S(1)} %get-tuple-element.322.slope_ref, bf16[2,2,2,256,768]{4,3,2,1,0:T(8,128)(2,1)S(1)} %copy-done.22, bf16[2,4,256,256]{3,2,1,0:T(8,128)(2,1)S(1)} %bitcast.166), custom_call_target="tpu_custom_call" | custom-call | flops 12000000000 | bytes 1 | tf_op jit(solution)/shard_map/pallas_call | solution.py:123
  497.3 10.9 %collective-permute-done.32.other_ref = bf16[256,2048]{1,0:T(8,128)(2,1)S(1)} collective-permute-done((bf16[256,2048]{1,0:T(8,128)(2,1)S(1)}, bf16[256,2048]{1,0:T(8,128)(2,1)S(1)}, u32[]{:S(2)}, u32[]{:S(2)}) %collective-permute-start.32) | collective-permute-done | bytes 1048608 | tf_op jit(solution)/shard_map/ppermute | solution.py:695
  530.2 15.7 %shard_map.280 = bf16[2,2,2,256,768]{4,3,2,1,0:T(8,128)(2,1)S(1)} custom-call(s32[3,4]{1,0:T(4,128)S(1)} %add_add_fusion.2.order_ref.a, s32[2]{0:T(128)S(1)} %pad_add_fusion.prefix_ref.b, f32[2]{0:T(128)S(1)} %get-tuple-element.323.c, bf16[2,2,2,256,768]{4,3,2,1,0:T(8,128)(2,1)S(1)} %copy-done.23, ...), custom_call_target="tpu_custom_call", output_to_operand_aliasing={{}: (5, {})} | custom-call | flops 12000000000 | bytes 1 | tf_op jit(solution)/shard_map/pallas_call | solution.py:123
  612.7 9.7 %reduce-scatter.11.cloned.1.call-done = bf16[512,512]{1,0:T(8,128)(2,1)} async-done(((bf16[2048,512]{1,0:T(8,128)(2,1)}), bf16[512,512]{1,0:T(8,128)(2,1)}) %reduce-scatter.11.cloned.1.call-update) | async-done | bytes 524304 | tf_op jit(solution)/shard_map/reduce_scatter | solution.py:842
  634.1 7.0 collective-permute-done.39
  663.1 13.6 %collective-permute-done.44 = bf16[64,2048]{1,0:T(8,128)(2,1)} collective-permute-done((bf16[64,2048]{1,0:T(8,128)(2,1)}, bf16[64,2048]{1,0:T(8,128)(2,1)}, u32[]{:S(2)}, u32[]{:S(2)}) %collective-permute-start.44) | collective-permute-done | bytes 262176 | tf_op jit(solution)/shard_map/ppermute | solution.py:642
  (449 shorter events, 380.1 us)
Async XLA Ops:
  7.2 129.1 %all-gather.8.cloned.1.call-start = ((), (), s32[]{:S(2)}) async-start(), calls=%async_computation.14 | async-start | bytes 4259840 | tf_op jit(solution)/shard_map/all_gather | solution.py:706
  21.6 28.0 %all-to-all-start = ((bf16[4,128,1792]{2,1,0:T(8,128)(2,1)}), bf16[4,128,1792]{2,1,0:T(8,128)(2,1)}, u32[]{:S(2)}, u32[]{:S(2)}) async-start(bf16[4,128,1792]{2,1,0:T(8,128)(2,1)} %copy-done.9), calls=%async_computation | async-start | bytes 3670016 | tf_op jit(solution)/shard_map/all_to_all | solution.py:709
  26.0 139.0 %all-gather.6.cloned.1.call-start = ((), (), s32[]{:S(2)}) async-start(), calls=%async_computation.9 | async-start | bytes 3932160 | tf_op jit(solution)/shard_map/all_gather | solution.py:688
  27.5 49.5 %collective-permute-start.2 = (bf16[512,2048]{1,0:T(8,128)(2,1)}, bf16[512,2048]{1,0:T(8,128)(2,1)}, u32[]{:S(2)}, u32[]{:S(2)}) collective-permute-start(bf16[512,2048]{1,0:T(8,128)(2,1)} %pad_maximum_fusion.3), channel_id=1, source_target_pairs={{0,16},{16,0},{1,17},{17,1},{2,18},{18,2},{3,19},{19,3},{4,20},{20... | collective-permute-start | bytes 6291464 | tf_op jit(solution)/shard_map/ppermute | solution.py:562
  54.0 48.9 %collective-permute-start.1 = (bf16[512,2048]{1,0:T(8,128)(2,1)}, bf16[512,2048]{1,0:T(8,128)(2,1)}, u32[]{:S(2)}, u32[]{:S(2)}) collective-permute-start(bf16[512,2048]{1,0:T(8,128)(2,1)} %pad_maximum_fusion.3), channel_id=1, source_target_pairs={{0,2},{1,3},{2,0},{3,1},{4,6},{5,7},{6,4},{7,5},{8,10},{9,11},{10,... | collective-permute-start | bytes 6291464 | tf_op jit(solution)/shard_map/ppermute | solution.py:559
  54.0 213.4 %all-gather.10.cloned.1.call-start = ((), (), s32[]{:S(2)}) async-start(), calls=%async_computation.15 | async-start | bytes 7864320 | tf_op jit(solution)/shard_map/all_gather | solution.py:724
  79.8 43.7 %collective-permute-start.3 = (bf16[256,2048]{1,0:T(8,128)(2,1)S(1)}, bf16[256,2048]{1,0:T(8,128)(2,1)S(1)}, u32[]{:S(2)}, u32[]{:S(2)}) collective-permute-start(bf16[256,2048]{1,0:T(8,128)(2,1)S(1)} %get-tuple-element.302), channel_id=1, source_target_pairs={{0,2},{1,3},{2,0},{3,1},{4,6},{5,7},{6,4},{7,5},{8,10},{9,11},{10,... | collective-permute-start | bytes 3145736 | tf_op jit(solution)/shard_map/ppermute | solution.py:559
  131.8 26.2 %collective-permute-start.9 = (bf16[1024,2048]{1,0:T(8,128)(2,1)}, bf16[1024,2048]{1,0:T(8,128)(2,1)}, u32[]{:S(2)}, u32[]{:S(2)}) collective-permute-start(bf16[1024,2048]{1,0:T(8,128)(2,1)} %pad_maximum_fusion.x_ref), channel_id=1, source_target_pairs={{0,1},{1,0},{2,3},{3,2},{4,5},{5,4},{6,7},{7,6},{8,9},{9,8},{10,11... | collective-permute-start | bytes 12582920 | tf_op jit(solution)/shard_map/ppermute | solution.py:559
  144.7 53.9 %collective-permute-start.10 = (bf16[1024,2048]{1,0:T(8,128)(2,1)}, bf16[1024,2048]{1,0:T(8,128)(2,1)}, u32[]{:S(2)}, u32[]{:S(2)}) collective-permute-start(bf16[1024,2048]{1,0:T(8,128)(2,1)} %pad_maximum_fusion.1), channel_id=1, source_target_pairs={{0,1},{1,0},{2,3},{3,2},{4,5},{5,4},{6,7},{7,6},{8,9},{9,8},{10,11... | collective-permute-start | bytes 12582920 | tf_op jit(solution)/shard_map/ppermute | solution.py:559
  146.5 29.0 %collective-permute-start.5 = (bf16[256,2048]{1,0:T(8,128)(2,1)S(1)}, bf16[256,2048]{1,0:T(8,128)(2,1)}, u32[]{:S(2)}, u32[]{:S(2)}) collective-permute-start(bf16[256,2048]{1,0:T(8,128)(2,1)S(1)} %bitcast.183), channel_id=1, source_target_pairs={{0,16},{16,0},{1,17},{17,1},{2,18},{18,2},{3,19},{19,3},{4,20},{20... | collective-permute-start | bytes 3145736 | tf_op jit(solution)/shard_map/ppermute | solution.py:562
  148.3 27.2 %collective-permute-start.6 = (bf16[256,2048]{1,0:T(8,128)(2,1)S(1)}, bf16[256,2048]{1,0:T(8,128)(2,1)}, u32[]{:S(2)}, u32[]{:S(2)}) collective-permute-start(bf16[256,2048]{1,0:T(8,128)(2,1)S(1)} %bitcast.184), channel_id=1, source_target_pairs={{0,2},{1,3},{2,0},{3,1},{4,6},{5,7},{6,4},{7,5},{8,10},{9,11},{10,... | collective-permute-start | bytes 3145736 | tf_op jit(solution)/shard_map/ppermute | solution.py:559
  209.7 228.5 %reduce-scatter.5.cloned.1.call-start = ((), (), s32[]{:S(2)}) async-start(), calls=%async_computation.10 | async-start | bytes 5242880 | tf_op jit(solution)/shard_map/reduce_scatter | solution.py:784
  346.1 162.2 %reduce-scatter.7.cloned.1.call-start = ((), (), s32[]{:S(2)}) async-start(), calls=%async_computation.11 | async-start | bytes 5242880 | tf_op jit(solution)/shard_map/reduce_scatter | solution.py:795
  456.4 26.3 %collective-permute-start.29 = (bf16[1024,2048]{1,0:T(8,128)(2,1)}, bf16[1024,2048]{1,0:T(8,128)(2,1)S(1)}, u32[]{:S(2)}, u32[]{:S(2)}) collective-permute-start(bf16[1024,2048]{1,0:T(8,128)(2,1)} %bitcast.179), channel_id=1, source_target_pairs={{0,1},{1,0},{2,3},{3,2},{4,5},{5,4},{6,7},{7,6},{8,9},{9,8},{10,11... | collective-permute-start | bytes 12582920 | tf_op jit(solution)/shard_map/ppermute | solution.py:559
  460.1 27.3 %collective-permute-start.30 = (bf16[256,2048]{1,0:T(8,128)(2,1)S(1)}, bf16[256,2048]{1,0:T(8,128)(2,1)S(1)}, u32[]{:S(2)}, u32[]{:S(2)}) collective-permute-start(bf16[256,2048]{1,0:T(8,128)(2,1)S(1)} %pad_maximum_fusion.9), channel_id=1, source_target_pairs={{0,16},{16,0},{1,17},{17,1},{2,18},{18,2},{3,19},{19,3},{4,20},{20... | collective-permute-start | bytes 3145736 | tf_op jit(solution)/shard_map/ppermute | solution.py:562
  466.3 41.9 %collective-permute-start.32 = (bf16[256,2048]{1,0:T(8,128)(2,1)S(1)}, bf16[256,2048]{1,0:T(8,128)(2,1)S(1)}, u32[]{:S(2)}, u32[]{:S(2)}) collective-permute-start(bf16[256,2048]{1,0:T(8,128)(2,1)S(1)} %copy-done.35), channel_id=1, source_target_pairs={{0,16},{16,0},{1,17},{17,1},{2,18},{18,2},{3,19},{19,3},{4,20},{20... | collective-permute-start | bytes 3145736 | tf_op jit(solution)/shard_map/ppermute | solution.py:695
  511.7 40.6 %all-to-all-start.3 = ((bf16[8,128,1024]{2,1,0:T(8,128)(2,1)}), bf16[8,128,1024]{2,1,0:T(8,128)(2,1)S(1)}, u32[]{:S(2)}, u32[]{:S(2)}) async-start(bf16[8,128,1024]{2,1,0:T(8,128)(2,1)} %pad_maximum_fusion.4), calls=%async_computation.5 | async-start | bytes 4194304 | tf_op jit(solution)/shard_map/all_to_all | solution.py:692
  515.3 62.7 %reduce-scatter.9.cloned.1.call-start = ((), (), s32[]{:S(2)}) async-start(), calls=%async_computation.12 | async-start | bytes 1966080 | tf_op jit(solution)/shard_map/reduce_scatter | solution.py:840
  521.8 30.5 %collective-permute-start.33 = (bf16[128,2048]{1,0:T(8,128)(2,1)}, bf16[128,2048]{1,0:T(8,128)(2,1)}, u32[]{:S(2)}, u32[]{:S(2)}) collective-permute-start(bf16[128,2048]{1,0:T(8,128)(2,1)} %get-tuple-element.294), channel_id=1, source_target_pairs={{0,2},{1,3},{2,0},{3,1},{4,6},{5,7},{6,4},{7,5},{8,10},{9,11},{10,... | collective-permute-start | bytes 1572872 | tf_op jit(solution)/shard_map/ppermute | solution.py:559
  523.6 28.6 %collective-permute-start.34 = (bf16[128,2048]{1,0:T(8,128)(2,1)}, bf16[128,2048]{1,0:T(8,128)(2,1)S(1)}, u32[]{:S(2)}, u32[]{:S(2)}) collective-permute-start(bf16[128,2048]{1,0:T(8,128)(2,1)} %get-tuple-element.293), channel_id=1, source_target_pairs={{0,16},{16,0},{1,17},{17,1},{2,18},{18,2},{3,19},{19,3},{4,20},{20... | collective-permute-start | bytes 1572872 | tf_op jit(solution)/shard_map/ppermute | solution.py:562
  525.1 97.3 %reduce-scatter.11.cloned.1.call-start = ((), (), s32[]{:S(2)}) async-start(), calls=%async_computation.13 | async-start | bytes 2621440 | tf_op jit(solution)/shard_map/reduce_scatter | solution.py:842
  630.5 62.1 %all-to-all-start.4 = ((bf16[8,128,896]{2,1,0:T(8,128)(2,1)}), bf16[8,128,896]{2,1,0:T(8,128)(2,1)S(1)}, u32[]{:S(2)}, u32[]{:S(2)}) async-start(bf16[8,128,896]{2,1,0:T(8,128)(2,1)} %pad_maximum_fusion.5), calls=%async_computation.8 | async-start | bytes 3670016 | tf_op jit(solution)/shard_map/all_to_all | solution.py:692
  646.5 36.7 %collective-permute-start.41 = (bf16[256,2048]{1,0:T(8,128)(2,1)}, bf16[256,2048]{1,0:T(8,128)(2,1)}, u32[]{:S(2)}, u32[]{:S(2)}) collective-permute-start(bf16[256,2048]{1,0:T(8,128)(2,1)} %pad_maximum_fusion.13), channel_id=1, source_target_pairs={{0,16},{16,0},{1,17},{17,1},{2,18},{18,2},{3,19},{19,3},{4,20},{20... | collective-permute-start | bytes 3145736 | tf_op jit(solution)/shard_map/ppermute | solution.py:562
  651.9 31.3 %collective-permute-start.42 = (bf16[256,2048]{1,0:T(8,128)(2,1)}, bf16[256,2048]{1,0:T(8,128)(2,1)}, u32[]{:S(2)}, u32[]{:S(2)}) collective-permute-start(bf16[256,2048]{1,0:T(8,128)(2,1)} %pad_maximum_fusion.14), channel_id=1, source_target_pairs={{0,2},{1,3},{2,0},{3,1},{4,6},{5,7},{6,4},{7,5},{8,10},{9,11},{10,... | collective-permute-start | bytes 3145736 | tf_op jit(solution)/shard_map/ppermute | solution.py:559
  (118 other events, 1093.9 us)
Sparse Core Ops, SparseCore 0:
  16.9 70.5 all-gather.7
  89.1 62.1 all-gather.5
  153.4 113.9 all-gather.9
  346.2 76.3 reduce-scatter.4
  424.9 77.2 reduce-scatter.6
  525.3 34.7 reduce-scatter.8
  578.1 44.2 reduce-scatter.10

commit v5 on v4

--- a/solution.py
+++ b/solution.py
@@ -572,10 +572,14 @@
 
     def gather_far(self, x, from_x, from_y):
         half = x.shape[0] // 2
-        return x, from_y, from_x, self.y(from_x[:half]), self.x(from_y[half:])
+        near = jnp.concatenate([x, from_y, from_x, jnp.zeros_like(x)], axis=0)
+        return near, self.y(from_x[:half]), self.x(from_y[half:])
 
     def gather_core(self, pieces):
-        own = jnp.concatenate(pieces, axis=0)
+        own, low, high = pieces
+        at = own.shape[0] - 2 * low.shape[0]
+        own = lax.dynamic_update_slice_in_dim(own, low, at, 0)
+        own = lax.dynamic_update_slice_in_dim(own, high, at + low.shape[0], 0)
         return [own, self.core(own)]
 
     def gather_two(self, x, g, ready):
@@ -768,8 +772,8 @@
 
     if near:
         pieces, late = together(tp.gather_far(a2, tp.x(a2), tp.y(a2)), late)
+        expand_cols, shrink_rows = part_weights(early, late, m, C * B)
         a2_all = tp.gather_core(pieces)
-        expand_cols, shrink_rows = part_weights(early, late, m, C * B)
     else:
         a2_all = tp.gather(a2)
     act, slope = [], []
@@ -783,6 +787,7 @@
     slope, shrink_grad, act = together(slope, shrink_grad, act)
     shrink_part = lax.psum_scatter(shrink_grad, "fsdp", scatter_dimension=0, tiled=True)
     d_exp = [(dot(g_all[i], shrink_rows, 1, 1) * slope[i].astype(F32)).astype(BF) for i in G]
+    d_exp_sum = sum(jnp.sum(d.astype(F32), axis=0) for d in d_exp)
 
     d_a2 = tp.scatter_core(t, lambda i, a, b: dot(d_exp[i][a:b], expand_cols, 1, 1))
     d_a2, act = together(d_a2, act)
@@ -807,20 +812,20 @@
     d_qkv, joined_grad, expand_all = None, [], ()
     for p in range(pairs):
         d_qkv = attention_backward(p, tp.order, prefixes, slopes[2 * p : 2 * p + 2], qkv, d_o, d_qkv)
-        d_qkv, dense_part, branch, expand_all = together(d_qkv, dense_part, branch, expand_all)
+        d_qkv, dense_part, branch = together(d_qkv, dense_part, branch)
+        if p == 0 and near:
+            dense_part = tp.scatter_far(dense_part)
+        if p == pairs - 1:
+            d_qkv, expand_part, shrink_other = together(d_qkv, expand_part, shrink_other)
+            expand_all = to_owners(expand_part)
         mine = d_qkv.reshape(K, n * t, 3 * W)[:, :, 384 * p : 384 * (p + 1)]
         grad = sum(dot(a1_all[i], mine[i], 0, 0) for i in G).astype(BF)
-        d_qkv, grad, d_o, expand_part, shrink_other = together(d_qkv, grad, d_o, expand_part, shrink_other)
+        d_qkv, grad, d_o = together(d_qkv, grad, d_o)
         joined_grad.append(grad)
-        if p == 0:
-            expand_all = to_owners(expand_part)
-            if near:
-                dense_part = tp.scatter_far(dense_part)
     d_qkv = d_qkv.reshape(K, n * t, 3 * W)
     layer_output = midway + added(tp.scatter_end(branch)) + sbias
 
     d_qkv_sum = jnp.sum(d_qkv.astype(F32), axis=(0, 1))
-    d_exp_sum = sum(jnp.sum(d.astype(F32), axis=0) for d in d_exp)
 
     def place(vector, width):
         if near or width != D:
@@ -838,24 +843,24 @@
     lanes = lambda a: jnp.broadcast_to(a[:, None], (D, 128))
     grad = with_columns(joined_grad, joined_cols, d_qkv_sum.reshape(1, 3 * W), lanes(gain_one), lanes(shift_one), rest)
     joined_part = [lax.psum_scatter(a, "fsdp", scatter_dimension=0, tiled=True) for a in joined_grad[:-1]]
-    grad, joined_part = together(grad, joined_part)
+    grad, joined_part, expand_all = together(grad, joined_part, expand_all)
     joined_part.append(lax.psum_scatter(grad, "fsdp", scatter_dimension=0, tiled=True))
     if near:
         dense_part = tp.scatter_near(dense_part)
     d_a1, dense_part = tp.scatter_core(t, lambda i, a, b: dot(d_qkv[i, a:b], joined_cols, 1, 1), dense_part)
-    expand_out = shrink_out = ()
+    shrink_out = ()
     if near:
         shrink_out = pair_up(rep, shrink_part, shrink_other)
-        expand_out = unpack(unpack_expand_kernel, F, expand_all)
         dense_part = added(tp.scatter_end(dense_part)).astype(BF).reshape(F, W // F, D)
-    d_a1, shrink_out, expand_out, layer_output, dense_part, joined_part = together(
-        d_a1, shrink_out, expand_out, layer_output, dense_part, joined_part
-    )
+    d_a1, shrink_out, layer_output, dense_part, joined_part = together(d_a1, shrink_out, layer_output, dense_part, joined_part)
     if near:
         dense_part = scatter_shifts(dense_part, "fsdp", F)
     d_a1 = together(*tp.scatter_far(d_a1)) if near else d_a1
     joined_all = to_owners(jnp.concatenate(joined_part, axis=1))
     d_a1 = tp.scatter_near(d_a1)
+    if near:
+        expand_out = unpack(unpack_expand_kernel, F, expand_all)
+        d_a1, expand_out = together(d_a1, expand_out)
     d_a1, dense_part = together(d_a1, dense_part)
     dense_other = over_rep(dense_part) if near else ()
     input_gradient = last(tp.scatter_end(d_a1), x, d_mid, gain_one)

time: 715 us -> 680 us (0.951)
  waiting for transfers between devices: 219 us -> 199 us
  local copies, waits for them, and re-layouts: 106 us -> 92.4 us
    ppermute x27, waiting for transfers between devices: 66.9 us -> 53.4 us  [over(): return lax.ppermute(x, 'ctx', [(i, i ^ d) for i in range(4)])]
    unnamed x183 -> x177, local copies, waits for them, and re-layouts: 61.6 us -> 49.6 us
    ppermute x2, waiting for transfers between devices: 10.9 us -> 0.01 us  [over_rep(): return lax.ppermute(x, 'rep', [(0, 1), (1, 0)])]
    concatenate x0 -> x2, other arithmetic: none -> 10.3 us  [gather_far(): near = jnp.concatenate([x, from_y, from_x, jnp.zeros_like(x)], axis=0)]
  transfers between devices with their start and end apart: 59 -> 59, of which waited for: 28 -> 25; matrix products, arithmetic and copies ran while one was open for 27% -> 28% of each run, Pallas kernels for 15% -> 15%
where the time goes in v5:
time: 680 us; the launch traced here: 675 us
  waiting for transfers between devices  199 us (29%)
  matrix products  138 us (20%)
  Pallas kernels  105 us (15%)
  local copies, waits for them, and re-layouts  92.4 us (14%)
  starting transfers between devices  66.1 us (10%)
  other arithmetic  58.6 us (9%)
  between operations  16.5 us (2%)
    dot_general x26, matrix products, dot(): lax.dot_general(a, b, (((ca,), (cb,)), ((), ())), preferred_element_type=...  138 us
    ppermute x15, waiting for transfers between devices, x(): return lax.ppermute(x, 'rep', [(0, 1), (1, 0)])  79.8 us
    ppermute x27, waiting for transfers between devices, over(): return lax.ppermute(x, 'ctx', [(i, i ^ d) for i in range(4)])  53.4 us
    unnamed x177, local copies, waits for them, and re-layouts  49.6 us
    pallas_call x2, Pallas kernels, attention_backward(): pl.pallas_call(kernel, out_shape=jax.ShapeDtypeStruct(qkv.shape, BF), gri...  30.5 us
    ppermute x15, starting transfers between devices, x(): return lax.ppermute(x, 'rep', [(0, 1), (1, 0)])  22.2 us
    all_to_all x1, waiting for transfers between devices, shards(): lax.all_to_all(pack(F, C, rep, joined_weight, expand_weight), 'ctx', 0, 0...  19.2 us
    pallas_call x1, Pallas kernels, attention_forward(): pl.pallas_call(forward_kernel, out_shape=jax.ShapeDtypeStruct((n, C, T, p...  18.9 us
  transfers between devices with their start and end apart: 59, of which 25 were waited for; matrix products, arithmetic and copies ran while one was open for 28% of the time, Pallas kernels for 15%

profile of v5, /device:TPU:0, one launch (start us, length us, event | category | flops | bytes accessed | tf_op | source)
XLA Modules:
  0.0 674.5 jit_solution(7539868599071409145)
XLA Ops:
  30.5 19.2 %all-to-all-done = bf16[4,128,1792]{2,1,0:T(8,128)(2,1)} async-done(((bf16[4,128,1792]{2,1,0:T(8,128)(2,1)}), bf16[4,128,1792]{2,1,0:T(8,128)(2,1)}, u32[]{:S(2)}, u32[]{:S(2)}) %all-to-all-start) | async-done | bytes 1835040 | tf_op jit(solution)/shard_map/all_to_all | solution.py:713
  54.6 22.4 %collective-permute-done.2 = bf16[512,2048]{1,0:T(8,128)(2,1)} collective-permute-done((bf16[512,2048]{1,0:T(8,128)(2,1)}, bf16[512,2048]{1,0:T(8,128)(2,1)}, u32[]{:S(2)}, u32[]{:S(2)}) %collective-permute-start.2) | collective-permute-done | bytes 2097184 | tf_op jit(solution)/shard_map/ppermute | solution.py:562
  81.4 21.5 %collective-permute-done.1 = bf16[512,2048]{1,0:T(8,128)(2,1)} collective-permute-done((bf16[512,2048]{1,0:T(8,128)(2,1)}, bf16[512,2048]{1,0:T(8,128)(2,1)}, u32[]{:S(2)}, u32[]{:S(2)}) %collective-permute-start.1) | collective-permute-done | bytes 2097184 | tf_op jit(solution)/shard_map/ppermute | solution.py:559
  107.8 15.7 %collective-permute-done.3 = bf16[256,2048]{1,0:T(8,128)(2,1)S(1)} collective-permute-done((bf16[256,2048]{1,0:T(8,128)(2,1)S(1)}, bf16[256,2048]{1,0:T(8,128)(2,1)S(1)}, u32[]{:S(2)}, u32[]{:S(2)}) %collective-permute-start.3) | collective-permute-done | bytes 1048608 | tf_op jit(solution)/shard_map/ppermute | solution.py:559
  164.9 6.7 add_convert_fusion.6
  179.6 18.9 %shard_map.274 = bf16[2,4,256,256]{3,2,1,0:T(8,128)(2,1)S(1)} custom-call(s32[3,4]{1,0:T(4,128)S(1)} %add_add_fusion.2.order_ref.a, s32[2]{0:T(128)S(1)} %pad_add_fusion.prefix_ref.b, f32[4]{0:T(128)S(1)} %fusion.88.slope_ref, bf16[2,2,2,256,768]{4,3,2,1,0:T(8,128)(2,1)S(1)} %pad_maximum_fusion.2.qkv_ref.d), custom_call_target="tpu_custom_call" | custom-call | flops 12000000000 | bytes 1 | tf_op jit(solution)/shard_map/pallas_call | solution.py:105
  207.9 14.3 %all-to-all-done.1.o_ref = bf16[8,256,256]{2,1,0:T(8,128)(2,1)S(1)} async-done(((bf16[8,256,256]{2,1,0:T(8,128)(2,1)}), bf16[8,256,256]{2,1,0:T(8,128)(2,1)S(1)}, u32[]{:S(2)}, u32[]{:S(2)}) %all-to-all-start.1) | async-done | bytes 1048608 | tf_op jit(solution)/shard_map/all_to_all | solution.py:536
  222.2 9.9 %shard_map.275 = (f32[256,2048]{1,0:T(8,128)S(1)}, bf16[256,2048]{1,0:T(8,128)(2,1)S(1)}) custom-call(s32[8]{0:T(128)S(1)} %fusion.35.table_ref, bf16[8,256,256]{2,1,0:T(8,128)(2,1)S(1)} %all-to-all-done.1.o_ref, bf16[4,256,2048]{2,1,0:T(8,128)(2,1)} %bitcast.22.w_ref, bf16[4,256,2048]{2,1,0:T(8,128)(2,1)} %bitcast.23.v_ref, ...), custom_call_target="tpu_custom_call" | custom-call | flops 1 | bytes 1 | tf_op jit(solution)/shard_map/pallas_call | solution.py:277
  235.5 22.8 %collective-permute-done.15 = bf16[256,2048]{1,0:T(8,128)(2,1)S(1)} collective-permute-done((bf16[256,2048]{1,0:T(8,128)(2,1)S(1)}, bf16[256,2048]{1,0:T(8,128)(2,1)S(1)}, u32[]{:S(2)}, u32[]{:S(2)}) %collective-permute-start.15) | collective-permute-done | bytes 1048608 | tf_op jit(solution)/shard_map/ppermute | solution.py:562
  283.7 7.1 %add_convert_fusion.3 = (bf16[1024,1024]{1,0:T(8,128)(2,1)}, bf16[1024,1024]{1,0:T(8,128)(2,1)S(1)}) fusion(f32[1024]{0:T(1024)S(1)} %bitcast.203, bf16[1024,2048]{1,0:T(8,128)(2,1)S(1)} %copy-done.61, bf16[2048,1024]{1,0:T(8,128)(2,1)S(1)} %get-tuple-element.168), kind=kOutput, calls=%fused_computation.23 | convolution fusion | flops 4307550208 | bytes 12587008 | tf_op jit(solution)/shard_map/dot_general | solution.py:19
  290.8 10.0 %multiply_convert_fusion.2 = (bf16[1024,1024]{1,0:T(8,128)(2,1)S(1)}, bf16[1024,1024]{1,0:T(8,128)(2,1)}) fusion(f32[1024]{0:T(1024)S(1)} %bitcast.204, bf16[1024,2048]{1,0:T(8,128)(2,1)} %collective-permute-done.18, bf16[2048,1024]{1,0:T(8,128)(2,1)S(1)} %get-tuple-element.168), kind=kOutput, calls=%fused_computation.20 | convolution fusion | flops 4307550208 | bytes 12587008 | tf_op jit(solution)/shard_map/dot_general | solution.py:19
  302.2 6.8 %fusion.50 = f32[1024,2048]{1,0:T(8,128)S(1)} fusion(bf16[1024,1024]{1,0:T(8,128)(2,1)S(1)} %get-tuple-element.182, bf16[1024,2048]{1,0:T(8,128)(2,1)} %collective-permute-done.10), kind=kOutput, calls=%fused_computation.167 | convolution fusion | flops 4294967296 | bytes 14680064 | tf_op jit(solution)/shard_map/dot_general | solution.py:19
  309.0 8.4 %add_convert_fusion.1 = bf16[1024,2048]{1,0:T(8,128)(2,1)} fusion(f32[1024,2048]{1,0:T(8,128)S(1)} %fusion.50, bf16[1024,1024]{1,0:T(8,128)(2,1)S(1)} %get-tuple-element.181, bf16[1024,2048]{1,0:T(8,128)(2,1)} %pad_maximum_fusion.1), kind=kOutput, calls=%fused_computation.4 | convolution fusion | flops 4299161600 | bytes 18874368 | tf_op jit(solution)/shard_map/dot_general | solution.py:19
  317.4 8.7 %convert_reduce_fusion.1 = (f32[1024]{0:T(1024)S(1)}, bf16[1024,1024]{1,0:T(8,128)(2,1)S(1)}) fusion(bf16[1024,1024]{1,0:T(8,128)(2,1)} %get-tuple-element.174, bf16[1024,2048]{1,0:T(8,128)(2,1)} %collective-permute-done.10, bf16[1024,2048]{1,0:T(8,128)(2,1)} %copy-done.51), kind=kOutput, calls=%fused_computation.10 | convolution fusion | flops 4300209152 | bytes 12587008 | tf_op jit(solution)/shard_map/dot_general | solution.py:19
  334.3 8.7 %convert_reduce_fusion.2 = (f32[1024]{0:T(1024)S(1)}, bf16[1024,1024]{1,0:T(8,128)(2,1)S(1)}) fusion(bf16[1024,1024]{1,0:T(8,128)(2,1)} %get-tuple-element.173, bf16[1024,2048]{1,0:T(8,128)(2,1)} %pad_maximum_fusion.1, bf16[1024,2048]{1,0:T(8,128)(2,1)} %copy-done.51), kind=kOutput, calls=%fused_computation.11 | convolution fusion | flops 4300209152 | bytes 12587008 | tf_op jit(solution)/shard_map/dot_general | solution.py:19
  376.3 9.4 %fusion.51 = f32[2048,1024]{1,0:T(8,128)} fusion(bf16[1024,2048]{1,0:T(8,128)(2,1)} %collective-permute-done.18, bf16[1024,1024]{1,0:T(8,128)(2,1)S(1)} %copy-done.83), kind=kOutput, calls=%fused_computation.168 | convolution fusion | flops 4294967296 | bytes 14680064 | tf_op jit(solution)/shard_map/dot_general | solution.py:19
  385.7 8.4 %add_convert_fusion = bf16[2048,1024]{1,0:T(8,128)(2,1)} fusion(f32[2048,1024]{1,0:T(8,128)} %fusion.51, bf16[1024,2048]{1,0:T(8,128)(2,1)S(1)} %copy-done.62, bf16[1024,1024]{1,0:T(8,128)(2,1)S(1)} %get-tuple-element.189), kind=kOutput, calls=%fused_computation.3 | convolution fusion | flops 4299161600 | bytes 18874368 | tf_op jit(solution)/shard_map/dot_general | solution.py:19
  407.3 14.2 %shard_map.277 = (f32[256,2048]{1,0:T(8,128)}, bf16[256,2048]{1,0:T(8,128)(2,1)S(1)}, f32[4,2048]{1,0:T(4,128)S(1)}, bf16[8,256,256]{2,1,0:T(8,128)(2,1)S(1)}) custom-call(s32[8]{0:T(128)S(1)} %fusion.35.table_ref, f32[512,2048]{1,0:T(8,128)} %copy-done.60, bf16[256,2048]{1,0:T(8,128)(2,1)S(1)} %copy-done.41, ...), custom_call_target="tpu_custom_call" | custom-call | flops 1 | bytes 1 | tf_op jit(solution)/shard_map/pallas_call | solution.py:330
  451.7 15.1 %shard_map.279._ = bf16[2,2,2,256,768]{4,3,2,1,0:T(8,128)(2,1)S(1)} custom-call(s32[3,4]{1,0:T(4,128)S(1)} %add_add_fusion.2.order_ref.a, s32[2]{0:T(128)S(1)} %pad_add_fusion.prefix_ref.b, f32[2]{0:T(128)S(1)} %get-tuple-element.320.slope_ref, bf16[2,2,2,256,768]{4,3,2,1,0:T(8,128)(2,1)S(1)} %copy-done.24, bf16[2,4,256,256]{3,2,1,0:T(8,128)(2,1)S(1)} %bitcast.166), custom_call_target="tpu_custom_call" | custom-call | flops 12000000000 | bytes 1 | tf_op jit(solution)/shard_map/pallas_call | solution.py:123
  491.9 15.5 %shard_map.280 = bf16[2,2,2,256,768]{4,3,2,1,0:T(8,128)(2,1)S(1)} custom-call(s32[3,4]{1,0:T(4,128)S(1)} %add_add_fusion.2.order_ref.a, s32[2]{0:T(128)S(1)} %pad_add_fusion.prefix_ref.b, f32[2]{0:T(128)S(1)} %get-tuple-element.321.c, bf16[2,2,2,256,768]{4,3,2,1,0:T(8,128)(2,1)S(1)} %copy-done.25, ...), custom_call_target="tpu_custom_call", output_to_operand_aliasing={{}: (5, {})} | custom-call | flops 12000000000 | bytes 1 | tf_op jit(solution)/shard_map/pallas_call | solution.py:123
  557.2 15.4 %collective-permute-done.35 = bf16[256,2048]{1,0:T(8,128)(2,1)} collective-permute-done((bf16[256,2048]{1,0:T(8,128)(2,1)}, bf16[256,2048]{1,0:T(8,128)(2,1)}, u32[]{:S(2)}, u32[]{:S(2)}) %collective-permute-start.35) | collective-permute-done | bytes 1048608 | tf_op jit(solution)/shard_map/ppermute | solution.py:562
  587.1 7.8 %reduce-scatter.11.cloned.1.call-done = bf16[512,512]{1,0:T(8,128)(2,1)} async-done(((bf16[2048,512]{1,0:T(8,128)(2,1)}), bf16[512,512]{1,0:T(8,128)(2,1)}) %reduce-scatter.11.cloned.1.call-update) | async-done | bytes 524304 | tf_op jit(solution)/shard_map/reduce_scatter | solution.py:847
  606.5 7.1 %collective-permute-done.39 = bf16[128,2048]{1,0:T(8,128)(2,1)} collective-permute-done((bf16[128,2048]{1,0:T(8,128)(2,1)}, bf16[128,2048]{1,0:T(8,128)(2,1)}, u32[]{:S(2)}, u32[]{:S(2)}) %collective-permute-start.39) | collective-permute-done | bytes 524320 | tf_op jit(solution)/shard_map/ppermute | solution.py:559
  634.4 13.5 %collective-permute-done.44 = bf16[64,2048]{1,0:T(8,128)(2,1)} collective-permute-done((bf16[64,2048]{1,0:T(8,128)(2,1)}, bf16[64,2048]{1,0:T(8,128)(2,1)}, u32[]{:S(2)}, u32[]{:S(2)}) %collective-permute-start.44) | collective-permute-done | bytes 262176 | tf_op jit(solution)/shard_map/ppermute | solution.py:646
  (447 shorter events, 350.7 us)
Async XLA Ops:
  7.2 129.0 %all-gather.8.cloned.1.call-start = ((), (), s32[]{:S(2)}) async-start(), calls=%async_computation.14 | async-start | bytes 4259840 | tf_op jit(solution)/shard_map/all_gather | solution.py:710
  21.6 28.0 %all-to-all-start = ((bf16[4,128,1792]{2,1,0:T(8,128)(2,1)}), bf16[4,128,1792]{2,1,0:T(8,128)(2,1)}, u32[]{:S(2)}, u32[]{:S(2)}) async-start(bf16[4,128,1792]{2,1,0:T(8,128)(2,1)} %copy-done.11), calls=%async_computation | async-start | bytes 3670016 | tf_op jit(solution)/shard_map/all_to_all | solution.py:713
  26.0 138.9 %all-gather.6.cloned.1.call-start = ((), (), s32[]{:S(2)}) async-start(), calls=%async_computation.9 | async-start | bytes 3932160 | tf_op jit(solution)/shard_map/all_gather | solution.py:692
  27.5 49.5 %collective-permute-start.2 = (bf16[512,2048]{1,0:T(8,128)(2,1)}, bf16[512,2048]{1,0:T(8,128)(2,1)}, u32[]{:S(2)}, u32[]{:S(2)}) collective-permute-start(bf16[512,2048]{1,0:T(8,128)(2,1)} %pad_maximum_fusion.3), channel_id=1, source_target_pairs={{0,16},{16,0},{1,17},{17,1},{2,18},{18,2},{3,19},{19,3},{4,20},{20... | collective-permute-start | bytes 6291464 | tf_op jit(solution)/shard_map/ppermute | solution.py:562
  54.0 48.9 %collective-permute-start.1 = (bf16[512,2048]{1,0:T(8,128)(2,1)}, bf16[512,2048]{1,0:T(8,128)(2,1)}, u32[]{:S(2)}, u32[]{:S(2)}) collective-permute-start(bf16[512,2048]{1,0:T(8,128)(2,1)} %pad_maximum_fusion.3), channel_id=1, source_target_pairs={{0,2},{1,3},{2,0},{3,1},{4,6},{5,7},{6,4},{7,5},{8,10},{9,11},{10,... | collective-permute-start | bytes 6291464 | tf_op jit(solution)/shard_map/ppermute | solution.py:559
  54.0 213.5 %all-gather.10.cloned.1.call-start = ((), (), s32[]{:S(2)}) async-start(), calls=%async_computation.15 | async-start | bytes 7864320 | tf_op jit(solution)/shard_map/all_gather | solution.py:728
  79.7 43.8 %collective-permute-start.3 = (bf16[256,2048]{1,0:T(8,128)(2,1)S(1)}, bf16[256,2048]{1,0:T(8,128)(2,1)S(1)}, u32[]{:S(2)}, u32[]{:S(2)}) collective-permute-start(bf16[256,2048]{1,0:T(8,128)(2,1)S(1)} %get-tuple-element.300), channel_id=1, source_target_pairs={{0,2},{1,3},{2,0},{3,1},{4,6},{5,7},{6,4},{7,5},{8,10},{9,11},{10,... | collective-permute-start | bytes 3145736 | tf_op jit(solution)/shard_map/ppermute | solution.py:559
  131.7 26.1 %collective-permute-start.9 = (bf16[1024,2048]{1,0:T(8,128)(2,1)}, bf16[1024,2048]{1,0:T(8,128)(2,1)}, u32[]{:S(2)}, u32[]{:S(2)}) collective-permute-start(bf16[1024,2048]{1,0:T(8,128)(2,1)} %pad_maximum_fusion.x_ref), channel_id=1, source_target_pairs={{0,1},{1,0},{2,3},{3,2},{4,5},{5,4},{6,7},{7,6},{8,9},{9,8},{10,11... | collective-permute-start | bytes 12582920 | tf_op jit(solution)/shard_map/ppermute | solution.py:559
  144.6 57.9 %collective-permute-start.10 = (bf16[1024,2048]{1,0:T(8,128)(2,1)}, bf16[1024,2048]{1,0:T(8,128)(2,1)}, u32[]{:S(2)}, u32[]{:S(2)}) collective-permute-start(bf16[1024,2048]{1,0:T(8,128)(2,1)} %pad_maximum_fusion.1), channel_id=1, source_target_pairs={{0,1},{1,0},{2,3},{3,2},{4,5},{5,4},{6,7},{7,6},{8,9},{9,8},{10,11... | collective-permute-start | bytes 12582920 | tf_op jit(solution)/shard_map/ppermute | solution.py:559
  146.4 29.0 %collective-permute-start.5 = (bf16[256,2048]{1,0:T(8,128)(2,1)S(1)}, bf16[256,2048]{1,0:T(8,128)(2,1)}, u32[]{:S(2)}, u32[]{:S(2)}) collective-permute-start(bf16[256,2048]{1,0:T(8,128)(2,1)S(1)} %bitcast.185), channel_id=1, source_target_pairs={{0,16},{16,0},{1,17},{17,1},{2,18},{18,2},{3,19},{19,3},{4,20},{20... | collective-permute-start | bytes 3145736 | tf_op jit(solution)/shard_map/ppermute | solution.py:562
  148.2 27.2 %collective-permute-start.6 = (bf16[256,2048]{1,0:T(8,128)(2,1)S(1)}, bf16[256,2048]{1,0:T(8,128)(2,1)}, u32[]{:S(2)}, u32[]{:S(2)}) collective-permute-start(bf16[256,2048]{1,0:T(8,128)(2,1)S(1)} %bitcast.186), channel_id=1, source_target_pairs={{0,2},{1,3},{2,0},{3,1},{4,6},{5,7},{6,4},{7,5},{8,10},{9,11},{10,... | collective-permute-start | bytes 3145736 | tf_op jit(solution)/shard_map/ppermute | solution.py:559
  176.9 25.6 %collective-permute-start.11 = (bf16[128,2048]{1,0:T(8,128)(2,1)S(1)}, bf16[128,2048]{1,0:T(8,128)(2,1)S(1)}, u32[]{:S(2)}, u32[]{:S(2)}) collective-permute-start(bf16[128,2048]{1,0:T(8,128)(2,1)S(1)} %slice.332), channel_id=1, source_target_pairs={{0,2},{1,3},{2,0},{3,1},{4,6},{5,7},{6,4},{7,5},{8,10},{9,11},{10,... | collective-permute-start | bytes 1572872 | tf_op jit(solution)/shard_map/ppermute | solution.py:559
  207.8 215.6 %reduce-scatter.5.cloned.1.call-start = ((), (), s32[]{:S(2)}) async-start(), calls=%async_computation.10 | async-start | bytes 5242880 | tf_op jit(solution)/shard_map/reduce_scatter | solution.py:788
  334.1 175.0 %reduce-scatter.7.cloned.1.call-start = ((), (), s32[]{:S(2)}) async-start(), calls=%async_computation.11 | async-start | bytes 5242880 | tf_op jit(solution)/shard_map/reduce_scatter | solution.py:800
  427.2 123.3 %reduce-scatter.9.cloned.1.call-start = ((), (), s32[]{:S(2)}) async-start(), calls=%async_computation.12 | async-start | bytes 1966080 | tf_op jit(solution)/shard_map/reduce_scatter | solution.py:845
  445.3 29.2 %collective-permute-start.30 = (bf16[256,2048]{1,0:T(8,128)(2,1)S(1)}, bf16[256,2048]{1,0:T(8,128)(2,1)S(1)}, u32[]{:S(2)}, u32[]{:S(2)}) collective-permute-start(bf16[256,2048]{1,0:T(8,128)(2,1)S(1)} %pad_maximum_fusion.9), channel_id=1, source_target_pairs={{0,16},{16,0},{1,17},{17,1},{2,18},{18,2},{3,19},{19,3},{4,20},{20... | collective-permute-start | bytes 3145736 | tf_op jit(solution)/shard_map/ppermute | solution.py:562
  450.6 58.5 %collective-permute-start.34 = (bf16[256,2048]{1,0:T(8,128)(2,1)S(1)}, bf16[256,2048]{1,0:T(8,128)(2,1)S(1)}, u32[]{:S(2)}, u32[]{:S(2)}) collective-permute-start(bf16[256,2048]{1,0:T(8,128)(2,1)S(1)} %copy-done.36), channel_id=1, source_target_pairs={{0,16},{16,0},{1,17},{17,1},{2,18},{18,2},{3,19},{19,3},{4,20},{20... | collective-permute-start | bytes 3145736 | tf_op jit(solution)/shard_map/ppermute | solution.py:699
  520.8 29.7 %all-to-all-start.3 = ((bf16[8,128,1024]{2,1,0:T(8,128)(2,1)}), bf16[8,128,1024]{2,1,0:T(8,128)(2,1)S(1)}, u32[]{:S(2)}, u32[]{:S(2)}) async-start(bf16[8,128,1024]{2,1,0:T(8,128)(2,1)} %pad_maximum_fusion.4), calls=%async_computation.6 | async-start | bytes 4194304 | tf_op jit(solution)/shard_map/all_to_all | solution.py:696
  524.4 70.5 %reduce-scatter.11.cloned.1.call-start = ((), (), s32[]{:S(2)}) async-start(), calls=%async_computation.13 | async-start | bytes 2621440 | tf_op jit(solution)/shard_map/reduce_scatter | solution.py:847
  530.7 41.9 %collective-permute-start.35 = (bf16[256,2048]{1,0:T(8,128)(2,1)}, bf16[256,2048]{1,0:T(8,128)(2,1)}, u32[]{:S(2)}, u32[]{:S(2)}) collective-permute-start(bf16[256,2048]{1,0:T(8,128)(2,1)} %pad_maximum_fusion.11), channel_id=1, source_target_pairs={{0,16},{16,0},{1,17},{17,1},{2,18},{18,2},{3,19},{19,3},{4,20},{20... | collective-permute-start | bytes 3145736 | tf_op jit(solution)/shard_map/ppermute | solution.py:562
  533.9 38.7 %collective-permute-start.36 = (bf16[256,2048]{1,0:T(8,128)(2,1)}, bf16[256,2048]{1,0:T(8,128)(2,1)}, u32[]{:S(2)}, u32[]{:S(2)}) collective-permute-start(bf16[256,2048]{1,0:T(8,128)(2,1)} %pad_maximum_fusion.12), channel_id=1, source_target_pairs={{0,2},{1,3},{2,0},{3,1},{4,6},{5,7},{6,4},{7,5},{8,10},{9,11},{10,... | collective-permute-start | bytes 3145736 | tf_op jit(solution)/shard_map/ppermute | solution.py:559
  602.9 60.5 %all-to-all-start.4 = ((bf16[8,128,896]{2,1,0:T(8,128)(2,1)}), bf16[8,128,896]{2,1,0:T(8,128)(2,1)S(1)}, u32[]{:S(2)}, u32[]{:S(2)}) async-start(bf16[8,128,896]{2,1,0:T(8,128)(2,1)} %pad_maximum_fusion.5), calls=%async_computation.8 | async-start | bytes 3670016 | tf_op jit(solution)/shard_map/all_to_all | solution.py:696
  619.0 36.7 %collective-permute-start.41 = (bf16[256,2048]{1,0:T(8,128)(2,1)}, bf16[256,2048]{1,0:T(8,128)(2,1)}, u32[]{:S(2)}, u32[]{:S(2)}) collective-permute-start(bf16[256,2048]{1,0:T(8,128)(2,1)} %pad_maximum_fusion.13), channel_id=1, source_target_pairs={{0,16},{16,0},{1,17},{17,1},{2,18},{18,2},{3,19},{19,3},{4,20},{20... | collective-permute-start | bytes 3145736 | tf_op jit(solution)/shard_map/ppermute | solution.py:562
  624.4 31.3 %collective-permute-start.42 = (bf16[256,2048]{1,0:T(8,128)(2,1)}, bf16[256,2048]{1,0:T(8,128)(2,1)}, u32[]{:S(2)}, u32[]{:S(2)}) collective-permute-start(bf16[256,2048]{1,0:T(8,128)(2,1)} %pad_maximum_fusion.14), channel_id=1, source_target_pairs={{0,2},{1,3},{2,0},{3,1},{4,6},{5,7},{6,4},{7,5},{8,10},{9,11},{10,... | collective-permute-start | bytes 3145736 | tf_op jit(solution)/shard_map/ppermute | solution.py:559
  (119 other events, 1197.6 us)
Sparse Core Ops, SparseCore 0:
  16.9 70.5 all-gather.7
  89.1 62.1 all-gather.5
  153.4 114.0 all-gather.9
  334.2 76.7 reduce-scatter.4
  413.3 77.2 reduce-scatter.6
  492.7 35.7 reduce-scatter.8
  550.6 44.2 reduce-scatter.10

commit v6 on v5

--- a/solution.py
+++ b/solution.py
@@ -302,7 +302,7 @@
 
     @pl.when(d == 0)
     def _():
-        grad = a_ref[...] + b_ref[...].astype(F32) + c_ref[...].astype(F32)
+        grad = a_ref[...].astype(F32) + b_ref[...].astype(F32) + c_ref[...].astype(F32)
         n, inverse = normed(mid_ref[...])
         g = g_ref[...].astype(F32)
         u = grad * gain_ref[...]
@@ -390,7 +390,7 @@
 
 
 def last_kernel(a_ref, b_ref, c_ref, x_ref, d_mid_ref, gain_ref, out_ref):
-    grad = a_ref[...] + b_ref[...].astype(F32) + c_ref[...].astype(F32)
+    grad = a_ref[...].astype(F32) + b_ref[...].astype(F32) + c_ref[...].astype(F32)
     n, inverse = normed(x_ref[...].astype(F32))
     u = grad * gain_ref[...]
     mean_u = jnp.mean(u, axis=-1, keepdims=True)
@@ -530,7 +530,7 @@
         return lax.psum_scatter(state, self.axes, scatter_dimension=0, tiled=True)
 
     def scatter_end(self, state):
-        return state.astype(F32), jnp.zeros_like(state), jnp.zeros_like(state)
+        return state, jnp.zeros_like(state), jnp.zeros_like(state)
 
     def swap(self, parts):
         return lax.all_to_all(parts, self.axes, 0, 0, tiled=True)
@@ -597,8 +597,8 @@
         far_x = part(1, 2 * rows, 4 * rows).astype(BF)
         near_x = part(1, 0, 2 * rows).astype(BF)
         far_x, near_x, halfway = together(far_x, near_x, () if ready is None else ready)
-        far_x = part(0, 2 * rows, 4 * rows) + self.core(far_x).astype(F32)
-        near_x = part(0, 0, 2 * rows) + self.core(near_x).astype(F32)
+        far_x = (part(0, 2 * rows, 4 * rows) + self.core(far_x).astype(F32)).astype(BF)
+        near_x = (part(0, 0, 2 * rows) + self.core(near_x).astype(F32)).astype(BF)
         return (far_x, near_x) if ready is None else ((far_x, near_x), halfway)
 
     def scatter_given(self, own, oth):
@@ -608,8 +608,8 @@
     def scatter_far(self, state):
         far_x, near_x = state
         rows = far_x.shape[0] // 2
-        far = far_x[rows:].astype(BF)
-        return far_x, near_x, self.y(far[: rows // 2]), self.x(far[rows // 2 :])
+        half = rows // 2
+        return far_x, near_x, self.y(far_x[rows : rows + half]), self.x(far_x[rows + half :])
 
     def scatter_near(self, state):
         far_x, near_x, to_y, to_x = state
@@ -843,11 +843,11 @@
     lanes = lambda a: jnp.broadcast_to(a[:, None], (D, 128))
     grad = with_columns(joined_grad, joined_cols, d_qkv_sum.reshape(1, 3 * W), lanes(gain_one), lanes(shift_one), rest)
     joined_part = [lax.psum_scatter(a, "fsdp", scatter_dimension=0, tiled=True) for a in joined_grad[:-1]]
-    grad, joined_part, expand_all = together(grad, joined_part, expand_all)
+    grad, joined_part = together(grad, joined_part)
     joined_part.append(lax.psum_scatter(grad, "fsdp", scatter_dimension=0, tiled=True))
     if near:
         dense_part = tp.scatter_near(dense_part)
-    d_a1, dense_part = tp.scatter_core(t, lambda i, a, b: dot(d_qkv[i, a:b], joined_cols, 1, 1), dense_part)
+    d_a1, expand_all = tp.scatter_core(t, lambda i, a, b: dot(d_qkv[i, a:b], joined_cols, 1, 1), expand_all)
     shrink_out = ()
     if near:
         shrink_out = pair_up(rep, shrink_part, shrink_other)

time: 680 us -> 664 us (0.976)
    ppermute x27, waiting for transfers between devices: 53.4 us -> 65.5 us  [over(): return lax.ppermute(x, 'ctx', [(i, i ^ d) for i in range(4)])]
    reduce_scatter x1, waiting for transfers between devices: 7.77 us -> 0.01 us  [shards(): lax.psum_scatter(grad, 'fsdp', scatter_dimension=0, tiled=True)]
    unnamed x177 -> x181, local copies, waits for them, and re-layouts: 49.6 us -> 48 us
  transfers between devices with their start and end apart: 59 -> 59, of which waited for: 25 -> 26; matrix products, arithmetic and copies ran while one was open for 28% -> 27% of each run, Pallas kernels for 15% -> 15%
where the time goes in v6:
time: 664 us; the launch traced here: 659 us
  waiting for transfers between devices  196 us (30%)
  matrix products  132 us (20%)
  Pallas kernels  104 us (16%)
  local copies, waits for them, and re-layouts  88.9 us (13%)
  starting transfers between devices  67.1 us (10%)
  other arithmetic  54.4 us (8%)
  between operations  16.5 us (2%)
    dot_general x26, matrix products, dot(): lax.dot_general(a, b, (((ca,), (cb,)), ((), ())), preferred_element_type=...  132 us
    ppermute x15, waiting for transfers between devices, x(): return lax.ppermute(x, 'rep', [(0, 1), (1, 0)])  77.7 us
    ppermute x27, waiting for transfers between devices, over(): return lax.ppermute(x, 'ctx', [(i, i ^ d) for i in range(4)])  65.5 us
    unnamed x181, local copies, waits for them, and re-layouts  48 us
    pallas_call x2, Pallas kernels, attention_backward(): pl.pallas_call(kernel, out_shape=jax.ShapeDtypeStruct(qkv.shape, BF), gri...  30.5 us
    ppermute x15, starting transfers between devices, x(): return lax.ppermute(x, 'rep', [(0, 1), (1, 0)])  22.4 us
    all_to_all x1, waiting for transfers between devices, shards(): lax.all_to_all(pack(F, C, rep, joined_weight, expand_weight), 'ctx', 0, 0...  19.1 us
    pallas_call x1, Pallas kernels, attention_forward(): pl.pallas_call(forward_kernel, out_shape=jax.ShapeDtypeStruct((n, C, T, p...  18.9 us
  transfers between devices with their start and end apart: 59, of which 26 were waited for; matrix products, arithmetic and copies ran while one was open for 27% of the time, Pallas kernels for 15%

profile of v6, /device:TPU:0, one launch (start us, length us, event | category | flops | bytes accessed | tf_op | source)
XLA Modules:
  0.0 659.2 jit_solution(3061286931920469969)
XLA Ops:
  29.2 19.1 %all-to-all-done = bf16[4,128,1792]{2,1,0:T(8,128)(2,1)} async-done(((bf16[4,128,1792]{2,1,0:T(8,128)(2,1)}), bf16[4,128,1792]{2,1,0:T(8,128)(2,1)}, u32[]{:S(2)}, u32[]{:S(2)}) %all-to-all-start) | async-done | bytes 1835040 | tf_op jit(solution)/shard_map/all_to_all | solution.py:713
  53.2 22.5 %collective-permute-done.2 = bf16[512,2048]{1,0:T(8,128)(2,1)} collective-permute-done((bf16[512,2048]{1,0:T(8,128)(2,1)}, bf16[512,2048]{1,0:T(8,128)(2,1)}, u32[]{:S(2)}, u32[]{:S(2)}) %collective-permute-start.2) | collective-permute-done | bytes 2097184 | tf_op jit(solution)/shard_map/ppermute | solution.py:562
  80.1 21.4 %collective-permute-done.1 = bf16[512,2048]{1,0:T(8,128)(2,1)} collective-permute-done((bf16[512,2048]{1,0:T(8,128)(2,1)}, bf16[512,2048]{1,0:T(8,128)(2,1)}, u32[]{:S(2)}, u32[]{:S(2)}) %collective-permute-start.1) | collective-permute-done | bytes 2097184 | tf_op jit(solution)/shard_map/ppermute | solution.py:559
  106.5 15.6 %collective-permute-done.3 = bf16[256,2048]{1,0:T(8,128)(2,1)S(1)} collective-permute-done((bf16[256,2048]{1,0:T(8,128)(2,1)S(1)}, bf16[256,2048]{1,0:T(8,128)(2,1)S(1)}, u32[]{:S(2)}, u32[]{:S(2)}) %collective-permute-start.3) | collective-permute-done | bytes 1048608 | tf_op jit(solution)/shard_map/ppermute | solution.py:559
  163.5 6.8 %add_convert_fusion.12 = bf16[1024,768]{1,0:T(8,128)(2,1)S(1)} fusion(bf16[1024,2048]{1,0:T(8,128)(2,1)} %copy-done.21, bf16[2048,768]{1,0:T(8,128)(2,1)} %all-gather.6.cloned.1.call-done.refs_2_, f32[768]{0:T(1024)S(1)} %add.267), kind=kOutput, calls=%fused_computation.29 | convolution fusion | flops 3222798336 | bytes 8915968 | tf_op jit(solution)/shard_map/dot_general | solution.py:19
  178.7 18.9 %shard_map.274 = bf16[2,4,256,256]{3,2,1,0:T(8,128)(2,1)S(1)} custom-call(s32[3,4]{1,0:T(4,128)S(1)} %add_add_fusion.2.order_ref.a, s32[2]{0:T(128)S(1)} %pad_add_fusion.prefix_ref.b, f32[4]{0:T(128)S(1)} %fusion.88.slope_ref, bf16[2,2,2,256,768]{4,3,2,1,0:T(8,128)(2,1)S(1)} %pad_maximum_fusion.2.qkv_ref.d), custom_call_target="tpu_custom_call" | custom-call | flops 12000000000 | bytes 1 | tf_op jit(solution)/shard_map/pallas_call | solution.py:105
  207.1 14.3 %all-to-all-done.1.o_ref = bf16[8,256,256]{2,1,0:T(8,128)(2,1)S(1)} async-done(((bf16[8,256,256]{2,1,0:T(8,128)(2,1)}), bf16[8,256,256]{2,1,0:T(8,128)(2,1)S(1)}, u32[]{:S(2)}, u32[]{:S(2)}) %all-to-all-start.1) | async-done | bytes 1048608 | tf_op jit(solution)/shard_map/all_to_all | solution.py:536
  221.4 9.9 %shard_map.275 = (f32[256,2048]{1,0:T(8,128)S(1)}, bf16[256,2048]{1,0:T(8,128)(2,1)S(1)}) custom-call(s32[8]{0:T(128)S(1)} %fusion.35.table_ref, bf16[8,256,256]{2,1,0:T(8,128)(2,1)S(1)} %all-to-all-done.1.o_ref, bf16[4,256,2048]{2,1,0:T(8,128)(2,1)} %bitcast.22.w_ref, bf16[4,256,2048]{2,1,0:T(8,128)(2,1)} %bitcast.23.v_ref, ...), custom_call_target="tpu_custom_call" | custom-call | flops 1 | bytes 1 | tf_op jit(solution)/shard_map/pallas_call | solution.py:277
  234.7 22.8 %collective-permute-done.15 = bf16[256,2048]{1,0:T(8,128)(2,1)S(1)} collective-permute-done((bf16[256,2048]{1,0:T(8,128)(2,1)S(1)}, bf16[256,2048]{1,0:T(8,128)(2,1)S(1)}, u32[]{:S(2)}, u32[]{:S(2)}) %collective-permute-start.15) | collective-permute-done | bytes 1048608 | tf_op jit(solution)/shard_map/ppermute | solution.py:562
  282.9 7.1 %add_convert_fusion.9 = (bf16[1024,1024]{1,0:T(8,128)(2,1)}, bf16[1024,1024]{1,0:T(8,128)(2,1)S(1)}) fusion(f32[1024]{0:T(1024)S(1)} %bitcast.203, bf16[1024,2048]{1,0:T(8,128)(2,1)S(1)} %copy-done.60, bf16[2048,1024]{1,0:T(8,128)(2,1)S(1)} %get-tuple-element.165), kind=kOutput, calls=%fused_computation.23 | convolution fusion | flops 4307550208 | bytes 12587008 | tf_op jit(solution)/shard_map/dot_general | solution.py:19
  290.0 10.0 %multiply_convert_fusion.2 = (bf16[1024,1024]{1,0:T(8,128)(2,1)S(1)}, bf16[1024,1024]{1,0:T(8,128)(2,1)}) fusion(f32[1024]{0:T(1024)S(1)} %bitcast.204, bf16[1024,2048]{1,0:T(8,128)(2,1)} %collective-permute-done.18, bf16[2048,1024]{1,0:T(8,128)(2,1)S(1)} %get-tuple-element.165), kind=kOutput, calls=%fused_computation.20 | convolution fusion | flops 4307550208 | bytes 12587008 | tf_op jit(solution)/shard_map/dot_general | solution.py:19
  301.3 6.8 %fusion.50 = f32[1024,2048]{1,0:T(8,128)S(1)} fusion(bf16[1024,1024]{1,0:T(8,128)(2,1)S(1)} %get-tuple-element.179, bf16[1024,2048]{1,0:T(8,128)(2,1)} %collective-permute-done.10), kind=kOutput, calls=%fused_computation.161 | convolution fusion | flops 4294967296 | bytes 14680064 | tf_op jit(solution)/shard_map/dot_general | solution.py:19
  308.1 8.3 %add_convert_fusion.1 = bf16[1024,2048]{1,0:T(8,128)(2,1)} fusion(f32[1024,2048]{1,0:T(8,128)S(1)} %fusion.50, bf16[1024,1024]{1,0:T(8,128)(2,1)S(1)} %get-tuple-element.178, bf16[1024,2048]{1,0:T(8,128)(2,1)} %pad_maximum_fusion.1), kind=kOutput, calls=%fused_computation.4 | convolution fusion | flops 4299161600 | bytes 18874368 | tf_op jit(solution)/shard_map/dot_general | solution.py:19
  316.4 8.7 %convert_reduce_fusion.1 = (f32[1024]{0:T(1024)S(1)}, bf16[1024,1024]{1,0:T(8,128)(2,1)S(1)}) fusion(bf16[1024,1024]{1,0:T(8,128)(2,1)} %get-tuple-element.171, bf16[1024,2048]{1,0:T(8,128)(2,1)} %collective-permute-done.10, bf16[1024,2048]{1,0:T(8,128)(2,1)} %copy-done.52), kind=kOutput, calls=%fused_computation.10 | convolution fusion | flops 4300209152 | bytes 12587008 | tf_op jit(solution)/shard_map/dot_general | solution.py:19
  333.3 8.7 %convert_reduce_fusion.2 = (f32[1024]{0:T(1024)S(1)}, bf16[1024,1024]{1,0:T(8,128)(2,1)S(1)}) fusion(bf16[1024,1024]{1,0:T(8,128)(2,1)} %get-tuple-element.170, bf16[1024,2048]{1,0:T(8,128)(2,1)} %pad_maximum_fusion.1, bf16[1024,2048]{1,0:T(8,128)(2,1)} %copy-done.52), kind=kOutput, calls=%fused_computation.11 | convolution fusion | flops 4300209152 | bytes 12587008 | tf_op jit(solution)/shard_map/dot_general | solution.py:19
  387.7 8.8 %collective-permute-done.25.b_ref = bf16[256,2048]{1,0:T(8,128)(2,1)} collective-permute-done((bf16[256,2048]{1,0:T(8,128)(2,1)}, bf16[256,2048]{1,0:T(8,128)(2,1)}, u32[]{:S(2)}, u32[]{:S(2)}) %collective-permute-start.25) | collective-permute-done | bytes 1048608 | tf_op jit(solution)/shard_map/ppermute | solution.py:562
  403.3 14.1 %shard_map.277 = (f32[256,2048]{1,0:T(8,128)}, bf16[256,2048]{1,0:T(8,128)(2,1)S(1)}, f32[4,2048]{1,0:T(4,128)S(1)}, bf16[8,256,256]{2,1,0:T(8,128)(2,1)S(1)}) custom-call(s32[8]{0:T(128)S(1)} %fusion.35.table_ref, bf16[512,2048]{1,0:T(8,128)(2,1)} %copy-done.59, bf16[256,2048]{1,0:T(8,128)(2,1)} %collective-permute-done.25.b_ref, ...), custom_call_target="tpu_custom_call" | custom-call | flops 1 | bytes 1 | tf_op jit(solution)/shard_map/pallas_call | solution.py:330
  445.8 15.1 %shard_map.279._ = bf16[2,2,2,256,768]{4,3,2,1,0:T(8,128)(2,1)S(1)} custom-call(s32[3,4]{1,0:T(4,128)S(1)} %add_add_fusion.2.order_ref.a, s32[2]{0:T(128)S(1)} %pad_add_fusion.prefix_ref.b, f32[2]{0:T(128)S(1)} %get-tuple-element.314.slope_ref, bf16[2,2,2,256,768]{4,3,2,1,0:T(8,128)(2,1)S(1)} %copy-done.24, bf16[2,4,256,256]{3,2,1,0:T(8,128)(2,1)S(1)} %bitcast.166), custom_call_target="tpu_custom_call" | custom-call | flops 12000000000 | bytes 1 | tf_op jit(solution)/shard_map/pallas_call | solution.py:123
  486.3 15.5 %shard_map.280 = bf16[2,2,2,256,768]{4,3,2,1,0:T(8,128)(2,1)S(1)} custom-call(s32[3,4]{1,0:T(4,128)S(1)} %add_add_fusion.2.order_ref.a, s32[2]{0:T(128)S(1)} %pad_add_fusion.prefix_ref.b, f32[2]{0:T(128)S(1)} %get-tuple-element.315.c, bf16[2,2,2,256,768]{4,3,2,1,0:T(8,128)(2,1)S(1)} %copy-done.25, ...), custom_call_target="tpu_custom_call", output_to_operand_aliasing={{}: (5, {})} | custom-call | flops 12000000000 | bytes 1 | tf_op jit(solution)/shard_map/pallas_call | solution.py:123
  555.7 11.4 %collective-permute-done.38 = bf16[256,2048]{1,0:T(8,128)(2,1)} collective-permute-done((bf16[256,2048]{1,0:T(8,128)(2,1)}, bf16[256,2048]{1,0:T(8,128)(2,1)}, u32[]{:S(2)}, u32[]{:S(2)}) %collective-permute-start.38) | collective-permute-done | bytes 1048608 | tf_op jit(solution)/shard_map/ppermute | solution.py:559
  567.1 8.2 %collective-permute-done.37 = bf16[256,2048]{1,0:T(8,128)(2,1)S(1)} collective-permute-done((bf16[256,2048]{1,0:T(8,128)(2,1)S(1)}, bf16[256,2048]{1,0:T(8,128)(2,1)S(1)}, u32[]{:S(2)}, u32[]{:S(2)}) %collective-permute-start.37) | collective-permute-done | bytes 1048608 | tf_op jit(solution)/shard_map/ppermute | solution.py:562
  592.4 6.8 %collective-permute-done.39 = bf16[128,2048]{1,0:T(8,128)(2,1)S(1)} collective-permute-done((bf16[128,2048]{1,0:T(8,128)(2,1)}, bf16[128,2048]{1,0:T(8,128)(2,1)S(1)}, u32[]{:S(2)}, u32[]{:S(2)}) %collective-permute-start.39) | collective-permute-done | bytes 524320 | tf_op jit(solution)/shard_map/ppermute | solution.py:559
  618.9 12.4 %collective-permute-done.44 = bf16[64,2048]{1,0:T(8,128)(2,1)} collective-permute-done((bf16[64,2048]{1,0:T(8,128)(2,1)}, bf16[64,2048]{1,0:T(8,128)(2,1)}, u32[]{:S(2)}, u32[]{:S(2)}) %collective-permute-start.44) | collective-permute-done | bytes 262176 | tf_op jit(solution)/shard_map/ppermute | solution.py:646
  632.7 7.6 %collective-permute-done.41.b_ref = bf16[256,2048]{1,0:T(8,128)(2,1)} collective-permute-done((bf16[256,2048]{1,0:T(8,128)(2,1)}, bf16[256,2048]{1,0:T(8,128)(2,1)}, u32[]{:S(2)}, u32[]{:S(2)}) %collective-permute-start.41) | collective-permute-done | bytes 1048608 | tf_op jit(solution)/shard_map/ppermute | solution.py:562
  (452 shorter events, 342.1 us)
Async XLA Ops:
  7.2 127.8 %all-gather.8.cloned.1.call-start = ((), (), s32[]{:S(2)}) async-start(), calls=%async_computation.14 | async-start | bytes 4259840 | tf_op jit(solution)/shard_map/all_gather | solution.py:710
  20.1 28.1 %all-to-all-start = ((bf16[4,128,1792]{2,1,0:T(8,128)(2,1)}), bf16[4,128,1792]{2,1,0:T(8,128)(2,1)}, u32[]{:S(2)}, u32[]{:S(2)}) async-start(bf16[4,128,1792]{2,1,0:T(8,128)(2,1)} %copy-done.11), calls=%async_computation | async-start | bytes 3670016 | tf_op jit(solution)/shard_map/all_to_all | solution.py:713
  24.7 138.8 %all-gather.6.cloned.1.call-start = ((), (), s32[]{:S(2)}) async-start(), calls=%async_computation.9 | async-start | bytes 3932160 | tf_op jit(solution)/shard_map/all_gather | solution.py:692
  26.2 49.5 %collective-permute-start.2 = (bf16[512,2048]{1,0:T(8,128)(2,1)}, bf16[512,2048]{1,0:T(8,128)(2,1)}, u32[]{:S(2)}, u32[]{:S(2)}) collective-permute-start(bf16[512,2048]{1,0:T(8,128)(2,1)} %pad_maximum_fusion.3), channel_id=1, source_target_pairs={{0,16},{16,0},{1,17},{17,1},{2,18},{18,2},{3,19},{19,3},{4,20},{20... | collective-permute-start | bytes 6291464 | tf_op jit(solution)/shard_map/ppermute | solution.py:562
  52.6 48.9 %collective-permute-start.1 = (bf16[512,2048]{1,0:T(8,128)(2,1)}, bf16[512,2048]{1,0:T(8,128)(2,1)}, u32[]{:S(2)}, u32[]{:S(2)}) collective-permute-start(bf16[512,2048]{1,0:T(8,128)(2,1)} %pad_maximum_fusion.3), channel_id=1, source_target_pairs={{0,2},{1,3},{2,0},{3,1},{4,6},{5,7},{6,4},{7,5},{8,10},{9,11},{10,... | collective-permute-start | bytes 6291464 | tf_op jit(solution)/shard_map/ppermute | solution.py:559
  52.6 214.9 %all-gather.10.cloned.1.call-start = ((), (), s32[]{:S(2)}) async-start(), calls=%async_computation.15 | async-start | bytes 7864320 | tf_op jit(solution)/shard_map/all_gather | solution.py:728
  78.5 43.6 %collective-permute-start.3 = (bf16[256,2048]{1,0:T(8,128)(2,1)S(1)}, bf16[256,2048]{1,0:T(8,128)(2,1)S(1)}, u32[]{:S(2)}, u32[]{:S(2)}) collective-permute-start(bf16[256,2048]{1,0:T(8,128)(2,1)S(1)} %get-tuple-element.294), channel_id=1, source_target_pairs={{0,2},{1,3},{2,0},{3,1},{4,6},{5,7},{6,4},{7,5},{8,10},{9,11},{10,... | collective-permute-start | bytes 3145736 | tf_op jit(solution)/shard_map/ppermute | solution.py:559
  143.4 58.3 %collective-permute-start.10 = (bf16[1024,2048]{1,0:T(8,128)(2,1)}, bf16[1024,2048]{1,0:T(8,128)(2,1)}, u32[]{:S(2)}, u32[]{:S(2)}) collective-permute-start(bf16[1024,2048]{1,0:T(8,128)(2,1)} %pad_maximum_fusion.1), channel_id=1, source_target_pairs={{0,1},{1,0},{2,3},{3,2},{4,5},{5,4},{6,7},{7,6},{8,9},{9,8},{10,11... | collective-permute-start | bytes 12582920 | tf_op jit(solution)/shard_map/ppermute | solution.py:559
  145.2 28.8 %collective-permute-start.5 = (bf16[256,2048]{1,0:T(8,128)(2,1)S(1)}, bf16[256,2048]{1,0:T(8,128)(2,1)}, u32[]{:S(2)}, u32[]{:S(2)}) collective-permute-start(bf16[256,2048]{1,0:T(8,128)(2,1)S(1)} %bitcast.185), channel_id=1, source_target_pairs={{0,16},{16,0},{1,17},{17,1},{2,18},{18,2},{3,19},{19,3},{4,20},{20... | collective-permute-start | bytes 3145736 | tf_op jit(solution)/shard_map/ppermute | solution.py:562
  146.8 27.2 %collective-permute-start.6 = (bf16[256,2048]{1,0:T(8,128)(2,1)S(1)}, bf16[256,2048]{1,0:T(8,128)(2,1)}, u32[]{:S(2)}, u32[]{:S(2)}) collective-permute-start(bf16[256,2048]{1,0:T(8,128)(2,1)S(1)} %bitcast.186), channel_id=1, source_target_pairs={{0,2},{1,3},{2,0},{3,1},{4,6},{5,7},{6,4},{7,5},{8,10},{9,11},{10,... | collective-permute-start | bytes 3145736 | tf_op jit(solution)/shard_map/ppermute | solution.py:559
  175.5 26.2 %collective-permute-start.11 = (bf16[128,2048]{1,0:T(8,128)(2,1)S(1)}, bf16[128,2048]{1,0:T(8,128)(2,1)S(1)}, u32[]{:S(2)}, u32[]{:S(2)}) collective-permute-start(bf16[128,2048]{1,0:T(8,128)(2,1)S(1)} %slice.335), channel_id=1, source_target_pairs={{0,2},{1,3},{2,0},{3,1},{4,6},{5,7},{6,4},{7,5},{8,10},{9,11},{10,... | collective-permute-start | bytes 1572872 | tf_op jit(solution)/shard_map/ppermute | solution.py:559
  207.0 212.4 %reduce-scatter.5.cloned.1.call-start = ((), (), s32[]{:S(2)}) async-start(), calls=%async_computation.10 | async-start | bytes 5242880 | tf_op jit(solution)/shard_map/reduce_scatter | solution.py:788
  333.1 170.4 %reduce-scatter.7.cloned.1.call-start = ((), (), s32[]{:S(2)}) async-start(), calls=%async_computation.11 | async-start | bytes 5242880 | tf_op jit(solution)/shard_map/reduce_scatter | solution.py:800
  423.9 113.6 %reduce-scatter.9.cloned.1.call-start = ((), (), s32[]{:S(2)}) async-start(), calls=%async_computation.12 | async-start | bytes 1966080 | tf_op jit(solution)/shard_map/reduce_scatter | solution.py:845
  440.9 27.7 %collective-permute-start.30 = (bf16[256,2048]{1,0:T(8,128)(2,1)S(1)}, bf16[256,2048]{1,0:T(8,128)(2,1)S(1)}, u32[]{:S(2)}, u32[]{:S(2)}) collective-permute-start(bf16[256,2048]{1,0:T(8,128)(2,1)S(1)} %pad_maximum_fusion.9), channel_id=1, source_target_pairs={{0,16},{16,0},{1,17},{17,1},{2,18},{18,2},{3,19},{19,3},{4,20},{20... | collective-permute-start | bytes 3145736 | tf_op jit(solution)/shard_map/ppermute | solution.py:562
  444.7 58.7 %collective-permute-start.34 = (bf16[256,2048]{1,0:T(8,128)(2,1)S(1)}, bf16[256,2048]{1,0:T(8,128)(2,1)S(1)}, u32[]{:S(2)}, u32[]{:S(2)}) collective-permute-start(bf16[256,2048]{1,0:T(8,128)(2,1)S(1)} %copy-done.37), channel_id=1, source_target_pairs={{0,16},{16,0},{1,17},{17,1},{2,18},{18,2},{3,19},{19,3},{4,20},{20... | collective-permute-start | bytes 3145736 | tf_op jit(solution)/shard_map/ppermute | solution.py:699
  515.4 32.2 %all-to-all-start.3 = ((bf16[8,128,1024]{2,1,0:T(8,128)(2,1)}), bf16[8,128,1024]{2,1,0:T(8,128)(2,1)S(1)}, u32[]{:S(2)}, u32[]{:S(2)}) async-start(bf16[8,128,1024]{2,1,0:T(8,128)(2,1)} %pad_maximum_fusion.4), calls=%async_computation.5 | async-start | bytes 4194304 | tf_op jit(solution)/shard_map/all_to_all | solution.py:696
  519.0 64.2 %reduce-scatter.11.cloned.1.call-start = ((), (), s32[]{:S(2)}) async-start(), calls=%async_computation.13 | async-start | bytes 2621440 | tf_op jit(solution)/shard_map/reduce_scatter | solution.py:847
  525.2 42.0 %collective-permute-start.38 = (bf16[256,2048]{1,0:T(8,128)(2,1)}, bf16[256,2048]{1,0:T(8,128)(2,1)}, u32[]{:S(2)}, u32[]{:S(2)}) collective-permute-start(bf16[256,2048]{1,0:T(8,128)(2,1)} %pad_maximum_fusion.12), channel_id=1, source_target_pairs={{0,2},{1,3},{2,0},{3,1},{4,6},{5,7},{6,4},{7,5},{8,10},{9,11},{10,... | collective-permute-start | bytes 3145736 | tf_op jit(solution)/shard_map/ppermute | solution.py:559
  547.5 30.6 %collective-permute-start.35 = (bf16[512,2048]{1,0:T(8,128)(2,1)}, bf16[512,2048]{1,0:T(8,128)(2,1)S(1)}, u32[]{:S(2)}, u32[]{:S(2)}) collective-permute-start(bf16[512,2048]{1,0:T(8,128)(2,1)} %convolution_convert_fusion.5), channel_id=1, source_target_pairs={{0,1},{1,0},{2,3},{3,2},{4,5},{5,4},{6,7},{7,6},{8,9},{9,8},{10,11... | collective-permute-start | bytes 6291464 | tf_op jit(solution)/shard_map/ppermute | solution.py:559
  551.4 28.6 %collective-permute-start.36 = (bf16[512,2048]{1,0:T(8,128)(2,1)}, bf16[512,2048]{1,0:T(8,128)(2,1)S(1)}, u32[]{:S(2)}, u32[]{:S(2)}) collective-permute-start(bf16[512,2048]{1,0:T(8,128)(2,1)} %convolution_convert_fusion.4), channel_id=1, source_target_pairs={{0,1},{1,0},{2,3},{3,2},{4,5},{5,4},{6,7},{7,6},{8,9},{9,8},{10,11... | collective-permute-start | bytes 6291464 | tf_op jit(solution)/shard_map/ppermute | solution.py:559
  588.7 59.5 %all-to-all-start.4 = ((bf16[8,128,896]{2,1,0:T(8,128)(2,1)}), bf16[8,128,896]{2,1,0:T(8,128)(2,1)S(1)}, u32[]{:S(2)}, u32[]{:S(2)}) async-start(bf16[8,128,896]{2,1,0:T(8,128)(2,1)} %pad_maximum_fusion.5), calls=%async_computation.8 | async-start | bytes 3670016 | tf_op jit(solution)/shard_map/all_to_all | solution.py:696
  602.5 37.8 %collective-permute-start.41 = (bf16[256,2048]{1,0:T(8,128)(2,1)}, bf16[256,2048]{1,0:T(8,128)(2,1)}, u32[]{:S(2)}, u32[]{:S(2)}) collective-permute-start(bf16[256,2048]{1,0:T(8,128)(2,1)} %pad_maximum_fusion.13), channel_id=1, source_target_pairs={{0,16},{16,0},{1,17},{17,1},{2,18},{18,2},{3,19},{19,3},{4,20},{20... | collective-permute-start | bytes 3145736 | tf_op jit(solution)/shard_map/ppermute | solution.py:562
  605.1 35.1 %collective-permute-start.42 = (bf16[256,2048]{1,0:T(8,128)(2,1)}, bf16[256,2048]{1,0:T(8,128)(2,1)S(1)}, u32[]{:S(2)}, u32[]{:S(2)}) collective-permute-start(bf16[256,2048]{1,0:T(8,128)(2,1)} %pad_maximum_fusion.14), channel_id=1, source_target_pairs={{0,2},{1,3},{2,0},{3,1},{4,6},{5,7},{6,4},{7,5},{8,10},{9,11},{10,... | collective-permute-start | bytes 3145736 | tf_op jit(solution)/shard_map/ppermute | solution.py:559
  (125 other events, 1189.2 us)
Sparse Core Ops, SparseCore 0:
  17.1 70.5 all-gather.7
  89.2 62.0 all-gather.5
  153.5 113.9 all-gather.9
  333.2 76.7 reduce-scatter.4
  412.2 77.2 reduce-scatter.6
  491.7 35.8 reduce-scatter.8
  537.7 43.9 reduce-scatter.10

commit v7 on v6

--- a/solution.py
+++ b/solution.py
@@ -107,7 +107,7 @@
         out_shape=jax.ShapeDtypeStruct((n, C, T, pairs * 128), BF),
         grid_spec=pltpu.PrefetchScalarGridSpec(num_scalar_prefetch=3, grid=(n, pairs), in_specs=[near], out_specs=true),
         compiler_params=vmem(32),
-        cost_estimate=pl.CostEstimate(flops=12 * 10**9, transcendentals=0, bytes_accessed=1),
+        cost_estimate=pl.CostEstimate(flops=6 * 10**9, transcendentals=0, bytes_accessed=1),
     )(order, prefix, slopes, qkv)
 
 
@@ -132,7 +132,7 @@
         ),
         input_output_aliases=aliases,
         compiler_params=vmem(32),
-        cost_estimate=pl.CostEstimate(flops=12 * 10**9, transcendentals=0, bytes_accessed=1),
+        cost_estimate=pl.CostEstimate(flops=6 * 10**9, transcendentals=0, bytes_accessed=1),
     )(order, prefix, slopes, qkv, d_out, *more)
 
 

time: 664 us -> 662 us (level)
    unnamed x181 -> x179, local copies, waits for them, and re-layouts: 48 us -> 47.8 us
  transfers between devices with their start and end apart: 59 -> 59, of which waited for: 26 -> 26; matrix products, arithmetic and copies ran while one was open for 27% -> 27% of each run, Pallas kernels for 15% -> 16%
where the time goes in v7:
time: 662 us; the launch traced here: 657 us
  waiting for transfers between devices  196 us (30%)
  matrix products  132 us (20%)
  Pallas kernels  104 us (16%)
  local copies, waits for them, and re-layouts  86.7 us (13%)
  starting transfers between devices  67.3 us (10%)
  other arithmetic  54.3 us (8%)
  between operations  16.5 us (2%)
    dot_general x26, matrix products, dot(): lax.dot_general(a, b, (((ca,), (cb,)), ((), ())), preferred_element_type=...  132 us
    ppermute x15, waiting for transfers between devices, x(): return lax.ppermute(x, 'rep', [(0, 1), (1, 0)])  77.4 us
    ppermute x27, waiting for transfers between devices, over(): return lax.ppermute(x, 'ctx', [(i, i ^ d) for i in range(4)])  65.5 us
    unnamed x179, local copies, waits for them, and re-layouts  47.8 us
    pallas_call x2, Pallas kernels, attention_backward(): pl.pallas_call(kernel, out_shape=jax.ShapeDtypeStruct(qkv.shape, BF), gri...  30.5 us
    ppermute x15, starting transfers between devices, x(): return lax.ppermute(x, 'rep', [(0, 1), (1, 0)])  22.3 us
    all_to_all x1, waiting for transfers between devices, shards(): lax.all_to_all(pack(F, C, rep, joined_weight, expand_weight), 'ctx', 0, 0...  19.1 us
    pallas_call x1, Pallas kernels, attention_forward(): pl.pallas_call(forward_kernel, out_shape=jax.ShapeDtypeStruct((n, C, T, p...  18.9 us
  transfers between devices with their start and end apart: 59, of which 26 were waited for; matrix products, arithmetic and copies ran while one was open for 27% of the time, Pallas kernels for 16%

profile of v7, /device:TPU:0, one launch (start us, length us, event | category | flops | bytes accessed | tf_op | source)
XLA Modules:
  0.0 656.6 jit_solution(3787362503793023337)
XLA Ops:
  29.1 19.1 %all-to-all-done = bf16[4,128,1792]{2,1,0:T(8,128)(2,1)} async-done(((bf16[4,128,1792]{2,1,0:T(8,128)(2,1)}), bf16[4,128,1792]{2,1,0:T(8,128)(2,1)}, u32[]{:S(2)}, u32[]{:S(2)}) %all-to-all-start) | async-done | bytes 1835040 | tf_op jit(solution)/shard_map/all_to_all | solution.py:713
  53.2 22.5 %collective-permute-done.2 = bf16[512,2048]{1,0:T(8,128)(2,1)} collective-permute-done((bf16[512,2048]{1,0:T(8,128)(2,1)}, bf16[512,2048]{1,0:T(8,128)(2,1)}, u32[]{:S(2)}, u32[]{:S(2)}) %collective-permute-start.2) | collective-permute-done | bytes 2097184 | tf_op jit(solution)/shard_map/ppermute | solution.py:562
  80.1 21.4 %collective-permute-done.1 = bf16[512,2048]{1,0:T(8,128)(2,1)} collective-permute-done((bf16[512,2048]{1,0:T(8,128)(2,1)}, bf16[512,2048]{1,0:T(8,128)(2,1)}, u32[]{:S(2)}, u32[]{:S(2)}) %collective-permute-start.1) | collective-permute-done | bytes 2097184 | tf_op jit(solution)/shard_map/ppermute | solution.py:559
  106.5 15.5 %collective-permute-done.3 = bf16[256,2048]{1,0:T(8,128)(2,1)S(1)} collective-permute-done((bf16[256,2048]{1,0:T(8,128)(2,1)S(1)}, bf16[256,2048]{1,0:T(8,128)(2,1)S(1)}, u32[]{:S(2)}, u32[]{:S(2)}) %collective-permute-start.3) | collective-permute-done | bytes 1048608 | tf_op jit(solution)/shard_map/ppermute | solution.py:559
  163.4 6.8 %add_convert_fusion.12 = bf16[1024,768]{1,0:T(8,128)(2,1)S(1)} fusion(bf16[1024,2048]{1,0:T(8,128)(2,1)} %copy-done.21, bf16[2048,768]{1,0:T(8,128)(2,1)} %all-gather.6.cloned.1.call-done.refs_2_, f32[768]{0:T(1024)S(1)} %add.267), kind=kOutput, calls=%fused_computation.29 | convolution fusion | flops 3222798336 | bytes 8915968 | tf_op jit(solution)/shard_map/dot_general | solution.py:19
  178.6 18.9 %shard_map.274 = bf16[2,4,256,256]{3,2,1,0:T(8,128)(2,1)S(1)} custom-call(s32[3,4]{1,0:T(4,128)S(1)} %add_add_fusion.2.order_ref.a, s32[2]{0:T(128)S(1)} %pad_add_fusion.prefix_ref.b, f32[4]{0:T(128)S(1)} %fusion.88.slope_ref, bf16[2,2,2,256,768]{4,3,2,1,0:T(8,128)(2,1)S(1)} %pad_maximum_fusion.2.qkv_ref.d), custom_call_target="tpu_custom_call" | custom-call | flops 6000000000 | bytes 1 | tf_op jit(solution)/shard_map/pallas_call | solution.py:105
  207.0 14.3 %all-to-all-done.1.o_ref = bf16[8,256,256]{2,1,0:T(8,128)(2,1)S(1)} async-done(((bf16[8,256,256]{2,1,0:T(8,128)(2,1)}), bf16[8,256,256]{2,1,0:T(8,128)(2,1)S(1)}, u32[]{:S(2)}, u32[]{:S(2)}) %all-to-all-start.1) | async-done | bytes 1048608 | tf_op jit(solution)/shard_map/all_to_all | solution.py:536
  221.3 9.9 %shard_map.275 = (f32[256,2048]{1,0:T(8,128)S(1)}, bf16[256,2048]{1,0:T(8,128)(2,1)S(1)}) custom-call(s32[8]{0:T(128)S(1)} %fusion.35.table_ref, bf16[8,256,256]{2,1,0:T(8,128)(2,1)S(1)} %all-to-all-done.1.o_ref, bf16[4,256,2048]{2,1,0:T(8,128)(2,1)} %bitcast.22.w_ref, bf16[4,256,2048]{2,1,0:T(8,128)(2,1)} %bitcast.23.v_ref, ...), custom_call_target="tpu_custom_call" | custom-call | flops 1 | bytes 1 | tf_op jit(solution)/shard_map/pallas_call | solution.py:277
  234.5 22.8 %collective-permute-done.15 = bf16[256,2048]{1,0:T(8,128)(2,1)S(1)} collective-permute-done((bf16[256,2048]{1,0:T(8,128)(2,1)S(1)}, bf16[256,2048]{1,0:T(8,128)(2,1)S(1)}, u32[]{:S(2)}, u32[]{:S(2)}) %collective-permute-start.15) | collective-permute-done | bytes 1048608 | tf_op jit(solution)/shard_map/ppermute | solution.py:562
  282.7 7.1 %add_convert_fusion.9 = (bf16[1024,1024]{1,0:T(8,128)(2,1)}, bf16[1024,1024]{1,0:T(8,128)(2,1)S(1)}) fusion(f32[1024]{0:T(1024)S(1)} %bitcast.203, bf16[1024,2048]{1,0:T(8,128)(2,1)S(1)} %copy-done.60, bf16[2048,1024]{1,0:T(8,128)(2,1)S(1)} %get-tuple-element.165), kind=kOutput, calls=%fused_computation.23 | convolution fusion | flops 4307550208 | bytes 12587008 | tf_op jit(solution)/shard_map/dot_general | solution.py:19
  289.8 10.0 %multiply_convert_fusion.2 = (bf16[1024,1024]{1,0:T(8,128)(2,1)S(1)}, bf16[1024,1024]{1,0:T(8,128)(2,1)}) fusion(f32[1024]{0:T(1024)S(1)} %bitcast.204, bf16[1024,2048]{1,0:T(8,128)(2,1)} %collective-permute-done.18, bf16[2048,1024]{1,0:T(8,128)(2,1)S(1)} %get-tuple-element.165), kind=kOutput, calls=%fused_computation.20 | convolution fusion | flops 4307550208 | bytes 12587008 | tf_op jit(solution)/shard_map/dot_general | solution.py:19
  301.1 6.8 %fusion.50 = f32[1024,2048]{1,0:T(8,128)S(1)} fusion(bf16[1024,1024]{1,0:T(8,128)(2,1)S(1)} %get-tuple-element.179, bf16[1024,2048]{1,0:T(8,128)(2,1)} %collective-permute-done.10), kind=kOutput, calls=%fused_computation.161 | convolution fusion | flops 4294967296 | bytes 14680064 | tf_op jit(solution)/shard_map/dot_general | solution.py:19
  307.9 8.3 %add_convert_fusion.1 = bf16[1024,2048]{1,0:T(8,128)(2,1)} fusion(f32[1024,2048]{1,0:T(8,128)S(1)} %fusion.50, bf16[1024,1024]{1,0:T(8,128)(2,1)S(1)} %get-tuple-element.178, bf16[1024,2048]{1,0:T(8,128)(2,1)} %pad_maximum_fusion.1), kind=kOutput, calls=%fused_computation.4 | convolution fusion | flops 4299161600 | bytes 18874368 | tf_op jit(solution)/shard_map/dot_general | solution.py:19
  316.3 8.7 %convert_reduce_fusion.1 = (f32[1024]{0:T(1024)S(1)}, bf16[1024,1024]{1,0:T(8,128)(2,1)S(1)}) fusion(bf16[1024,1024]{1,0:T(8,128)(2,1)} %get-tuple-element.171, bf16[1024,2048]{1,0:T(8,128)(2,1)} %collective-permute-done.10, bf16[1024,2048]{1,0:T(8,128)(2,1)} %copy-done.52), kind=kOutput, calls=%fused_computation.10 | convolution fusion | flops 4300209152 | bytes 12587008 | tf_op jit(solution)/shard_map/dot_general | solution.py:19
  333.2 8.7 %convert_reduce_fusion.2 = (f32[1024]{0:T(1024)S(1)}, bf16[1024,1024]{1,0:T(8,128)(2,1)S(1)}) fusion(bf16[1024,1024]{1,0:T(8,128)(2,1)} %get-tuple-element.170, bf16[1024,2048]{1,0:T(8,128)(2,1)} %pad_maximum_fusion.1, bf16[1024,2048]{1,0:T(8,128)(2,1)} %copy-done.52), kind=kOutput, calls=%fused_computation.11 | convolution fusion | flops 4300209152 | bytes 12587008 | tf_op jit(solution)/shard_map/dot_general | solution.py:19
  387.6 8.8 %collective-permute-done.25.b_ref = bf16[256,2048]{1,0:T(8,128)(2,1)} collective-permute-done((bf16[256,2048]{1,0:T(8,128)(2,1)}, bf16[256,2048]{1,0:T(8,128)(2,1)}, u32[]{:S(2)}, u32[]{:S(2)}) %collective-permute-start.25) | collective-permute-done | bytes 1048608 | tf_op jit(solution)/shard_map/ppermute | solution.py:562
  402.2 14.2 %shard_map.277 = (f32[256,2048]{1,0:T(8,128)}, bf16[256,2048]{1,0:T(8,128)(2,1)S(1)}, f32[4,2048]{1,0:T(4,128)S(1)}, bf16[8,256,256]{2,1,0:T(8,128)(2,1)S(1)}) custom-call(s32[8]{0:T(128)S(1)} %fusion.35.table_ref, bf16[512,2048]{1,0:T(8,128)(2,1)} %copy-done.59, bf16[256,2048]{1,0:T(8,128)(2,1)} %collective-permute-done.25.b_ref, ...), custom_call_target="tpu_custom_call" | custom-call | flops 1 | bytes 1 | tf_op jit(solution)/shard_map/pallas_call | solution.py:330
  444.0 15.1 %shard_map.279._ = bf16[2,2,2,256,768]{4,3,2,1,0:T(8,128)(2,1)S(1)} custom-call(s32[3,4]{1,0:T(4,128)S(1)} %add_add_fusion.2.order_ref.a, s32[2]{0:T(128)S(1)} %pad_add_fusion.prefix_ref.b, f32[2]{0:T(128)S(1)} %get-tuple-element.314.slope_ref, bf16[2,2,2,256,768]{4,3,2,1,0:T(8,128)(2,1)S(1)} %copy-done.24, bf16[2,4,256,256]{3,2,1,0:T(8,128)(2,1)S(1)} %bitcast.166), custom_call_target="tpu_custom_call" | custom-call | flops 6000000000 | bytes 1 | tf_op jit(solution)/shard_map/pallas_call | solution.py:123
  483.4 15.5 %shard_map.280 = bf16[2,2,2,256,768]{4,3,2,1,0:T(8,128)(2,1)S(1)} custom-call(s32[3,4]{1,0:T(4,128)S(1)} %add_add_fusion.2.order_ref.a, s32[2]{0:T(128)S(1)} %pad_add_fusion.prefix_ref.b, f32[2]{0:T(128)S(1)} %get-tuple-element.315.c, bf16[2,2,2,256,768]{4,3,2,1,0:T(8,128)(2,1)S(1)} %copy-done.25, ...), custom_call_target="tpu_custom_call", output_to_operand_aliasing={{}: (5, {})} | custom-call | flops 6000000000 | bytes 1 | tf_op jit(solution)/shard_map/pallas_call | solution.py:123
  553.2 11.7 %collective-permute-done.38 = bf16[256,2048]{1,0:T(8,128)(2,1)} collective-permute-done((bf16[256,2048]{1,0:T(8,128)(2,1)}, bf16[256,2048]{1,0:T(8,128)(2,1)}, u32[]{:S(2)}, u32[]{:S(2)}) %collective-permute-start.38) | collective-permute-done | bytes 1048608 | tf_op jit(solution)/shard_map/ppermute | solution.py:559
  564.9 7.9 %collective-permute-done.37 = bf16[256,2048]{1,0:T(8,128)(2,1)S(1)} collective-permute-done((bf16[256,2048]{1,0:T(8,128)(2,1)S(1)}, bf16[256,2048]{1,0:T(8,128)(2,1)S(1)}, u32[]{:S(2)}, u32[]{:S(2)}) %collective-permute-start.37) | collective-permute-done | bytes 1048608 | tf_op jit(solution)/shard_map/ppermute | solution.py:562
  590.0 6.7 %collective-permute-done.39 = bf16[128,2048]{1,0:T(8,128)(2,1)S(1)} collective-permute-done((bf16[128,2048]{1,0:T(8,128)(2,1)}, bf16[128,2048]{1,0:T(8,128)(2,1)S(1)}, u32[]{:S(2)}, u32[]{:S(2)}) %collective-permute-start.39) | collective-permute-done | bytes 524320 | tf_op jit(solution)/shard_map/ppermute | solution.py:559
  616.6 12.5 %collective-permute-done.44 = bf16[64,2048]{1,0:T(8,128)(2,1)} collective-permute-done((bf16[64,2048]{1,0:T(8,128)(2,1)}, bf16[64,2048]{1,0:T(8,128)(2,1)}, u32[]{:S(2)}, u32[]{:S(2)}) %collective-permute-start.44) | collective-permute-done | bytes 262176 | tf_op jit(solution)/shard_map/ppermute | solution.py:646
  630.4 7.4 %collective-permute-done.41.b_ref = bf16[256,2048]{1,0:T(8,128)(2,1)} collective-permute-done((bf16[256,2048]{1,0:T(8,128)(2,1)}, bf16[256,2048]{1,0:T(8,128)(2,1)}, u32[]{:S(2)}, u32[]{:S(2)}) %collective-permute-start.41) | collective-permute-done | bytes 1048608 | tf_op jit(solution)/shard_map/ppermute | solution.py:562
  (450 shorter events, 339.8 us)
Async XLA Ops:
  7.2 127.8 %all-gather.8.cloned.1.call-start = ((), (), s32[]{:S(2)}) async-start(), calls=%async_computation.14 | async-start | bytes 4259840 | tf_op jit(solution)/shard_map/all_gather | solution.py:710
  20.1 28.1 %all-to-all-start = ((bf16[4,128,1792]{2,1,0:T(8,128)(2,1)}), bf16[4,128,1792]{2,1,0:T(8,128)(2,1)}, u32[]{:S(2)}, u32[]{:S(2)}) async-start(bf16[4,128,1792]{2,1,0:T(8,128)(2,1)} %copy-done.11), calls=%async_computation | async-start | bytes 3670016 | tf_op jit(solution)/shard_map/all_to_all | solution.py:713
  24.6 138.8 %all-gather.6.cloned.1.call-start = ((), (), s32[]{:S(2)}) async-start(), calls=%async_computation.9 | async-start | bytes 3932160 | tf_op jit(solution)/shard_map/all_gather | solution.py:692
  26.2 49.5 %collective-permute-start.2 = (bf16[512,2048]{1,0:T(8,128)(2,1)}, bf16[512,2048]{1,0:T(8,128)(2,1)}, u32[]{:S(2)}, u32[]{:S(2)}) collective-permute-start(bf16[512,2048]{1,0:T(8,128)(2,1)} %pad_maximum_fusion.3), channel_id=1, source_target_pairs={{0,16},{16,0},{1,17},{17,1},{2,18},{18,2},{3,19},{19,3},{4,20},{20... | collective-permute-start | bytes 6291464 | tf_op jit(solution)/shard_map/ppermute | solution.py:562
  52.6 48.9 %collective-permute-start.1 = (bf16[512,2048]{1,0:T(8,128)(2,1)}, bf16[512,2048]{1,0:T(8,128)(2,1)}, u32[]{:S(2)}, u32[]{:S(2)}) collective-permute-start(bf16[512,2048]{1,0:T(8,128)(2,1)} %pad_maximum_fusion.3), channel_id=1, source_target_pairs={{0,2},{1,3},{2,0},{3,1},{4,6},{5,7},{6,4},{7,5},{8,10},{9,11},{10,... | collective-permute-start | bytes 6291464 | tf_op jit(solution)/shard_map/ppermute | solution.py:559
  52.6 214.9 %all-gather.10.cloned.1.call-start = ((), (), s32[]{:S(2)}) async-start(), calls=%async_computation.15 | async-start | bytes 7864320 | tf_op jit(solution)/shard_map/all_gather | solution.py:728
  78.4 43.6 %collective-permute-start.3 = (bf16[256,2048]{1,0:T(8,128)(2,1)S(1)}, bf16[256,2048]{1,0:T(8,128)(2,1)S(1)}, u32[]{:S(2)}, u32[]{:S(2)}) collective-permute-start(bf16[256,2048]{1,0:T(8,128)(2,1)S(1)} %get-tuple-element.294), channel_id=1, source_target_pairs={{0,2},{1,3},{2,0},{3,1},{4,6},{5,7},{6,4},{7,5},{8,10},{9,11},{10,... | collective-permute-start | bytes 3145736 | tf_op jit(solution)/shard_map/ppermute | solution.py:559
  143.4 58.2 %collective-permute-start.10 = (bf16[1024,2048]{1,0:T(8,128)(2,1)}, bf16[1024,2048]{1,0:T(8,128)(2,1)}, u32[]{:S(2)}, u32[]{:S(2)}) collective-permute-start(bf16[1024,2048]{1,0:T(8,128)(2,1)} %pad_maximum_fusion.1), channel_id=1, source_target_pairs={{0,1},{1,0},{2,3},{3,2},{4,5},{5,4},{6,7},{7,6},{8,9},{9,8},{10,11... | collective-permute-start | bytes 12582920 | tf_op jit(solution)/shard_map/ppermute | solution.py:559
  145.1 28.8 %collective-permute-start.5 = (bf16[256,2048]{1,0:T(8,128)(2,1)S(1)}, bf16[256,2048]{1,0:T(8,128)(2,1)}, u32[]{:S(2)}, u32[]{:S(2)}) collective-permute-start(bf16[256,2048]{1,0:T(8,128)(2,1)S(1)} %bitcast.185), channel_id=1, source_target_pairs={{0,16},{16,0},{1,17},{17,1},{2,18},{18,2},{3,19},{19,3},{4,20},{20... | collective-permute-start | bytes 3145736 | tf_op jit(solution)/shard_map/ppermute | solution.py:562
  146.8 27.2 %collective-permute-start.6 = (bf16[256,2048]{1,0:T(8,128)(2,1)S(1)}, bf16[256,2048]{1,0:T(8,128)(2,1)}, u32[]{:S(2)}, u32[]{:S(2)}) collective-permute-start(bf16[256,2048]{1,0:T(8,128)(2,1)S(1)} %bitcast.186), channel_id=1, source_target_pairs={{0,2},{1,3},{2,0},{3,1},{4,6},{5,7},{6,4},{7,5},{8,10},{9,11},{10,... | collective-permute-start | bytes 3145736 | tf_op jit(solution)/shard_map/ppermute | solution.py:559
  175.5 26.1 %collective-permute-start.11 = (bf16[128,2048]{1,0:T(8,128)(2,1)S(1)}, bf16[128,2048]{1,0:T(8,128)(2,1)S(1)}, u32[]{:S(2)}, u32[]{:S(2)}) collective-permute-start(bf16[128,2048]{1,0:T(8,128)(2,1)S(1)} %slice.335), channel_id=1, source_target_pairs={{0,2},{1,3},{2,0},{3,1},{4,6},{5,7},{6,4},{7,5},{8,10},{9,11},{10,... | collective-permute-start | bytes 1572872 | tf_op jit(solution)/shard_map/ppermute | solution.py:559
  206.9 211.5 %reduce-scatter.5.cloned.1.call-start = ((), (), s32[]{:S(2)}) async-start(), calls=%async_computation.10 | async-start | bytes 5242880 | tf_op jit(solution)/shard_map/reduce_scatter | solution.py:788
  333.0 168.4 %reduce-scatter.7.cloned.1.call-start = ((), (), s32[]{:S(2)}) async-start(), calls=%async_computation.11 | async-start | bytes 5242880 | tf_op jit(solution)/shard_map/reduce_scatter | solution.py:800
  422.1 113.0 %reduce-scatter.9.cloned.1.call-start = ((), (), s32[]{:S(2)}) async-start(), calls=%async_computation.12 | async-start | bytes 1966080 | tf_op jit(solution)/shard_map/reduce_scatter | solution.py:845
  439.1 27.7 %collective-permute-start.30 = (bf16[256,2048]{1,0:T(8,128)(2,1)S(1)}, bf16[256,2048]{1,0:T(8,128)(2,1)S(1)}, u32[]{:S(2)}, u32[]{:S(2)}) collective-permute-start(bf16[256,2048]{1,0:T(8,128)(2,1)S(1)} %pad_maximum_fusion.9), channel_id=1, source_target_pairs={{0,16},{16,0},{1,17},{17,1},{2,18},{18,2},{3,19},{19,3},{4,20},{20... | collective-permute-start | bytes 3145736 | tf_op jit(solution)/shard_map/ppermute | solution.py:562
  442.9 58.5 %collective-permute-start.34 = (bf16[256,2048]{1,0:T(8,128)(2,1)S(1)}, bf16[256,2048]{1,0:T(8,128)(2,1)S(1)}, u32[]{:S(2)}, u32[]{:S(2)}) collective-permute-start(bf16[256,2048]{1,0:T(8,128)(2,1)S(1)} %copy-done.37), channel_id=1, source_target_pairs={{0,16},{16,0},{1,17},{17,1},{2,18},{18,2},{3,19},{19,3},{4,20},{20... | collective-permute-start | bytes 3145736 | tf_op jit(solution)/shard_map/ppermute | solution.py:699
  513.1 31.9 %all-to-all-start.3 = ((bf16[8,128,1024]{2,1,0:T(8,128)(2,1)}), bf16[8,128,1024]{2,1,0:T(8,128)(2,1)S(1)}, u32[]{:S(2)}, u32[]{:S(2)}) async-start(bf16[8,128,1024]{2,1,0:T(8,128)(2,1)} %pad_maximum_fusion.4), calls=%async_computation.5 | async-start | bytes 4194304 | tf_op jit(solution)/shard_map/all_to_all | solution.py:696
  516.7 63.8 %reduce-scatter.11.cloned.1.call-start = ((), (), s32[]{:S(2)}) async-start(), calls=%async_computation.13 | async-start | bytes 2621440 | tf_op jit(solution)/shard_map/reduce_scatter | solution.py:847
  522.8 42.1 %collective-permute-start.38 = (bf16[256,2048]{1,0:T(8,128)(2,1)}, bf16[256,2048]{1,0:T(8,128)(2,1)}, u32[]{:S(2)}, u32[]{:S(2)}) collective-permute-start(bf16[256,2048]{1,0:T(8,128)(2,1)} %pad_maximum_fusion.12), channel_id=1, source_target_pairs={{0,2},{1,3},{2,0},{3,1},{4,6},{5,7},{6,4},{7,5},{8,10},{9,11},{10,... | collective-permute-start | bytes 3145736 | tf_op jit(solution)/shard_map/ppermute | solution.py:559
  545.0 30.5 %collective-permute-start.35 = (bf16[512,2048]{1,0:T(8,128)(2,1)}, bf16[512,2048]{1,0:T(8,128)(2,1)S(1)}, u32[]{:S(2)}, u32[]{:S(2)}) collective-permute-start(bf16[512,2048]{1,0:T(8,128)(2,1)} %convolution_convert_fusion.5), channel_id=1, source_target_pairs={{0,1},{1,0},{2,3},{3,2},{4,5},{5,4},{6,7},{7,6},{8,9},{9,8},{10,11... | collective-permute-start | bytes 6291464 | tf_op jit(solution)/shard_map/ppermute | solution.py:559
  548.8 28.6 %collective-permute-start.36 = (bf16[512,2048]{1,0:T(8,128)(2,1)}, bf16[512,2048]{1,0:T(8,128)(2,1)S(1)}, u32[]{:S(2)}, u32[]{:S(2)}) collective-permute-start(bf16[512,2048]{1,0:T(8,128)(2,1)} %convolution_convert_fusion.4), channel_id=1, source_target_pairs={{0,1},{1,0},{2,3},{3,2},{4,5},{5,4},{6,7},{7,6},{8,9},{9,8},{10,11... | collective-permute-start | bytes 6291464 | tf_op jit(solution)/shard_map/ppermute | solution.py:559
  586.2 59.3 %all-to-all-start.4 = ((bf16[8,128,896]{2,1,0:T(8,128)(2,1)}), bf16[8,128,896]{2,1,0:T(8,128)(2,1)S(1)}, u32[]{:S(2)}, u32[]{:S(2)}) async-start(bf16[8,128,896]{2,1,0:T(8,128)(2,1)} %pad_maximum_fusion.5), calls=%async_computation.8 | async-start | bytes 3670016 | tf_op jit(solution)/shard_map/all_to_all | solution.py:696
  599.9 37.8 %collective-permute-start.41 = (bf16[256,2048]{1,0:T(8,128)(2,1)}, bf16[256,2048]{1,0:T(8,128)(2,1)}, u32[]{:S(2)}, u32[]{:S(2)}) collective-permute-start(bf16[256,2048]{1,0:T(8,128)(2,1)} %pad_maximum_fusion.13), channel_id=1, source_target_pairs={{0,16},{16,0},{1,17},{17,1},{2,18},{18,2},{3,19},{19,3},{4,20},{20... | collective-permute-start | bytes 3145736 | tf_op jit(solution)/shard_map/ppermute | solution.py:562
  602.6 35.2 %collective-permute-start.42 = (bf16[256,2048]{1,0:T(8,128)(2,1)}, bf16[256,2048]{1,0:T(8,128)(2,1)S(1)}, u32[]{:S(2)}, u32[]{:S(2)}) collective-permute-start(bf16[256,2048]{1,0:T(8,128)(2,1)} %pad_maximum_fusion.14), channel_id=1, source_target_pairs={{0,2},{1,3},{2,0},{3,1},{4,6},{5,7},{6,4},{7,5},{8,10},{9,11},{10,... | collective-permute-start | bytes 3145736 | tf_op jit(solution)/shard_map/ppermute | solution.py:559
  (124 other events, 1182.3 us)
Sparse Core Ops, SparseCore 0:
  17.1 70.5 all-gather.7
  89.2 62.1 all-gather.5
  153.5 113.9 all-gather.9
  333.1 76.7 reduce-scatter.4
  412.1 77.2 reduce-scatter.6
  491.5 35.7 reduce-scatter.8
  535.3 44.1 reduce-scatter.10
